TPU v7x, 128 devices: a whole 4x4x4 slice. The times are simulated.
128 devices in a mesh: head: 8 (over z, core), query: 8 (over x, y_lo), ctx: 2 (over y_hi).
Axes of the slice: x: 4, y: 4 (y_hi: 2, y_lo: 2; y = y_hi * 2 + y_lo), z: 4, core: 2. Of those that a mesh axis runs over, the one named last changes fastest.
Arguments:
- queries: bfloat16 [1024, 128, 576], P('query', 'head'), may hold values from -3 to 3, as said below
- latent: bfloat16 [4096, 576], P(('head', 'query', 'ctx')), may hold values from -8 to 8
- out_grad: bfloat16 [1024, 128, 512], P('query', 'head'), may hold values from -6 to 6
- log_norms: float32 [1024, 128], P('query', 'head'), as said below
- row_dots: float32 [1024, 128], P('query', 'head'), may hold values from -48 to 48
Outputs:
- query_grad: float32 [1024, 128, 576], P(('query', 'ctx'), 'head')
- latent_grad: float32 [4096, 576], P(('head', 'query', 'ctx'))
Inputs may be any that keep to these rules, and one draw needn't show every extreme that they name: queries and latent are of order one; latent rows may differ in scale. log_norms[i,h] is the log of the sum over all 4096 latent rows of exp(scores[i,h,j]), computed from the given queries and latent.
All inputs are finite; a program needn't handle non-finite values.
Results may differ from a plain program's by a relative error of at most 0.0029.
Values may be sent and summed in bfloat16 or wider, within the bound.
No kernel may reach another device: no remote copies, remote signals or barrier semaphores. Data moves between devices by JAX's collectives and lax.ppermute only.
A program may use at most 64 MiB of HBM per device.

v0:
```python
import math

import jax
import jax.numpy as jnp
from jax import lax
from jax.sharding import PartitionSpec as P

softmax_scale = 192.0 ** (-0.5) * (0.1 * math.log(40.0) + 1.0) ** 2


def tile_grads(flat_q, flat_dout, norms, dots, latent_block):
    value_width = flat_dout.shape[1]
    key_width = latent_block.shape[1]
    scores = (
        lax.dot_general(
            flat_q, latent_block, (((1,), (1,)), ((), ())), preferred_element_type=jnp.float32
        )
        * softmax_scale
    )
    probs = jnp.exp(scores - norms[:, None])
    probs_low = probs.astype(jnp.bfloat16)
    dprobs = lax.dot_general(
        flat_dout,
        latent_block[:, :value_width],
        (((1,), (1,)), ((), ())),
        preferred_element_type=jnp.float32,
    )
    dscores = (probs * (dprobs - dots[:, None])).astype(jnp.bfloat16)
    query_part = jnp.dot(dscores, latent_block, preferred_element_type=jnp.float32)
    latent_key = (
        lax.dot_general(
            dscores, flat_q, (((0,), (0,)), ((), ())), preferred_element_type=jnp.float32
        )
        * softmax_scale
    )
    latent_value = lax.dot_general(
        probs_low, flat_dout, (((0,), (0,)), ((), ())), preferred_element_type=jnp.float32
    )
    latent_part = latent_key + jnp.pad(latent_value, ((0, 0), (0, key_width - value_width)))
    return (query_part, latent_part)


def span_grads(flat_q, flat_dout, norms, dots, latent_rows):
    row_count = latent_rows.shape[0]
    key_width = latent_rows.shape[1]
    block_rows = 512
    stacked = latent_rows.reshape(row_count // block_rows, block_rows, key_width)

    def single(carry, latent_block):
        query_part, latent_part = tile_grads(flat_q, flat_dout, norms, dots, latent_block)
        return (carry + query_part, latent_part)

    initial = jnp.zeros((flat_q.shape[0], key_width), jnp.float32)
    query_sum, latent_parts = lax.scan(single, initial, stacked)
    return (query_sum, latent_parts.reshape(row_count, key_width))


def on_device(queries, latent, out_grad, log_norms, row_dots):
    local_queries, local_heads, key_width = queries.shape
    flat_rows = local_queries * local_heads
    flat_q = queries.reshape(flat_rows, key_width)
    flat_dout = out_grad.reshape(flat_rows, out_grad.shape[2])
    norms = log_norms.reshape(flat_rows)
    dots = row_dots.reshape(flat_rows)
    gathered = lax.all_gather(latent, ("head", "query"), axis=0, tiled=True)
    query_sum, latent_all = span_grads(flat_q, flat_dout, norms, dots, gathered)
    latent_grad = lax.psum_scatter(latent_all, ("head", "query"), scatter_dimension=0, tiled=True)
    query_terms = (query_sum * softmax_scale).reshape(local_queries, local_heads, key_width)
    query_grad = lax.psum_scatter(query_terms, "ctx", scatter_dimension=0, tiled=True)
    return (query_grad, latent_grad)


def solution(mesh):
    in_specs = (
        P("query", "head", None),
        P(("head", "query", "ctx"), None),
        P("query", "head", None),
        P("query", "head"),
        P("query", "head"),
    )
    out_specs = (P(("query", "ctx"), "head", None), P(("head", "query", "ctx"), None))
    return jax.shard_map(
        on_device, mesh=mesh, in_specs=in_specs, out_specs=out_specs, check_vma=False
    )
```

profile of v0, /device:TPU:0, one launch (start us, length us, event | category | flops | bytes accessed | tf_op | source)
XLA Modules:
  0.0 595.6 jit_solution(4269715359291730156)
XLA Ops:
  7.2 0.0 all-gather.2.cloned.1.call-start
  7.2 0.7 all-gather.2.cloned.1.call-update
  7.9 0.0 reduce-scatter.5.cloned.1.call-start
  8.0 0.8 copy.11
  8.8 0.1 sub.60
  8.8 0.8 copy.12
  9.7 0.1 sub.59
  9.7 3.9 copy.10
  13.7 156.6 %all-gather.2.cloned.1.call-done = bf16[2048,576]{1,0:T(8,128)(2,1)} async-done(((bf16[32,576]{1,0:T(8,128)(2,1)}), bf16[2048,576]{1,0:T(8,128)(2,1)}) %all-gather.2.cloned.1.call-update) | async-done | bytes 2359312 | tf_op jit(solution)/shard_map/all_gather | solution.py:65
  170.3 49.7 %while.16 = (s32[]{:T(128)}, f32[2048,576]{0,1:T(8,128)}, f32[4,512,576]{1,2,0:T(8,128)}, bf16[4,512,576]{2,1,0:T(8,128)(2,1)}, bf16[2048,576]{1,0:T(8,128)(2,1)...) while((s32[]{:T(128)}, f32[2048,576]{0,1:T(8,128)}, ...), condition=%wide.wide.region_1.2_spmd.clone, body=%wide.wide.region_0.1_spmd.clone.sunk | while | flops 5782700032 | bytes 84828408 | solution.py:54
  170.3 1.1 dynamic-slice_bitcast_fusion.3
  171.4 0.0 copy-start.3
  171.5 1.8 fusion.55
  173.3 1.3 fusion.56
  174.6 1.3 multiply_convert_fusion.3
  176.0 2.4 fusion.57
  178.4 2.1 select_add_fusion.3
  180.6 2.1 copy-done
  182.7 1.1 dynamic-slice_bitcast_fusion.3
  183.8 0.0 copy-start.3
  183.9 1.8 fusion.55
  185.7 1.3 fusion.56
  187.0 1.3 multiply_convert_fusion.3
  188.4 2.4 fusion.57
  190.8 2.1 select_add_fusion.3
  193.0 2.1 copy-done
  195.1 1.1 dynamic-slice_bitcast_fusion.3
  196.3 1.8 fusion.55
  198.1 1.3 fusion.56
  199.4 1.3 multiply_convert_fusion.3
  200.8 2.5 fusion.57
  203.3 2.1 select_add_fusion.3
  205.4 2.1 copy-done
  207.6 1.1 dynamic-slice_bitcast_fusion.3
  208.7 1.8 fusion.55
  210.6 1.3 fusion.56
  211.9 1.3 multiply_convert_fusion.3
  213.3 2.4 fusion.57
  215.7 2.1 select_add_fusion.3
  217.8 2.1 copy-done
  220.0 5.8 copy.14
  225.7 0.0 reduce-scatter.5.cloned.1.call-update
  225.8 0.0 reduce-scatter.3.cloned.1.call-start
  225.8 5.4 broadcast_multiply_fusion
  231.3 5.8 copy.13
  237.1 0.0 reduce-scatter.3.cloned.1.call-update
  237.1 282.8 %reduce-scatter.5.cloned.1.call-done = f32[32,576]{1,0:T(8,128)} async-done(((f32[2048,576]{1,0:T(8,128)}), f32[32,576]{1,0:T(8,128)}) %reduce-scatter.5.cloned.1.call-update) | async-done | bytes 73744 | tf_op jit(solution)/shard_map/reduce_scatter | solution.py:67
  519.9 69.2 %reduce-scatter.3.cloned.1.call-done = f32[64,16,576]{2,1,0:T(8,128)} async-done(((f32[128,16,576]{2,1,0:T(8,128)}), f32[64,16,576]{2,1,0:T(8,128)}) %reduce-scatter.3.cloned.1.call-update) | async-done | bytes 2359312 | tf_op jit(solution)/shard_map/reduce_scatter | solution.py:69
  (36 shorter events, 0.1 us)
Async XLA Ops:
  7.2 163.1 %all-gather.2.cloned.1.call-start = ((), (), s32[]{:S(2)}) async-start(), calls=%async_computation.2 | async-start | bytes 2662400 | tf_op jit(solution)/shard_map/all_gather | solution.py:65
  7.9 512.0 %reduce-scatter.5.cloned.1.call-start = ((), (), s32[]{:S(2)}) async-start(), calls=%async_computation.4 | async-start | bytes 5324800 | tf_op jit(solution)/shard_map/reduce_scatter | solution.py:67
  8.8 161.5 %copy-start.1 = (f32[128,16]{1,0:T(8,128)}, f32[128,16]{1,0:T(8,128)S(1)}, u32[]{:S(2)}) copy-start(f32[128,16]{1,0:T(8,128)S(1)} %copy.11) | copy-start | bytes 24580
  9.6 160.6 %copy-start.2 = (f32[128,16]{1,0:T(8,128)}, f32[128,16]{1,0:T(8,128)S(1)}, u32[]{:S(2)}) copy-start(f32[128,16]{1,0:T(8,128)S(1)} %copy.12) | copy-start | bytes 24580
  171.4 1.9 copy-start.3
  174.6 3.8 slice-start
  176.0 2.5 slice-start.1
  180.6 2.1 copy-start
  183.8 1.8 copy-start.3
  187.0 3.8 slice-start
  188.4 2.5 slice-start.1
  193.0 2.1 copy-start
  196.3 1.8 copy-start.3
  199.4 3.9 slice-start
  200.8 2.5 slice-start.1
  205.4 2.1 copy-start
  208.7 1.8 copy-start.3
  211.9 3.8 slice-start
  213.3 2.5 slice-start.1
  217.8 2.1 copy-start
  225.8 363.3 %reduce-scatter.3.cloned.1.call-start = ((), (), s32[]{:S(2)}) async-start(), calls=%async_computation.3 | async-start | bytes 7864320 | tf_op jit(solution)/shard_map/reduce_scatter | solution.py:69
Sparse Core Ops, SparseCore 0:
  9.7 160.5 all-gather.1
  225.9 293.9 reduce-scatter.4
  522.9 66.1 reduce-scatter.2
where the time goes:
time: 597 us; the launch traced here: 596 us
  waiting for transfers between devices  509 us (85%)
  matrix products  36.2 us (6%)
  local copies, waits for them, and re-layouts  30.5 us (5%)
  between operations  13.8 us (2%)
    reduce_scatter x1, waiting for transfers between devices, on_device(): lax.psum_scatter(latent_all, ('head', 'query'), scatter_dimension=0, tile...  283 us
    all_gather x1, waiting for transfers between devices, on_device(): gathered = lax.all_gather(latent, ('head', 'query'), axis=0, tiled=True)  157 us
    reduce_scatter x1, waiting for transfers between devices, on_device(): lax.psum_scatter(query_terms, 'ctx', scatter_dimension=0, tiled=True)  69.2 us
  transfers between devices with their start and end apart: 3, of which 3 were waited for; matrix products, arithmetic and copies ran while one was open for 3% of the time, Pallas kernels for 0%

commit v1 on v0

v1 whole, which is shorter than its diff:
```python
import functools
import math

import jax
import jax.numpy as jnp
from jax import lax
from jax.experimental import pallas as pl
from jax.experimental.pallas import tpu as pltpu
from jax.sharding import Mesh, PartitionSpec as P

softmax_scale = 192.0 ** (-0.5) * (0.1 * math.log(40.0) + 1.0) ** 2
log2_e = math.log2(math.e)

FINE_AXES = ("z", "core", "x", "y_lo", "y_hi")
CHIP_AXES = ("z", "x", "y_lo", "y_hi")
CHUNKS = (16, 16)
TILE = 256

NT = (((1,), (1,)), ((), ()))
NN = (((1,), (0,)), ((), ()))
TN = (((0,), (0,)), ((), ()))


def f32_dot(left, right, dims):
    return lax.dot_general(left, right, dims, preferred_element_type=jnp.float32)


def chunk_kernel(first, *refs):
    if first:
        k_ref, q_ref, do_ref, norm_ref, dot_ref, dkv_ref, dq_ref, key_acc, value_acc = refs
    else:
        k_ref, q_ref, do_ref, norm_ref, dot_ref, dq_in_ref, dkv_ref, dq_ref, key_acc, value_acc = refs
    step = pl.program_id(0)
    width = do_ref.shape[1]

    @pl.when(step == 0)
    def _():
        key_acc[...] = jnp.zeros_like(key_acc)
        value_acc[...] = jnp.zeros_like(value_acc)

    keys = k_ref[...]
    queries = q_ref[...]
    douts = do_ref[...]
    scores = f32_dot(keys, queries, NT)
    dprobs = f32_dot(keys[:, :width], douts, NT)
    probs = jnp.exp2(scores * (softmax_scale * log2_e) - norm_ref[...] * log2_e)
    dscores = (probs * (dprobs - dot_ref[...])).astype(jnp.bfloat16)
    query_part = f32_dot(dscores, keys, TN)
    dq_ref[...] = query_part if first else dq_in_ref[...] + query_part
    key_acc[...] += f32_dot(dscores, queries, NN)
    value_acc[...] += f32_dot(probs.astype(jnp.bfloat16), douts, NN)

    @pl.when(step == pl.num_programs(0) - 1)
    def _():
        dkv_ref[:, :width] = (key_acc[:, :width] * softmax_scale + value_acc[...]).astype(dkv_ref.dtype)
        dkv_ref[:, width:] = (key_acc[:, width:] * softmax_scale).astype(dkv_ref.dtype)


def chunk_grads(keys, queries, douts, norms, dots, dq):
    rows, key_width = keys.shape
    total, width = douts.shape
    first = dq is None
    whole = pl.BlockSpec((rows, key_width), lambda i: (0, 0))
    tile = lambda n: pl.BlockSpec((TILE, n), lambda i: (i, 0))
    row = pl.BlockSpec((1, TILE), lambda i: (0, i))
    in_specs = [whole, tile(key_width), tile(width), row, row]
    operands = [keys, queries, douts, norms, dots]
    if not first:
        in_specs.append(tile(key_width))
        operands.append(dq)
    flops = 2 * rows * total * (3 * key_width + 2 * width)
    moved = total * (key_width * 2 + width * 2 + key_width * (4 if first else 8)) + rows * key_width * 4
    return pl.pallas_call(
        functools.partial(chunk_kernel, first),
        grid=(total // TILE,),
        in_specs=in_specs,
        out_specs=[whole, tile(key_width)],
        out_shape=[
            jax.ShapeDtypeStruct((rows, key_width), jnp.bfloat16),
            jax.ShapeDtypeStruct((total, key_width), jnp.float32),
        ],
        scratch_shapes=[
            pltpu.VMEM((rows, key_width), jnp.float32),
            pltpu.VMEM((rows, width), jnp.float32),
        ],
        input_output_aliases={} if first else {5: 1},
        compiler_params=pltpu.CompilerParams(vmem_limit_bytes=48 << 20),
        cost_estimate=pl.CostEstimate(flops=flops, bytes_accessed=moved, transcendentals=rows * total),
        name="chunk_grads",
    )(*operands)


def on_device(queries, latent, out_grad, log_norms, row_dots):
    key_width = queries.shape[2]
    heads = queries.shape[1]
    chips = lax.axis_size(CHIP_AXES)
    half = queries.shape[0] // lax.axis_size("y_hi")

    def gather(start, rows):
        piece = lax.slice_in_dim(latent, start, start + rows, axis=0)
        spread = jnp.broadcast_to(piece[None], (chips, rows, key_width))
        got = lax.all_to_all(spread, CHIP_AXES, 0, 0, tiled=True)
        return got.reshape(chips * rows, key_width)

    starts = [sum(CHUNKS[:n]) for n in range(len(CHUNKS))]
    gathered = [gather(start, rows) for start, rows in zip(starts, CHUNKS)]

    def both(array):
        first = lax.axis_index("y_hi") * half
        mine = lax.dynamic_slice_in_dim(array, first, half, axis=0)
        theirs = lax.ppermute(mine, "core", [(0, 1), (1, 0)])
        return jnp.concatenate([mine.reshape((half * heads,) + mine.shape[2:]), theirs.reshape((half * heads,) + mine.shape[2:])])

    flat_q = both(queries)
    flat_dout = both(out_grad)
    stats = both(jnp.stack([log_norms, row_dots], axis=-1))
    norms = stats[:, 0][None]
    dots = stats[:, 1][None]

    dq = None
    latent_parts = []
    for rows, keys in zip(CHUNKS, gathered):
        dkv, dq = chunk_grads(keys, flat_q, flat_dout, norms, dots, dq)
        parts = lax.all_to_all(dkv.reshape(chips, rows, key_width), CHIP_AXES, 0, 0, tiled=True)
        latent_parts.append(jnp.sum(parts.astype(jnp.float32), axis=0))
    latent_grad = jnp.concatenate(latent_parts, axis=0)
    count = half * heads
    returned = lax.ppermute(dq[count:], "core", [(0, 1), (1, 0)])
    query_grad = ((dq[:count] + returned) * softmax_scale).reshape(half, heads, key_width)
    return (query_grad, latent_grad)


def solution(mesh):
    fine = Mesh(mesh.devices.reshape(4, 2, 4, 2, 2), FINE_AXES)
    query, head = ("x", "y_lo"), ("z", "core")
    in_specs = (
        P(query, head, None),
        P(FINE_AXES, None),
        P(query, head, None),
        P(query, head),
        P(query, head),
    )
    out_specs = (P(query + ("y_hi",), head, None), P(FINE_AXES, None))
    return jax.shard_map(on_device, mesh=fine, in_specs=in_specs, out_specs=out_specs, check_vma=False)
```

time: 597 us -> 158 us (0.26)
  waiting for transfers between devices: 509 us -> 39.2 us
  Pallas kernels: 0 us -> 39.8 us
  starting transfers between devices: 0.12 us -> 38.7 us
  matrix products: 36.2 us -> 0 us
  between operations: 13.8 us -> 0.78 us
  other arithmetic: 5.45 us -> 14.4 us
    reduce_scatter x2 -> x0, waiting for transfers between devices: 352 us -> none  [the longest x1 283 us: on_device(): lax.psum_scatter(latent_all, ('head', 'query'), scatter_dimension=0, tile...]
    all_gather x1 -> x0, waiting for transfers between devices: 157 us -> none  [on_device(): gathered = lax.all_gather(latent, ('head', 'query'), axis=0, tiled=True)]
    pallas_call x0 -> x2, Pallas kernels: none -> 39.8 us  [chunk_grads(): pl.pallas_call(functools.partial(chunk_kernel, first), grid=(total // TIL...]
    all_to_all x0 -> x4, waiting for transfers between devices: none -> 38.4 us  [the longest x2 20.6 us: on_device(): lax.all_to_all(dkv.reshape(chips, rows, key_width), CHIP_AXES, 0, 0, tile...]
    all_to_all x0 -> x4, starting transfers between devices: none -> 38.3 us  [the longest x2 21 us: on_device(): lax.all_to_all(dkv.reshape(chips, rows, key_width), CHIP_AXES, 0, 0, tile...]
    dot_general x20 -> x0, matrix products: 36.2 us -> none  [the longest x4 9.86 us: tile_grads(): lax.dot_general(dscores, flat_q, (((0,), (0,)), ((), ())), preferred_elem...]
    while x33 -> x0, local copies, waits for them, and re-layouts: 14.4 us -> none
    concatenate x0 -> x3, other arithmetic: none -> 6.94 us  [the longest x2 6.3 us: both(): jnp.concatenate([mine.reshape((half * heads,) + mine.shape[2:]), theirs.r...]
  transfers between devices with their start and end apart: 3 -> 8, of which waited for: 3 -> 3; matrix products, arithmetic and copies ran while one was open for 3% -> 17% of each run, Pallas kernels for 0% -> 25%
where the time goes in v1:
time: 158 us
  Pallas kernels  39.8 us (25%)
  waiting for transfers between devices  39.2 us (25%)
  starting transfers between devices  38.7 us (24%)
  local copies, waits for them, and re-layouts  24.8 us (16%)
  other arithmetic  14.4 us (9%)
    pallas_call x2, Pallas kernels, chunk_grads(): pl.pallas_call(functools.partial(chunk_kernel, first), grid=(total // TIL...  39.8 us
    all_to_all x2, starting transfers between devices, on_device(): lax.all_to_all(dkv.reshape(chips, rows, key_width), CHIP_AXES, 0, 0, tile...  21 us
    all_to_all x2, waiting for transfers between devices, on_device(): lax.all_to_all(dkv.reshape(chips, rows, key_width), CHIP_AXES, 0, 0, tile...  20.6 us
    all_to_all x2, waiting for transfers between devices, gather(): got = lax.all_to_all(spread, CHIP_AXES, 0, 0, tiled=True)  17.8 us
    all_to_all x2, starting transfers between devices, gather(): got = lax.all_to_all(spread, CHIP_AXES, 0, 0, tiled=True)  17.3 us
    unnamed x18, local copies, waits for them, and re-layouts  8.79 us
    slice x2, local copies, waits for them, and re-layouts, on_device(): returned = lax.ppermute(dq[count:], 'core', [(0, 1), (1, 0)])  6.57 us
    concatenate x2, other arithmetic, both(): jnp.concatenate([mine.reshape((half * heads,) + mine.shape[2:]), theirs.r...  6.3 us
  transfers between devices with their start and end apart: 8, of which 3 were waited for; matrix products, arithmetic and copies ran while one was open for 17% of the time, Pallas kernels for 25%

profile of v1, /device:TPU:0, one launch (start us, length us, event | category | flops | bytes accessed | tf_op | source)
XLA Modules:
  0.0 157.6 jit_solution(4505283387314649678)
XLA Ops:
  0.6 0.0 copy-start
  0.6 1.4 constant_dynamic-slice_fusion
  2.1 0.1 collective-permute-start.1
  2.2 0.4 copy-done
  2.6 2.1 %constant_dynamic-slice_fusion.1 = bf16[64,16,576]{0,2,1:T(8,128)(2,1)} fusion(bf16[128,16,576]{0,2,1:T(8,128)(2,1)S(1)} %copy-done, s32[]{:T(128)S(6)} %select_n.2), kind=kLoop, calls=%fused_computation.12 | loop fusion | bytes 2359300 | tf_op jit(solution)/shard_map/dynamic_slice | solution.py:110
  4.7 4.6 %copy.19 = bf16[64,16,576]{2,1,0:T(8,128)(2,1)} copy(bf16[64,16,576]{0,2,1:T(8,128)(2,1)} %constant_dynamic-slice_fusion.1) | data formatting | bytes 2359296
  9.3 0.1 collective-permute-start
  9.4 0.0 copy-done.5
  9.4 1.2 broadcast_in_dim.5
  10.5 11.7 %all-to-all-start.1 = ((bf16[64,16,576]{2,1,0:T(8,128)(2,1)}), bf16[64,16,576]{2,1,0:T(8,128)(2,1)}, u32[]{:S(2)}, u32[]{:S(2)}) async-start(bf16[64,16,576]{2,1,0:T(8,128)(2,1)} %broadcast_in_dim.5), calls=%async_computation.1 | async-start | bytes 2621440 | tf_op jit(solution)/shard_map/all_to_all | solution.py:102
  22.3 0.0 copy-done.6
  22.3 0.0 copy-done.7
  22.3 0.1 dynamic-slice_maximum_fusion
  22.4 0.2 collective-permute-start.2
  22.6 0.1 copy.15
  22.7 0.1 reshape.44
  22.8 0.8 collective-permute-done.2
  23.6 0.1 copy.16
  23.7 0.1 reshape.45
  23.8 0.0 collective-permute-done.1
  23.8 2.7 %pad_maximum_fusion.1.refs_2_ = bf16[2048,512]{1,0:T(8,128)(2,1)} fusion(bf16[1024,512]{1,0:T(8,128)(2,1)} %bitcast.4, bf16[1024,512]{1,0:T(8,128)(2,1)S(1)} %bitcast.22), kind=kLoop, calls=%fused_computation.4 | loop fusion | flops 4194304 | bytes 4194304 | tf_op jit(solution)/shard_map/concatenate | solution.py:112
  26.5 17.8 %all-to-all-done.1 = bf16[64,16,576]{2,1,0:T(8,128)(2,1)} async-done(((bf16[64,16,576]{2,1,0:T(8,128)(2,1)}), bf16[64,16,576]{2,1,0:T(8,128)(2,1)}, u32[]{:S(2)}, u32[]{:S(2)}) %all-to-all-start.1) | async-done | bytes 1179680 | tf_op jit(solution)/shard_map/all_to_all | solution.py:102
  44.3 1.2 broadcast_in_dim.4
  45.5 5.6 %all-to-all-start = ((bf16[64,16,576]{2,1,0:T(8,128)(2,1)}), bf16[64,16,576]{2,1,0:T(8,128)(2,1)}, u32[]{:S(2)}, u32[]{:S(2)}) async-start(bf16[64,16,576]{2,1,0:T(8,128)(2,1)} %broadcast_in_dim.4), calls=%async_computation | async-start | bytes 2621440 | tf_op jit(solution)/shard_map/all_to_all | solution.py:102
  51.1 0.0 collective-permute-done
  51.1 0.0 copy-start.1
  51.1 3.6 %pad_maximum_fusion.refs_1_ = bf16[2048,576]{1,0:T(8,128)(2,1)} fusion(bf16[1024,576]{1,0:T(8,128)(2,1)} %bitcast.2, bf16[1024,576]{1,0:T(8,128)(2,1)} %bitcast.21), kind=kLoop, calls=%fused_computation | loop fusion | flops 4718592 | bytes 4718592 | tf_op jit(solution)/shard_map/concatenate | solution.py:112
  54.7 0.0 copy-done.1
  54.7 19.7 %chunk_grads.2 = (bf16[1024,576]{1,0:T(8,128)(2,1)S(1)}, f32[2048,576]{1,0:T(8,128)}) custom-call(bf16[1024,576]{1,0:T(8,128)(2,1)} %bitcast.9.refs_0_, bf16[2048,576]{1,0:T(8,128)(2,1)} %pad_maximum_fusion.refs_1_, bf16[2048,512]{1,0:T(8,128)(2,1)S(1)} %copy-done.1, f32[1,2048]{1,0:T(1,128)S(1)} %get-tuple-element.13.refs_3_, ...), custom_call_target="tpu_custom_call" | custom-call | flops 11542724608 | bytes 11534336 | tf_op jit(solution)/shard_map/chunk_grads/pallas_call | solution.py:73
  74.4 1.1 copy-done.3
  75.4 0.0 all-to-all-done
  75.4 10.5 %all-to-all-start.2 = ((bf16[64,16,576]{2,1,0:T(8,128)(2,1)}), bf16[64,16,576]{2,1,0:T(8,128)(2,1)}, u32[]{:S(2)}, u32[]{:S(2)}) async-start(bf16[64,16,576]{2,1,0:T(8,128)(2,1)} %bitcast.19), calls=%async_computation.2 | async-start | bytes 2621440 | tf_op jit(solution)/shard_map/all_to_all | solution.py:124
  85.9 0.0 copy-start.2
  86.0 1.6 %copy-done.2 = bf16[2048,512]{1,0:T(8,128)(2,1)S(1)} copy-done((bf16[2048,512]{1,0:T(8,128)(2,1)S(1)}, bf16[2048,512]{1,0:T(8,128)(2,1)}, u32[]{:S(2)}) %copy-start.2) | copy-done | bytes 2097176
  87.5 20.1 %chunk_grads.3 = (bf16[1024,576]{1,0:T(8,128)(2,1)S(1)}, f32[2048,576]{1,0:T(8,128)}) custom-call(bf16[1024,576]{1,0:T(8,128)(2,1)} %bitcast.refs_0_, bf16[2048,576]{1,0:T(8,128)(2,1)} %pad_maximum_fusion.refs_1_, bf16[2048,512]{1,0:T(8,128)(2,1)S(1)} %copy-done.2, f32[1,2048]{1,0:T(1,128)S(1)} %get-tuple-element.13.refs_3_, ...), custom_call_target="tpu_custom_call", output_to_operand_aliasing={{1}: (5, {})} | custom-call | flops 11542724608 | bytes 16252928 | tf_op jit(solution)/shard_map/chunk_grads/pallas_call | solution.py:73
  107.6 1.1 copy-done.4
  108.8 3.4 %slice.23 = f32[1024,576]{1,0:T(8,128)} slice(f32[2048,576]{1,0:T(8,128)} %get-tuple-element.7), slice={[1024:2048], [0:576]} | slice | bytes 4718592 | tf_op jit(solution)/shard_map/slice | solution.py:128
  112.2 3.2 %copy.17 = f32[1024,576]{0,1:T(8,128)} copy(f32[1024,576]{1,0:T(8,128)} %slice.23) | data formatting | bytes 4718592 | tf_op jit(solution)/shard_map/slice | solution.py:128
  115.3 0.0 collective-permute-start.3
  115.3 0.0 all-to-all-done.2
  115.3 10.5 %all-to-all-start.3 = ((bf16[64,16,576]{2,1,0:T(8,128)(2,1)}), bf16[64,16,576]{2,1,0:T(8,128)(2,1)}, u32[]{:S(2)}, u32[]{:S(2)}) async-start(bf16[64,16,576]{2,1,0:T(8,128)(2,1)} %bitcast.20), calls=%async_computation.3 | async-start | bytes 2621440 | tf_op jit(solution)/shard_map/all_to_all | solution.py:124
  125.8 1.5 convert_reduce_fusion.1
  127.4 20.6 %all-to-all-done.3 = bf16[64,16,576]{2,1,0:T(8,128)(2,1)} async-done(((bf16[64,16,576]{2,1,0:T(8,128)(2,1)}), bf16[64,16,576]{2,1,0:T(8,128)(2,1)}, u32[]{:S(2)}, u32[]{:S(2)}) %all-to-all-start.3) | async-done | bytes 1179680 | tf_op jit(solution)/shard_map/all_to_all | solution.py:124
  148.0 1.5 convert_reduce_fusion
  149.5 0.6 pad_maximum_fusion.2
  150.1 0.0 collective-permute-done.3
  150.1 3.2 %copy.18 = f32[1024,576]{1,0:T(8,128)} copy(f32[1024,576]{0,1:T(8,128)} %collective-permute-done.3) | data formatting | bytes 4718592 | tf_op jit(solution)/shard_map/ppermute | solution.py:128
  153.3 4.3 %add_multiply_fusion = f32[1024,576]{1,0:T(8,128)} fusion(f32[1024,576]{1,0:T(8,128)} %copy.18, f32[2048,576]{1,0:T(8,128)} %get-tuple-element.7), kind=kLoop, calls=%fused_computation.3 | loop fusion | flops 1179648 | bytes 7077888 | tf_op jit(solution)/shard_map/mul | solution.py:129
  (9 shorter events, 0.0 us)
Async XLA Ops:
  0.6 2.0 %copy-start = (bf16[128,16,576]{0,2,1:T(8,128)(2,1)S(1)}, bf16[128,16,576]{0,2,1:T(8,128)(2,1)}, u32[]{:S(2)}) copy-start(bf16[128,16,576]{0,2,1:T(8,128)(2,1)} %param.5) | copy-start | bytes 7077892
  2.1 21.7 %collective-permute-start.1 = (bf16[64,16,512]{2,1,0:T(8,128)(2,1)S(1)}, bf16[64,16,512]{2,1,0:T(8,128)(2,1)}, u32[]{:S(2)}, u32[]{:S(2)}) collective-permute-start(bf16[64,16,512]{2,1,0:T(8,128)(2,1)S(1)} %constant_dynamic-slice_fusion), channel_id=1, source_target_pairs={{0,16},{16,0},{1,17},{17,1},{2,18},{18,2},{3,19},{19,3},{4,20},{20... | collective-permute-start | bytes 3145736 | tf_op jit(solution)/shard_map/ppermute | solution.py:111
  4.7 4.6 %copy-start.5 = (bf16[32,576]{1,0:T(8,128)(2,1)S(1)}, bf16[32,576]{1,0:T(8,128)(2,1)}, u32[]{:S(2)}) copy-start(bf16[32,576]{1,0:T(8,128)(2,1)} %param.6) | copy-start | bytes 110596
  9.3 13.0 %copy-start.6 = (f32[128,16]{0,1:T(8,128)S(1)}, f32[128,16]{0,1:T(8,128)}, u32[]{:S(2)}) copy-start(f32[128,16]{0,1:T(8,128)} %param.9) | copy-start | bytes 24580
  9.3 13.0 %copy-start.7 = (f32[128,16]{0,1:T(8,128)S(1)}, f32[128,16]{0,1:T(8,128)}, u32[]{:S(2)}) copy-start(f32[128,16]{0,1:T(8,128)} %param.8) | copy-start | bytes 24580
  9.3 41.8 %collective-permute-start = (bf16[64,16,576]{2,1,0:T(8,128)(2,1)}, bf16[64,16,576]{2,1,0:T(8,128)(2,1)}, u32[]{:S(2)}, u32[]{:S(2)}) collective-permute-start(bf16[64,16,576]{2,1,0:T(8,128)(2,1)} %copy.19), channel_id=1, source_target_pairs={{0,16},{16,0},{1,17},{17,1},{2,18},{18,2},{3,19},{19,3},{4,20},{20... | collective-permute-start | bytes 3538952 | tf_op jit(solution)/shard_map/ppermute | solution.py:111
  10.5 33.8 %all-to-all-start.1 = ((bf16[64,16,576]{2,1,0:T(8,128)(2,1)}), bf16[64,16,576]{2,1,0:T(8,128)(2,1)}, u32[]{:S(2)}, u32[]{:S(2)}) async-start(bf16[64,16,576]{2,1,0:T(8,128)(2,1)} %broadcast_in_dim.5), calls=%async_computation.1 | async-start | bytes 2621440 | tf_op jit(solution)/shard_map/all_to_all | solution.py:102
  22.4 1.2 collective-permute-start.2
  45.5 30.0 %all-to-all-start = ((bf16[64,16,576]{2,1,0:T(8,128)(2,1)}), bf16[64,16,576]{2,1,0:T(8,128)(2,1)}, u32[]{:S(2)}, u32[]{:S(2)}) async-start(bf16[64,16,576]{2,1,0:T(8,128)(2,1)} %broadcast_in_dim.4), calls=%async_computation | async-start | bytes 2621440 | tf_op jit(solution)/shard_map/all_to_all | solution.py:102
  51.1 3.6 %copy-start.1 = (bf16[2048,512]{1,0:T(8,128)(2,1)S(1)}, bf16[2048,512]{1,0:T(8,128)(2,1)}, u32[]{:S(2)}) copy-start(bf16[2048,512]{1,0:T(8,128)(2,1)} %pad_maximum_fusion.1.refs_2_) | copy-start | bytes 6291460
  74.4 1.1 copy-start.3
  75.4 39.9 %all-to-all-start.2 = ((bf16[64,16,576]{2,1,0:T(8,128)(2,1)}), bf16[64,16,576]{2,1,0:T(8,128)(2,1)}, u32[]{:S(2)}, u32[]{:S(2)}) async-start(bf16[64,16,576]{2,1,0:T(8,128)(2,1)} %bitcast.19), calls=%async_computation.2 | async-start | bytes 2621440 | tf_op jit(solution)/shard_map/all_to_all | solution.py:124
  85.9 1.6 %copy-start.2 = (bf16[2048,512]{1,0:T(8,128)(2,1)S(1)}, bf16[2048,512]{1,0:T(8,128)(2,1)}, u32[]{:S(2)}) copy-start(bf16[2048,512]{1,0:T(8,128)(2,1)} %pad_maximum_fusion.1.refs_2_) | copy-start | bytes 6291460
  107.6 1.1 copy-start.4
  115.3 34.8 %collective-permute-start.3 = (f32[1024,576]{0,1:T(8,128)}, f32[1024,576]{0,1:T(8,128)}, u32[]{:S(2)}, u32[]{:S(2)}) collective-permute-start(f32[1024,576]{0,1:T(8,128)} %copy.17), channel_id=1, source_target_pairs={{0,16},{16,0},{1,17},{17,1},{2,18},{18,2},{3,19},{19,3},{4,20},{20... | collective-permute-start | bytes 7077896 | tf_op jit(solution)/shard_map/ppermute | solution.py:128
  115.3 32.6 %all-to-all-start.3 = ((bf16[64,16,576]{2,1,0:T(8,128)(2,1)}), bf16[64,16,576]{2,1,0:T(8,128)(2,1)}, u32[]{:S(2)}, u32[]{:S(2)}) async-start(bf16[64,16,576]{2,1,0:T(8,128)(2,1)} %bitcast.20), calls=%async_computation.3 | async-start | bytes 2621440 | tf_op jit(solution)/shard_map/all_to_all | solution.py:124

commit v2 on v1

v2 whole, which is shorter than its diff:
```python
import functools
import math

import jax
import jax.numpy as jnp
from jax import lax
from jax.experimental import pallas as pl
from jax.experimental.pallas import tpu as pltpu
from jax.sharding import Mesh, PartitionSpec as P

softmax_scale = 192.0 ** (-0.5) * (0.1 * math.log(40.0) + 1.0) ** 2
log2_e = math.log2(math.e)

FINE_AXES = ("z", "core", "x", "y_lo", "y_hi")
CHIPS = ("z", "x", "y_lo")
PLANE = ("z", "x")
TILE = 512

NT = (((1,), (1,)), ((), ()))
NN = (((1,), (0,)), ((), ()))
TN = (((0,), (0,)), ((), ()))
VMEM = pl.BlockSpec(memory_space=pltpu.VMEM)
HBM = pl.BlockSpec(memory_space=pl.ANY)


def f32_dot(left, right, dims):
    return lax.dot_general(left, right, dims, preferred_element_type=jnp.float32)


def in_vmem(array):
    return pltpu.with_memory_space_constraint(array, pltpu.VMEM)


def in_hbm(array):
    return pltpu.with_memory_space_constraint(array, pltpu.HBM)


def swap(array, axis):
    return lax.ppermute(array, axis, [(0, 1), (1, 0)])


def grads_kernel(first, last, n_before, *refs):
    refs = list(refs)
    take = lambda number: [refs.pop(0) for _ in range(number)]
    _, key_ref, q_ref, do_ref, stat_ref = take(5)
    sum_in = [] if first else take(2)
    take(n_before)
    dq_ref = refs.pop(0)
    dkv_ref = refs.pop(0) if last else None
    key_acc, value_acc = refs
    step = pl.program_id(0)
    rows, width = value_acc.shape
    key_width = key_ref.shape[-1]

    @pl.when(step == 0)
    def _():
        key_acc[...] = jnp.zeros_like(key_acc) if first else sum_in[0][...]
        value_acc[...] = jnp.zeros_like(value_acc) if first else sum_in[1][...]

    keys = key_ref[...].reshape(rows, key_width)
    queries = q_ref[...]
    douts = do_ref[...]
    scores = f32_dot(keys, queries, NT)
    dprobs = f32_dot(keys[:, :width], douts, NT)
    probs = jnp.exp2(scores * (softmax_scale * log2_e) - stat_ref[0:1, :] * log2_e)
    dscores = (probs * (dprobs - stat_ref[1:2, :])).astype(jnp.bfloat16)
    dq = f32_dot(dscores, keys, TN)
    if dq_ref.shape[0] == dq.shape[0]:
        dq_ref[...] = dq
    else:
        dq_ref[pl.ds(pl.multiple_of(step * TILE, TILE), TILE), :] = dq
    key_acc[...] += f32_dot(dscores, queries, NN)
    value_acc[...] += f32_dot(probs.astype(jnp.bfloat16), douts, NN)

    if last:

        @pl.when(step == pl.num_programs(0) - 1)
        def _():
            shape = dkv_ref.shape[:2]
            summed = key_acc[:, :width] * softmax_scale + value_acc[...]
            dkv_ref[:, :, :width] = summed.astype(dkv_ref.dtype).reshape(shape + (width,))
            rest = key_acc[:, width:] * softmax_scale
            dkv_ref[:, :, width:] = rest.astype(dkv_ref.dtype).reshape(shape + (key_width - width,))


def grads(keys, half, side, sums=None, last=False, stays=False, before=()):
    shards, shard, key_width = keys.shape
    rows = shards * shard
    total, width = side[1].shape
    count = total // 2
    tiles = count // TILE
    first = sums is None
    tile = lambda columns: pl.BlockSpec((TILE, columns), lambda i, at: (at[0] * tiles + i, 0))
    operands = [half, in_vmem(keys)] + [in_hbm(array) for array in side]
    in_specs = [VMEM, tile(key_width), tile(width), pl.BlockSpec((2, TILE), lambda i, at: (0, at[0] * tiles + i))]
    sum_shapes = [(rows, key_width), (rows, width)]
    out_shape = [(pltpu.VMEM if stays else pltpu.HBM)((count, key_width), jnp.float32)]
    out_specs = [VMEM if stays else pl.BlockSpec((TILE, key_width), lambda i, at: (i, 0))]
    aliases, scratch = {}, []
    if last:
        out_shape.append(pltpu.HBM(keys.shape, keys.dtype))
        out_specs.append(pl.BlockSpec(keys.shape, lambda i, at: (0, 0, 0)))
        scratch = [pltpu.VMEM(shape, jnp.float32) for shape in sum_shapes]
    else:
        out_shape += [pltpu.VMEM(shape, jnp.float32) for shape in sum_shapes]
        out_specs += [VMEM, VMEM]
    if not first:
        if not last:
            aliases = {len(operands): 1, len(operands) + 1: 2}
        operands += [in_vmem(array) for array in sums]
        in_specs += [VMEM, VMEM]
    operands += before
    in_specs += [HBM] * len(before)
    return pl.pallas_call(
        functools.partial(grads_kernel, first, last, len(before)),
        grid_spec=pltpu.PrefetchScalarGridSpec(
            num_scalar_prefetch=1, grid=(tiles,), in_specs=in_specs, out_specs=out_specs, scratch_shapes=scratch
        ),
        out_shape=out_shape,
        input_output_aliases=aliases,
        compiler_params=pltpu.CompilerParams(vmem_limit_bytes=30 << 20),
        cost_estimate=pl.CostEstimate(
            flops=2 * rows * count * (3 * key_width + 2 * width),
            bytes_accessed=count * (key_width * 6 + width * 2) + rows * key_width * 4,
            transcendentals=rows * count,
        ),
        name="grads",
    )(*operands)


def add_kernel(out_scale, *refs):
    *addends, out_ref = refs
    rows = out_ref.shape[0]
    at = pl.ds(pl.program_id(0) * rows, rows)
    total = addends[0][at].astype(jnp.float32)
    for addend in addends[1:]:
        total += addend[at].astype(jnp.float32)
    out_ref[...] = (total * out_scale if out_scale else total).astype(out_ref.dtype)


def add(addends, dtype, out_scale=None):
    rows, heads, key_width = addends[0].shape
    steps = 4
    return pl.pallas_call(
        functools.partial(add_kernel, out_scale),
        grid=(steps,),
        in_specs=[VMEM] * len(addends),
        out_specs=pl.BlockSpec((rows // steps, heads, key_width), lambda i: (i, 0, 0)),
        out_shape=pltpu.HBM((rows, heads, key_width), dtype),
        compiler_params=pltpu.CompilerParams(vmem_limit_bytes=12 << 20),
        cost_estimate=pl.CostEstimate(
            flops=rows * heads * key_width * 2, bytes_accessed=rows * heads * key_width * 4, transcendentals=0
        ),
        name="add",
    )(*[in_vmem(addend) for addend in addends])


def sum_kernel(place, parts_ref, after_ref, mine_ref, other_ref):
    shard = mine_ref.shape[0]
    for out_ref, at in ((mine_ref, place[0]), (other_ref, 1 - place[0])):
        rows = pl.ds(pl.multiple_of(at * shard, shard), shard)
        total = parts_ref[0, rows, :].astype(jnp.float32)
        for part in range(1, parts_ref.shape[0]):
            total += parts_ref[part, rows, :].astype(jnp.float32)
        out_ref[...] = total


def sum_parts(parts, place, after):
    _, rows, key_width = parts.shape
    return pl.pallas_call(
        sum_kernel,
        grid_spec=pltpu.PrefetchScalarGridSpec(
            num_scalar_prefetch=1, grid=(1,), in_specs=[VMEM, HBM], out_specs=[VMEM, VMEM]
        ),
        out_shape=[jax.ShapeDtypeStruct((rows // 2, key_width), jnp.float32)] * 2,
        name="sum_parts",
    )(place, in_vmem(parts), after)


def on_device(queries, latent, out_grad, log_norms, row_dots):
    number, heads, key_width = queries.shape
    shard = latent.shape[0]
    half = number // 2

    spread = jnp.broadcast_to(latent[None], (lax.axis_size(CHIPS), shard, key_width))
    keys = lax.all_to_all(spread, CHIPS, 0, 0, tiled=True)

    def flat(queries, out_grad, stats):
        rows = number * heads
        return (
            queries.reshape(rows, key_width),
            out_grad.reshape(rows, out_grad.shape[2]),
            stats.reshape(2, rows),
        )

    mine = (queries, out_grad, jnp.stack([log_norms, row_dots]))
    theirs = flat(*[swap(array, "core") for array in mine])
    mine = flat(*mine)

    kept = lax.axis_index("y_hi").astype(jnp.int32)[None]
    sent = 1 - kept
    whole = (half, heads, key_width)
    dq_sent_theirs, *sums = grads(keys, sent, theirs, before=mine)
    dq_sent_mine, *sums = grads(keys, sent, mine, sums=sums, stays=True)
    returned = swap(dq_sent_theirs.reshape(whole), "core")
    over_cores = add([dq_sent_mine.reshape(whole), returned], jnp.bfloat16)
    received = swap(over_cores, "y_hi")
    dq_theirs, *sums = grads(keys, kept, theirs, sums=sums, before=[over_cores])
    dq_mine, dkv = grads(keys, kept, mine, sums=sums, last=True, stays=True)
    returned = swap(dq_theirs.reshape(whole), "core")
    query_grad = add([dq_mine.reshape(whole), returned, received], jnp.float32, softmax_scale)
    parts = lax.all_to_all(dkv.reshape(-1, 2 * shard, key_width), PLANE, 0, 0, tiled=True)
    own, other = sum_parts(parts, lax.axis_index("y_lo").astype(jnp.int32)[None], query_grad)
    return (query_grad, own + swap(other, "y_lo"))


def solution(mesh):
    fine = Mesh(mesh.devices.reshape(4, 2, 4, 2, 2), FINE_AXES)
    query, head = ("x", "y_lo"), ("z", "core")
    in_specs = (
        P(query, head, None),
        P(FINE_AXES, None),
        P(query, head, None),
        P(query, head),
        P(query, head),
    )
    out_specs = (P(query + ("y_hi",), head, None), P(FINE_AXES, None))
    return jax.shard_map(on_device, mesh=fine, in_specs=in_specs, out_specs=out_specs, check_vma=False)
```

time: 158 us -> 116 us (0.73)
  starting transfers between devices: 38.7 us -> 17.4 us
  other arithmetic: 14.4 us -> 1.56 us
  waiting for transfers between devices: 39.2 us -> 30.9 us
  Pallas kernels: 39.8 us -> 47.8 us
  local copies, waits for them, and re-layouts: 24.8 us -> 17.1 us
    all_to_all x4 -> x2, waiting for transfers between devices: 38.4 us -> 13 us  [the longest x1 10.5 us: on_device(): keys = lax.all_to_all(spread, CHIPS, 0, 0, tiled=True)]
    all_to_all x4 -> x2, starting transfers between devices: 38.3 us -> 13.1 us  [the longest x1 9.37 us: on_device(): keys = lax.all_to_all(spread, CHIPS, 0, 0, tiled=True)]
    ppermute x4 -> x7, waiting for transfers between devices: 0.83 us -> 17.9 us  [swap(): return lax.ppermute(array, axis, [(0, 1), (1, 0)])]
    pallas_call x2 -> x7, Pallas kernels: 39.8 us -> 47.8 us  [the longest x4 41.4 us: grads(): pl.pallas_call(functools.partial(grads_kernel, first, last, len(before)),...]
    concatenate x3 -> x0, other arithmetic: 6.94 us -> none  [the longest x2 6.3 us: both(): jnp.concatenate([mine.reshape((half * heads,) + mine.shape[2:]), theirs.r...]
    slice x3 -> x0, local copies, waits for them, and re-layouts: 6.58 us -> none  [the longest x2 6.57 us: on_device(): returned = lax.ppermute(dq[count:], 'core', [(0, 1), (1, 0)])]
    mul x1 -> x0, other arithmetic: 4.32 us -> none  [on_device(): (dq[:count] + returned) * softmax_scale]
    ppermute x4 -> x7, starting transfers between devices: 0.35 us -> 4.3 us  [swap(): return lax.ppermute(array, axis, [(0, 1), (1, 0)])]
  transfers between devices with their start and end apart: 8 -> 9, of which waited for: 3 -> 4; matrix products, arithmetic and copies ran while one was open for 17% -> 11% of each run, Pallas kernels for 25% -> 22%
where the time goes in v2:
time: 116 us; the launch traced here: 115 us
  Pallas kernels  47.8 us (41%)
  waiting for transfers between devices  30.9 us (27%)
  starting transfers between devices  17.4 us (15%)
  local copies, waits for them, and re-layouts  17.1 us (15%)
  other arithmetic  1.56 us (1%)
    pallas_call x4, Pallas kernels, grads(): pl.pallas_call(functools.partial(grads_kernel, first, last, len(before)),...  41.4 us
    ppermute x7, waiting for transfers between devices, swap(): return lax.ppermute(array, axis, [(0, 1), (1, 0)])  17.9 us
    all_to_all x1, waiting for transfers between devices, on_device(): keys = lax.all_to_all(spread, CHIPS, 0, 0, tiled=True)  10.5 us
    all_to_all x1, starting transfers between devices, on_device(): keys = lax.all_to_all(spread, CHIPS, 0, 0, tiled=True)  9.37 us
    unnamed x17, local copies, waits for them, and re-layouts  8.96 us
    pallas_call x2, Pallas kernels, add(): pl.pallas_call(functools.partial(add_kernel, out_scale), grid=(steps,), i...  5.58 us
    ppermute x2, local copies, waits for them, and re-layouts, swap(): return lax.ppermute(array, axis, [(0, 1), (1, 0)])  5 us
    ppermute x7, starting transfers between devices, swap(): return lax.ppermute(array, axis, [(0, 1), (1, 0)])  4.3 us
  transfers between devices with their start and end apart: 9, of which 4 were waited for; matrix products, arithmetic and copies ran while one was open for 11% of the time, Pallas kernels for 22%

profile of v2, /device:TPU:0, one launch (start us, length us, event | category | flops | bytes accessed | tf_op | source)
XLA Modules:
  0.0 115.5 jit_solution(991627403240630250)
XLA Ops:
  0.6 0.0 copy-start.5
  0.6 0.0 copy-start.6
  0.7 0.1 collective-permute-start
  0.7 0.5 collective-permute-start.1
  1.2 2.0 %broadcast_in_dim.13 = bf16[32,32,576]{2,1,0:T(8,128)(2,1)} broadcast(bf16[32,576]{1,0:T(8,128)(2,1)} %param.6), dimensions={1,2} | broadcast | bytes 1216512 | tf_op jit(solution)/shard_map/broadcast_in_dim | solution.py:185
  3.2 9.4 %all-to-all-start = ((bf16[32,32,576]{2,1,0:T(8,128)(2,1)}), bf16[32,32,576]{2,1,0:T(8,128)(2,1)}, u32[]{:S(2)}, u32[]{:S(2)}) async-start(bf16[32,32,576]{2,1,0:T(8,128)(2,1)} %broadcast_in_dim.13), calls=%async_computation | async-start | bytes 2621440 | tf_op jit(solution)/shard_map/all_to_all | solution.py:186
  12.6 0.0 copy-done.5
  12.6 0.0 copy-done.6
  12.6 0.1 collective-permute-start.2
  12.7 0.1 copy.17
  12.8 0.1 copy.18
  12.9 0.1 stack.15
  13.0 0.1 stack.16
  13.1 0.0 copy-start.3
  13.1 3.9 %copy.16 = bf16[128,16,576]{2,1,0:T(8,128)(2,1)S(1)} copy(bf16[128,16,576]{0,2,1:T(8,128)(2,1)} %param.5) | data formatting | bytes 4718592 | tf_op args[0]
  17.1 0.0 copy-start
  17.1 0.0 collective-permute-done.2
  17.1 0.1 copy.20
  17.2 1.0 reshape.44.refs_4_
  18.2 0.0 collective-permute-done
  18.2 4.9 %copy.19 = bf16[128,16,576]{2,1,0:T(8,128)(2,1)} copy(bf16[128,16,576]{0,2,1:T(8,128)(2,1)} %collective-permute-done) | data formatting | bytes 4718592 | tf_op jit(solution)/shard_map/ppermute | solution.py:39
  23.1 10.5 %all-to-all-done.refs_1_ = bf16[32,32,576]{2,1,0:T(8,128)(2,1)} async-done(((bf16[32,32,576]{2,1,0:T(8,128)(2,1)}), bf16[32,32,576]{2,1,0:T(8,128)(2,1)}, u32[]{:S(2)}, u32[]{:S(2)}) %all-to-all-start) | async-done | bytes 1179680 | tf_op jit(solution)/shard_map/all_to_all | solution.py:186
  33.5 0.0 collective-permute-done.1
  33.5 0.0 copy-done.3
  33.5 0.0 copy-done
  33.5 0.0 copy-start.4
  33.5 1.6 %copy-done.4 = bf16[128,16,512]{2,1,0:T(8,128)(2,1)S(1)} copy-done((bf16[128,16,512]{2,1,0:T(8,128)(2,1)S(1)}, bf16[128,16,512]{2,1,0:T(8,128)(2,1)}, u32[]{:S(2)}) %copy-start.4) | copy-done | bytes 2097176
  35.1 9.7 %grads.4 = (f32[1024,576]{1,0:T(8,128)}, f32[1024,576]{1,0:T(8,128)S(1)}, f32[1024,512]{1,0:T(8,128)S(1)}) custom-call(s32[1]{0:T(128)S(6)} %sub.3.refs_0_, bf16[32,32,576]{2,1,0:T(8,128)(2,1)} %all-to-all-done.refs_1_, bf16[2048,576]{1,0:T(8,128)(2,1)} %bitcast.21, bf16[2048,512]{1,0:T(8,128)(2,1)} %bitcast.4.refs_3_, f32[2,2048]{1,0:T(2,128)} %reshape.44.refs_4_, ...), custom_call_target="tpu_custom_call" | custom-call | flops 5771362304 | bytes 6946816 | tf_op jit(solution)/shard_map/grads/pallas_call | solution.py:114
  44.9 0.3 collective-permute-start.3
  45.2 10.1 %grads.5 = (f32[1024,576]{1,0:T(8,128)S(1)}, f32[1024,576]{1,0:T(8,128)S(1)}, f32[1024,512]{1,0:T(8,128)S(1)}) custom-call(s32[1]{0:T(128)S(6)} %sub.3.refs_0_, bf16[32,32,576]{2,1,0:T(8,128)(2,1)} %all-to-all-done.refs_1_, bf16[2048,576]{1,0:T(8,128)(2,1)} %bitcast.15, bf16[2048,512]{1,0:T(8,128)(2,1)} %bitcast.18, ...), custom_call_target="tpu_custom_call", output_to_operand_aliasing={{1}: (5, {}), {2}: (6, {})} | custom-call | flops 5771362304 | bytes 6946816 | tf_op jit(solution)/shard_map/grads/pallas_call | solution.py:114
  55.2 0.0 collective-permute-done.3.refs_1_
  55.2 1.8 %add.6.refs_7_ = bf16[64,16,576]{2,1,0:T(8,128)(2,1)} custom-call(f32[64,16,576]{2,1,0:T(8,128)S(1)} %bitcast.13, f32[64,16,576]{2,1,0:T(8,128)S(1)} %collective-permute-done.3.refs_1_), custom_call_target="tpu_custom_call" | custom-call | flops 1179648 | bytes 2359296 | tf_op jit(solution)/shard_map/add/pallas_call | solution.py:144
  57.0 10.5 %grads.6 = (f32[1024,576]{1,0:T(8,128)}, f32[1024,576]{1,0:T(8,128)S(1)}, f32[1024,512]{1,0:T(8,128)S(1)}) custom-call(s32[1]{0:T(128)} %bitcast.refs_0_, bf16[32,32,576]{2,1,0:T(8,128)(2,1)} %all-to-all-done.refs_1_, bf16[2048,576]{1,0:T(8,128)(2,1)} %bitcast.22, bf16[2048,512]{1,0:T(8,128)(2,1)} %bitcast.4.refs_3_, ...), custom_call_target="tpu_custom_call", output_to_operand_aliasing={{1}: (5, {}), {2}: (6, {})} | custom-call | flops 5771362304 | bytes 6946816 | tf_op jit(solution)/shard_map/grads/pallas_call | solution.py:114
  67.5 0.5 collective-permute-start.4
  68.0 2.9 %collective-permute-start.5 = (bf16[64,16,576]{2,1,0:T(8,128)(2,1)}, bf16[64,16,576]{2,1,0:T(8,128)(2,1)S(1)}, u32[]{:S(2)}, u32[]{:S(2)}) collective-permute-start(bf16[64,16,576]{2,1,0:T(8,128)(2,1)} %add.6.refs_7_), channel_id=1, source_target_pairs={{0,1},{1,0},{2,3},{3,2},{4,5},{5,4},{6,7},{7,6},{8,9},{9,8},{10,11... | collective-permute-start | bytes 3538952 | tf_op jit(solution)/shard_map/ppermute | solution.py:39
  70.9 11.1 %grads.7 = (f32[1024,576]{1,0:T(8,128)S(1)}, bf16[32,32,576]{2,1,0:T(8,128)(2,1)}) custom-call(s32[1]{0:T(128)} %bitcast.refs_0_, bf16[32,32,576]{2,1,0:T(8,128)(2,1)} %all-to-all-done.refs_1_, bf16[2048,576]{1,0:T(8,128)(2,1)} %bitcast.16, bf16[2048,512]{1,0:T(8,128)(2,1)} %bitcast.19, f32[2,2048]{1,0:T(2,128)} %copy-done.3, ...), custom_call_target="tpu_custom_call" | custom-call | flops 5771362304 | bytes 6946816 | tf_op jit(solution)/shard_map/grads/pallas_call | solution.py:114
  82.0 0.0 copy-start.1
  82.0 1.5 %copy-done.1 = f32[1024,576]{1,0:T(8,128)} copy-done((f32[1024,576]{1,0:T(8,128)}, f32[1024,576]{1,0:T(8,128)S(1)}, u32[]{:S(2)}) %copy-start.1) | copy-done | bytes 2359320
  83.4 3.7 %all-to-all-start.1 = ((bf16[16,64,576]{2,1,0:T(8,128)(2,1)}), bf16[16,64,576]{2,1,0:T(8,128)(2,1)S(1)}, u32[]{:S(2)}, u32[]{:S(2)}) async-start(bf16[16,64,576]{2,1,0:T(8,128)(2,1)} %bitcast.23), calls=%async_computation.1 | async-start | bytes 2621440 | tf_op jit(solution)/shard_map/all_to_all | solution.py:212
  87.2 13.3 %collective-permute-done.5.refs_2_ = bf16[64,16,576]{2,1,0:T(8,128)(2,1)S(1)} collective-permute-done((bf16[64,16,576]{2,1,0:T(8,128)(2,1)}, bf16[64,16,576]{2,1,0:T(8,128)(2,1)S(1)}, u32[]{:S(2)}, u32[]{:S(2)}) %collective-permute-start.5) | collective-permute-done | bytes 1179680 | tf_op jit(solution)/shard_map/ppermute | solution.py:39
  100.4 0.0 collective-permute-done.4.refs_1_
  100.4 1.7 %copy-done.2 = f32[1024,576]{1,0:T(8,128)S(1)} copy-done((f32[1024,576]{1,0:T(8,128)S(1)}, f32[1024,576]{1,0:T(8,128)}, u32[]{:S(2)}) %copy-start.2) | copy-done | bytes 2359320
  102.2 3.8 %add.7.after_ref = f32[64,16,576]{2,1,0:T(8,128)} custom-call(f32[64,16,576]{2,1,0:T(8,128)S(1)} %bitcast.17, f32[64,16,576]{2,1,0:T(8,128)} %collective-permute-done.4.refs_1_, bf16[64,16,576]{2,1,0:T(8,128)(2,1)S(1)} %collective-permute-done.5.refs_2_), custom_call_target="tpu_custom_call" | custom-call | flops 1179648 | bytes 2359296 | tf_op jit(solution)/shard_map/add/pallas_call | solution.py:144
  106.0 2.5 %all-to-all-done.1.parts_ref = bf16[16,64,576]{2,1,0:T(8,128)(2,1)S(1)} async-done(((bf16[16,64,576]{2,1,0:T(8,128)(2,1)}), bf16[16,64,576]{2,1,0:T(8,128)(2,1)S(1)}, u32[]{:S(2)}, u32[]{:S(2)}) %all-to-all-start.1) | async-done | bytes 1179680 | tf_op jit(solution)/shard_map/all_to_all | solution.py:212
  108.5 0.8 sum_parts.1
  109.3 0.0 collective-permute-start.6
  109.3 4.6 %collective-permute-done.6 = f32[32,576]{1,0:T(8,128)S(1)} collective-permute-done((f32[32,576]{1,0:T(8,128)}, f32[32,576]{1,0:T(8,128)S(1)}, u32[]{:S(2)}, u32[]{:S(2)}) %collective-permute-start.6) | collective-permute-done | bytes 73760 | tf_op jit(solution)/shard_map/ppermute | solution.py:39
  113.9 1.5 %add.5 = f32[32,576]{1,0:T(8,128)} add(f32[32,576]{1,0:T(8,128)} %get-tuple-element.26, f32[32,576]{1,0:T(8,128)S(1)} %collective-permute-done.6) | non-fusion elementwise | flops 18432 | bytes 221184 | tf_op jit(solution)/shard_map/add | solution.py:214
  (3 shorter events, 0.0 us)
Async XLA Ops:
  0.6 12.0 %copy-start.5 = (f32[128,16]{0,1:T(8,128)S(1)}, f32[128,16]{0,1:T(8,128)}, u32[]{:S(2)}) copy-start(f32[128,16]{0,1:T(8,128)} %param.8) | copy-start | bytes 24580
  0.6 12.0 %copy-start.6 = (f32[128,16]{0,1:T(8,128)S(1)}, f32[128,16]{0,1:T(8,128)}, u32[]{:S(2)}) copy-start(f32[128,16]{0,1:T(8,128)} %param.9) | copy-start | bytes 24580
  0.7 17.5 %collective-permute-start = (bf16[128,16,576]{0,2,1:T(8,128)(2,1)}, bf16[128,16,576]{0,2,1:T(8,128)(2,1)}, u32[]{:S(2)}, u32[]{:S(2)}) collective-permute-start(bf16[128,16,576]{0,2,1:T(8,128)(2,1)} %param.5), channel_id=1, source_target_pairs={{0,16},{16,0},{1,17},{17,1},{2,18},{18,2},{3,19},{19,3},{4,20},{20... | collective-permute-start | bytes 7077896 | tf_op jit(solution)/shard_map/ppermute | solution.py:39
  0.7 32.8 %collective-permute-start.1 = (bf16[128,16,512]{2,1,0:T(8,128)(2,1)}, bf16[128,16,512]{2,1,0:T(8,128)(2,1)}, u32[]{:S(2)}, u32[]{:S(2)}) collective-permute-start(bf16[128,16,512]{2,1,0:T(8,128)(2,1)} %param.7), channel_id=1, source_target_pairs={{0,16},{16,0},{1,17},{17,1},{2,18},{18,2},{3,19},{19,3},{4,20},{20... | collective-permute-start | bytes 6291464 | tf_op jit(solution)/shard_map/ppermute | solution.py:39
  3.2 30.3 %all-to-all-start = ((bf16[32,32,576]{2,1,0:T(8,128)(2,1)}), bf16[32,32,576]{2,1,0:T(8,128)(2,1)}, u32[]{:S(2)}, u32[]{:S(2)}) async-start(bf16[32,32,576]{2,1,0:T(8,128)(2,1)} %broadcast_in_dim.13), calls=%async_computation | async-start | bytes 2621440 | tf_op jit(solution)/shard_map/all_to_all | solution.py:186
  12.6 4.5 %collective-permute-start.2 = (f32[2,128,16]{1,2,0:T(8,128)S(1)}, f32[2,128,16]{1,2,0:T(8,128)S(1)}, u32[]{:S(2)}, u32[]{:S(2)}) collective-permute-start(f32[2,128,16]{1,2,0:T(8,128)S(1)} %pad_maximum_fusion.1), channel_id=1, source_target_pairs={{0,16},{16,0},{1,17},{17,1},{2,18},{18,2},{3,19},{19,3},{4,20},{20... | collective-permute-start | bytes 49160 | tf_op jit(solution)/shard_map/ppermute | solution.py:39
  13.1 20.4 %copy-start.3 = (f32[2,2048]{1,0:T(2,128)}, f32[2,2048]{1,0:T(2,128)S(1)}, u32[]{:S(2)}) copy-start(f32[2,2048]{1,0:T(2,128)S(1)} %pad_maximum_fusion.refs_7_.refs_4_) | copy-start | bytes 49156
  17.1 16.5 %copy-start = (bf16[128,16,576]{2,1,0:T(8,128)(2,1)}, bf16[128,16,576]{2,1,0:T(8,128)(2,1)S(1)}, u32[]{:S(2)}) copy-start(bf16[128,16,576]{2,1,0:T(8,128)(2,1)S(1)} %copy.16) | copy-start | bytes 7077892
  33.5 1.6 %copy-start.4 = (bf16[128,16,512]{2,1,0:T(8,128)(2,1)S(1)}, bf16[128,16,512]{2,1,0:T(8,128)(2,1)}, u32[]{:S(2)}) copy-start(bf16[128,16,512]{2,1,0:T(8,128)(2,1)} %param.7) | copy-start | bytes 6291460
  44.9 10.3 %collective-permute-start.3 = (f32[64,16,576]{2,1,0:T(8,128)}, f32[64,16,576]{2,1,0:T(8,128)S(1)}, u32[]{:S(2)}, u32[]{:S(2)}) collective-permute-start(f32[64,16,576]{2,1,0:T(8,128)} %bitcast.27), channel_id=1, source_target_pairs={{0,16},{16,0},{1,17},{17,1},{2,18},{18,2},{3,19},{19,3},{4,20},{20... | collective-permute-start | bytes 7077896 | tf_op jit(solution)/shard_map/ppermute | solution.py:39
  67.5 32.9 %collective-permute-start.4 = (f32[64,16,576]{2,1,0:T(8,128)}, f32[64,16,576]{2,1,0:T(8,128)}, u32[]{:S(2)}, u32[]{:S(2)}) collective-permute-start(f32[64,16,576]{2,1,0:T(8,128)} %bitcast.26), channel_id=1, source_target_pairs={{0,16},{16,0},{1,17},{17,1},{2,18},{18,2},{3,19},{19,3},{4,20},{20... | collective-permute-start | bytes 7077896 | tf_op jit(solution)/shard_map/ppermute | solution.py:39
  68.0 32.4 %collective-permute-start.5 = (bf16[64,16,576]{2,1,0:T(8,128)(2,1)}, bf16[64,16,576]{2,1,0:T(8,128)(2,1)S(1)}, u32[]{:S(2)}, u32[]{:S(2)}) collective-permute-start(bf16[64,16,576]{2,1,0:T(8,128)(2,1)} %add.6.refs_7_), channel_id=1, source_target_pairs={{0,1},{1,0},{2,3},{3,2},{4,5},{5,4},{6,7},{7,6},{8,9},{9,8},{10,11... | collective-permute-start | bytes 3538952 | tf_op jit(solution)/shard_map/ppermute | solution.py:39
  82.0 1.5 %copy-start.1 = (f32[1024,576]{1,0:T(8,128)}, f32[1024,576]{1,0:T(8,128)S(1)}, u32[]{:S(2)}) copy-start(f32[1024,576]{1,0:T(8,128)S(1)} %get-tuple-element.23) | copy-start | bytes 7077892
  83.4 25.0 %all-to-all-start.1 = ((bf16[16,64,576]{2,1,0:T(8,128)(2,1)}), bf16[16,64,576]{2,1,0:T(8,128)(2,1)S(1)}, u32[]{:S(2)}, u32[]{:S(2)}) async-start(bf16[16,64,576]{2,1,0:T(8,128)(2,1)} %bitcast.23), calls=%async_computation.1 | async-start | bytes 2621440 | tf_op jit(solution)/shard_map/all_to_all | solution.py:212
  100.4 1.7 %copy-start.2 = (f32[1024,576]{1,0:T(8,128)S(1)}, f32[1024,576]{1,0:T(8,128)}, u32[]{:S(2)}) copy-start(f32[1024,576]{1,0:T(8,128)} %copy-done.1) | copy-start | bytes 7077892
  109.3 4.7 %collective-permute-start.6 = (f32[32,576]{1,0:T(8,128)}, f32[32,576]{1,0:T(8,128)S(1)}, u32[]{:S(2)}, u32[]{:S(2)}) collective-permute-start(f32[32,576]{1,0:T(8,128)} %get-tuple-element.27), channel_id=1, source_target_pairs={{0,2},{2,0},{1,3},{3,1},{4,6},{6,4},{5,7},{7,5},{8,10},{10,8},{9,1... | collective-permute-start | bytes 221192 | tf_op jit(solution)/shard_map/ppermute | solution.py:39

commit v3 on v2

v3 whole, which is shorter than its diff:
```python
import functools
import math

import jax
import jax.numpy as jnp
from jax import lax
from jax.experimental import pallas as pl
from jax.experimental.pallas import tpu as pltpu
from jax.sharding import Mesh, PartitionSpec as P

softmax_scale = 192.0 ** (-0.5) * (0.1 * math.log(40.0) + 1.0) ** 2
log2_e = math.log2(math.e)

FINE_AXES = ("z", "core", "x", "y_lo", "y_hi")
CHIPS = ("z", "x", "y_lo")
PLANE = ("z", "x")
TILE = 512

NT = (((1,), (1,)), ((), ()))
NN = (((1,), (0,)), ((), ()))
TN = (((0,), (0,)), ((), ()))
VMEM = pl.BlockSpec(memory_space=pltpu.VMEM)
HBM = pl.BlockSpec(memory_space=pl.ANY)


def f32_dot(left, right, dims):
    return lax.dot_general(left, right, dims, preferred_element_type=jnp.float32)


def in_vmem(array):
    return pltpu.with_memory_space_constraint(array, pltpu.VMEM)


def in_hbm(array):
    return pltpu.with_memory_space_constraint(array, pltpu.HBM)


def swap(array, axis):
    return lax.ppermute(array, axis, [(0, 1), (1, 0)])


def grads_kernel(first, last, stays, do_stays, n_halves, n_before, *refs):
    refs = list(refs)
    take = lambda number: [refs.pop(0) for _ in range(number)]
    half, key_ref, q_hbm, do_hbm, stat_ref = take(5)
    sum_in = [] if first else take(2)
    take(n_before)
    dq_refs = take(n_halves)
    dkv_ref = refs.pop(0) if last else None
    key_acc, value_acc, q_tiles, sems, *refs = refs
    dq_tiles = [] if stays else [refs.pop(0)]
    do_tiles = refs
    rows, width = value_acc.shape
    key_width = key_ref.shape[-1]
    count = dq_refs[0].shape[0]
    per_half = count // TILE

    def begin(tile):
        side = half[0] if tile < per_half else 1 - half[0]
        return pl.multiple_of(side * count, TILE) + tile % per_half * TILE

    copies, results = [], []
    for tile in range(n_halves * per_half):
        at = pl.ds(begin(tile), TILE)
        pair = [pltpu.make_async_copy(q_hbm.at[at, :], q_tiles.at[tile], sems.at[0, tile])]
        if not do_stays:
            pair.append(pltpu.make_async_copy(do_hbm.at[at, :], do_tiles[0].at[tile], sems.at[1, tile]))
        for copy in pair:
            copy.start()
        copies.append(pair)

    keys = key_ref[...].reshape(rows, key_width)
    for tile, pair in enumerate(copies):
        for copy in pair:
            copy.wait()
        queries = q_tiles[tile]
        douts = do_hbm[pl.ds(begin(tile), TILE), :] if do_stays else do_tiles[0][tile]
        side = half[0] if tile < per_half else 1 - half[0]
        stats = stat_ref[side * per_half + tile % per_half]
        scores = f32_dot(keys, queries, NT)
        dprobs = f32_dot(keys[:, :width], douts, NT)
        probs = jnp.exp2(scores * (softmax_scale * log2_e) - stats[0:1, :] * log2_e)
        dscores = (probs * (dprobs - stats[1:2, :])).astype(jnp.bfloat16)
        dq_at = dq_refs[tile // per_half].at[pl.ds(tile % per_half * TILE, TILE), :]
        if stays:
            dq_at[...] = f32_dot(dscores, keys, TN)
        else:
            dq_tiles[0][tile] = f32_dot(dscores, keys, TN)
            result = pltpu.make_async_copy(dq_tiles[0].at[tile], dq_at, sems.at[2, tile])
            result.start()
            results.append(result)
        key_part = f32_dot(dscores, queries, NN)
        value_part = f32_dot(probs.astype(jnp.bfloat16), douts, NN)
        if tile > 0:
            key_acc[...] += key_part
            value_acc[...] += value_part
        elif first:
            key_acc[...] = key_part
            value_acc[...] = value_part
        else:
            key_acc[...] = sum_in[0][...] + key_part
            value_acc[...] = sum_in[1][...] + value_part

    if last:
        shape = dkv_ref.shape[:2]
        summed = key_acc[:, :width] * softmax_scale + value_acc[...]
        dkv_ref[:, :, :width] = summed.astype(dkv_ref.dtype).reshape(shape + (width,))
        rest = key_acc[:, width:] * softmax_scale
        dkv_ref[:, :, width:] = rest.astype(dkv_ref.dtype).reshape(shape + (key_width - width,))
    for result in results:
        result.wait()


def grads(keys, half, side, halves=1, sums=None, last=False, stays=False, do_stays=False, before=()):
    shards, shard, key_width = keys.shape
    rows = shards * shard
    queries, douts, stats = side
    total, width = douts.shape
    count = total // 2
    tiles = halves * count // TILE
    first = sums is None
    operands = [half, in_vmem(keys), in_hbm(queries), (in_vmem if do_stays else in_hbm)(douts), in_vmem(stats)]
    in_specs = [VMEM, HBM, VMEM if do_stays else HBM, VMEM]
    sum_shapes = [(rows, key_width), (rows, width)]
    out_shape = [(pltpu.VMEM if stays else pltpu.HBM)((count, key_width), jnp.float32)] * halves
    out_specs = [VMEM if stays else HBM] * halves
    scratch = [
        pltpu.VMEM((tiles, TILE, key_width), queries.dtype),
        pltpu.SemaphoreType.DMA((3, tiles)),
    ]
    if not stays:
        scratch.append(pltpu.VMEM((tiles, TILE, key_width), jnp.float32))
    if not do_stays:
        scratch.append(pltpu.VMEM((tiles, TILE, width), douts.dtype))
    aliases = {}
    if not first:
        if not last:
            aliases = {len(operands): halves, len(operands) + 1: halves + 1}
        operands += [in_vmem(array) for array in sums]
        in_specs += [VMEM, VMEM]
    if last:
        out_shape.append(pltpu.HBM(keys.shape, keys.dtype))
        out_specs.append(pl.BlockSpec(keys.shape, lambda i, at: (0, 0, 0)))
        scratch = [pltpu.VMEM(shape, jnp.float32) for shape in sum_shapes] + scratch
    else:
        out_shape += [pltpu.VMEM(shape, jnp.float32) for shape in sum_shapes]
        out_specs += [VMEM, VMEM]
    operands += [in_hbm(array) for array in before]
    in_specs += [HBM] * len(before)
    return pl.pallas_call(
        functools.partial(grads_kernel, first, last, stays, do_stays, halves, len(before)),
        grid_spec=pltpu.PrefetchScalarGridSpec(
            num_scalar_prefetch=1, grid=(1,), in_specs=in_specs, out_specs=out_specs, scratch_shapes=scratch
        ),
        out_shape=out_shape,
        input_output_aliases=aliases,
        compiler_params=pltpu.CompilerParams(vmem_limit_bytes=32 << 20),
        cost_estimate=pl.CostEstimate(flops=rows * count, bytes_accessed=rows * key_width * 2, transcendentals=rows),
        name="grads",
    )(*operands)


def add_kernel(out_scale, *refs):
    *addends, out_ref = refs
    rows = out_ref.shape[0]
    at = pl.ds(pl.program_id(0) * rows, rows)
    parts = [addend[...] if addend.shape[0] == rows else addend[at] for addend in addends]
    total = parts[0].astype(jnp.float32)
    for part in parts[1:]:
        total += part.astype(jnp.float32)
    out_ref[...] = (total * out_scale if out_scale else total).astype(out_ref.dtype)


def add(addends, dtype, out_scale=None, resident=True):
    rows, heads, key_width = addends[0].shape
    steps = 4
    block = pl.BlockSpec((rows // steps, heads, key_width), lambda i: (i, 0, 0))
    return pl.pallas_call(
        functools.partial(add_kernel, out_scale),
        grid=(steps,),
        in_specs=[VMEM if resident else block] * len(addends),
        out_specs=block,
        out_shape=pltpu.HBM((rows, heads, key_width), dtype),
        compiler_params=pltpu.CompilerParams(vmem_limit_bytes=12 << 20),
        cost_estimate=pl.CostEstimate(
            flops=rows * heads * key_width * 2, bytes_accessed=rows * heads * key_width * 4, transcendentals=0
        ),
        name="add",
    )(*[(in_vmem if resident else in_hbm)(addend) for addend in addends])


def sum_kernel(place, parts_ref, after_ref, mine_ref, other_ref):
    shard = mine_ref.shape[0]
    for out_ref, at in ((mine_ref, place[0]), (other_ref, 1 - place[0])):
        rows = pl.ds(pl.multiple_of(at * shard, shard), shard)
        total = parts_ref[0, rows, :].astype(jnp.float32)
        for part in range(1, parts_ref.shape[0]):
            total += parts_ref[part, rows, :].astype(jnp.float32)
        out_ref[...] = total


def sum_parts(parts, place, after):
    _, rows, key_width = parts.shape
    return pl.pallas_call(
        sum_kernel,
        grid_spec=pltpu.PrefetchScalarGridSpec(
            num_scalar_prefetch=1, grid=(1,), in_specs=[VMEM, HBM], out_specs=[VMEM, VMEM]
        ),
        out_shape=[jax.ShapeDtypeStruct((rows // 2, key_width), jnp.float32)] * 2,
        compiler_params=pltpu.CompilerParams(vmem_limit_bytes=4 << 20),
        name="sum_parts",
    )(place, in_vmem(parts), in_hbm(after))


def on_device(queries, latent, out_grad, log_norms, row_dots):
    number, heads, key_width = queries.shape
    shard = latent.shape[0]
    half = number // 2

    spread = jnp.broadcast_to(latent[None], (lax.axis_size(CHIPS), shard, key_width))
    keys = lax.all_to_all(spread, CHIPS, 0, 0, tiled=True)

    def flat(queries, out_grad, stats):
        rows = number * heads
        return (
            queries.reshape(rows, key_width),
            out_grad.reshape(rows, out_grad.shape[2]),
            stats.reshape(2, rows // TILE, TILE).transpose(1, 0, 2),
        )

    mine = (queries, out_grad, jnp.stack([log_norms, row_dots]))
    theirs = flat(*[swap(array, "core") for array in mine])
    mine = flat(*mine)

    kept = lax.axis_index("y_hi").astype(jnp.int32)[None]
    sent = 1 - kept
    whole = (half, heads, key_width)
    dq_sent_theirs, dq_theirs, *sums = grads(keys, sent, theirs, halves=2, do_stays=True, before=mine)
    returned = swap(dq_sent_theirs.reshape(whole), "core")
    dq_sent_mine, *sums = grads(keys, sent, mine, sums=sums, stays=True)
    over_cores = add([dq_sent_mine.reshape(whole), returned], jnp.bfloat16)
    received = swap(over_cores, "y_hi")
    dq_mine, dkv = grads(keys, kept, mine, sums=sums, last=True, before=[over_cores])
    returned = swap(dq_theirs.reshape(whole), "core")
    query_grad = add([dq_mine.reshape(whole), returned, received], jnp.float32, softmax_scale, resident=False)
    parts = lax.all_to_all(dkv.reshape(-1, 2 * shard, key_width), PLANE, 0, 0, tiled=True)
    own, other = sum_parts(parts, lax.axis_index("y_lo").astype(jnp.int32)[None], query_grad)
    return (query_grad, own + swap(other, "y_lo"))


def solution(mesh):
    fine = Mesh(mesh.devices.reshape(4, 2, 4, 2, 2), FINE_AXES)
    query, head = ("x", "y_lo"), ("z", "core")
    in_specs = (
        P(query, head, None),
        P(FINE_AXES, None),
        P(query, head, None),
        P(query, head),
        P(query, head),
    )
    out_specs = (P(query + ("y_hi",), head, None), P(FINE_AXES, None))
    return jax.shard_map(on_device, mesh=fine, in_specs=in_specs, out_specs=out_specs, check_vma=False)
```

time: 116 us -> 106 us (0.914)
  Pallas kernels: 47.8 us -> 42.1 us
  waiting for transfers between devices: 30.9 us -> 27.1 us
  local copies, waits for them, and re-layouts: 17.1 us -> 15.3 us
    pallas_call x4 -> x3, Pallas kernels: 41.4 us -> 35.5 us  [grads(): pl.pallas_call(functools.partial(grads_kernel, first, last, stays, do_sta...]
    all_to_all x1, waiting for transfers between devices: 10.5 us -> 6.71 us  [on_device(): keys = lax.all_to_all(spread, CHIPS, 0, 0, tiled=True)]
    unnamed x17 -> x11, local copies, waits for them, and re-layouts: 8.96 us -> 6.13 us
    all_to_all x1, waiting for transfers between devices: 2.5 us -> 0.23 us  [on_device(): lax.all_to_all(dkv.reshape(-1, 2 * shard, key_width), PLANE, 0, 0, tiled=...]
    ppermute x7, waiting for transfers between devices: 17.9 us -> 20.2 us  [swap(): return lax.ppermute(array, axis, [(0, 1), (1, 0)])]
    transpose x0 -> x1, other arithmetic: none -> 1.34 us  [flat(): stats.reshape(2, rows // TILE, TILE).transpose(1, 0, 2)]
    another operation x2, local copies, waits for them, and re-layouts: 0.18 us -> 1.37 us  [on_device(): mine = (queries, out_grad, jnp.stack([log_norms, row_dots]))]
  transfers between devices with their start and end apart: 9 -> 9, of which waited for: 4 -> 4; matrix products, arithmetic and copies ran while one was open for 11% -> 15% of each run, Pallas kernels for 22% -> 24%
where the time goes in v3:
time: 106 us; the launch traced here: 105 us
  Pallas kernels  42.1 us (40%)
  waiting for transfers between devices  27.1 us (26%)
  starting transfers between devices  17.2 us (16%)
  local copies, waits for them, and re-layouts  15.3 us (14%)
  other arithmetic  2.6 us (2%)
    pallas_call x3, Pallas kernels, grads(): pl.pallas_call(functools.partial(grads_kernel, first, last, stays, do_sta...  35.5 us
    ppermute x7, waiting for transfers between devices, swap(): return lax.ppermute(array, axis, [(0, 1), (1, 0)])  20.2 us
    all_to_all x1, starting transfers between devices, on_device(): keys = lax.all_to_all(spread, CHIPS, 0, 0, tiled=True)  9.26 us
    all_to_all x1, waiting for transfers between devices, on_device(): keys = lax.all_to_all(spread, CHIPS, 0, 0, tiled=True)  6.71 us
    pallas_call x2, Pallas kernels, add(): pl.pallas_call(functools.partial(add_kernel, out_scale), grid=(steps,), i...  6.51 us
    unnamed x11, local copies, waits for them, and re-layouts  6.13 us
    ppermute x2, local copies, waits for them, and re-layouts, swap(): return lax.ppermute(array, axis, [(0, 1), (1, 0)])  5.71 us
    ppermute x7, starting transfers between devices, swap(): return lax.ppermute(array, axis, [(0, 1), (1, 0)])  4.19 us
  transfers between devices with their start and end apart: 9, of which 4 were waited for; matrix products, arithmetic and copies ran while one was open for 15% of the time, Pallas kernels for 24%

profile of v3, /device:TPU:0, one launch (start us, length us, event | category | flops | bytes accessed | tf_op | source)
XLA Modules:
  0.0 105.1 jit_solution(8470744809312496764)
XLA Ops:
  0.6 0.0 copy-start.2
  0.6 0.0 copy-start.3
  0.7 0.1 collective-permute-start
  0.7 0.5 collective-permute-start.1
  1.2 2.0 %broadcast_in_dim.13 = bf16[32,32,576]{2,1,0:T(8,128)(2,1)} broadcast(bf16[32,576]{1,0:T(8,128)(2,1)} %param.6), dimensions={1,2} | broadcast | bytes 1216512 | tf_op jit(solution)/shard_map/broadcast_in_dim | solution.py:220
  3.2 9.3 %all-to-all-start = ((bf16[32,32,576]{2,1,0:T(8,128)(2,1)}), bf16[32,32,576]{2,1,0:T(8,128)(2,1)S(1)}, u32[]{:S(2)}, u32[]{:S(2)}) async-start(bf16[32,32,576]{2,1,0:T(8,128)(2,1)} %broadcast_in_dim.13), calls=%async_computation | async-start | bytes 2621440 | tf_op jit(solution)/shard_map/all_to_all | solution.py:221
  12.5 0.0 copy-done.2
  12.5 0.0 copy-done.3
  12.5 0.6 pad_maximum_fusion
  13.1 0.0 collective-permute-start.2
  13.1 0.1 copy.14
  13.2 0.1 copy.15
  13.3 4.8 %copy.13 = bf16[128,16,576]{2,1,0:T(8,128)(2,1)} copy(bf16[128,16,576]{0,2,1:T(8,128)(2,1)} %param.5) | data formatting | bytes 4718592 | tf_op args[0]
  18.2 0.7 stack.21
  18.9 0.7 stack.22
  19.6 0.0 collective-permute-done.2
  19.6 0.8 copy.19
  20.4 0.1 reshape.44
  20.5 1.3 %maximum_bitcast_fusion = (f32[4,2,512]{2,1,0:T(2,128)}, f32[4,2,512]{2,1,0:T(2,128)S(1)}) fusion(f32[1,4,512]{2,0,1:T(1,128)} %stack.22, f32[1,4,512]{2,0,1:T(1,128)} %stack.21, f32[2,4,512]{2,1,0:T(4,128)S(1)} %reshape.44), kind=kLoop, calls=%fused_computation | loop fusion | flops 4096 | bytes 65536 | tf_op jit(solution)/shard_map/transpose | solution.py:228
  21.8 0.0 collective-permute-done
  21.8 4.9 %copy.18 = bf16[128,16,576]{2,1,0:T(8,128)(2,1)} copy(bf16[128,16,576]{0,2,1:T(8,128)(2,1)} %collective-permute-done) | data formatting | bytes 4718592 | tf_op jit(solution)/shard_map/ppermute | solution.py:39
  26.7 6.7 %all-to-all-done.refs_1_ = bf16[32,32,576]{2,1,0:T(8,128)(2,1)S(1)} async-done(((bf16[32,32,576]{2,1,0:T(8,128)(2,1)}), bf16[32,32,576]{2,1,0:T(8,128)(2,1)S(1)}, u32[]{:S(2)}, u32[]{:S(2)}) %all-to-all-start) | async-done | bytes 1179680 | tf_op jit(solution)/shard_map/all_to_all | solution.py:221
  33.5 0.0 collective-permute-done.1
  33.5 0.0 copy-start
  33.5 16.2 %grads.3 = (f32[1024,576]{1,0:T(8,128)}, f32[1024,576]{1,0:T(8,128)}, f32[1024,576]{1,0:T(8,128)S(1)}, f32[1024,512]{1,0:T(8,128)S(1)}) custom-call(s32[1]{0:T(128)S(6)} %sub.3.refs_0_, bf16[32,32,576]{2,1,0:T(8,128)(2,1)S(1)} %all-to-all-done.refs_1_, bf16[2048,576]{1,0:T(8,128)(2,1)} %bitcast.25, bf16[2048,512]{1,0:T(8,128)(2,1)S(1)} %bitcast.18, ...), custom_call_target="tpu_custom_call" | custom-call | flops 1048576 | bytes 1179648 | tf_op jit(solution)/shard_map/grads/pallas_call | solution.py:150
  49.7 0.1 collective-permute-start.3
  49.8 0.5 collective-permute-start.4
  50.3 0.0 copy-done
  50.3 9.0 %grads.4 = (f32[1024,576]{1,0:T(8,128)S(1)}, f32[1024,576]{1,0:T(8,128)S(1)}, f32[1024,512]{1,0:T(8,128)S(1)}) custom-call(s32[1]{0:T(128)S(6)} %sub.3.refs_0_, bf16[32,32,576]{2,1,0:T(8,128)(2,1)S(1)} %all-to-all-done.refs_1_, bf16[2048,576]{1,0:T(8,128)(2,1)} %bitcast.20, ...), custom_call_target="tpu_custom_call", output_to_operand_aliasing={{1}: (5, {}), {2}: (6, {})} | custom-call | flops 1048576 | bytes 1179648 | tf_op jit(solution)/shard_map/grads/pallas_call | solution.py:150
  59.2 0.0 collective-permute-done.3.refs_1_
  59.2 1.7 %add.6.refs_7_ = bf16[64,16,576]{2,1,0:T(8,128)(2,1)} custom-call(f32[64,16,576]{2,1,0:T(8,128)S(1)} %bitcast.17, f32[64,16,576]{2,1,0:T(8,128)S(1)} %collective-permute-done.3.refs_1_), custom_call_target="tpu_custom_call" | custom-call | flops 1179648 | bytes 2359296 | tf_op jit(solution)/shard_map/add/pallas_call | solution.py:178
  61.0 2.9 %collective-permute-start.5 = (bf16[64,16,576]{2,1,0:T(8,128)(2,1)}, bf16[64,16,576]{2,1,0:T(8,128)(2,1)S(1)}, u32[]{:S(2)}, u32[]{:S(2)}) collective-permute-start(bf16[64,16,576]{2,1,0:T(8,128)(2,1)} %add.6.refs_7_), channel_id=1, source_target_pairs={{0,1},{1,0},{2,3},{3,2},{4,5},{5,4},{6,7},{7,6},{8,9},{9,8},{10,11... | collective-permute-start | bytes 3538952 | tf_op jit(solution)/shard_map/ppermute | solution.py:39
  63.9 10.3 %grads.5 = (f32[1024,576]{1,0:T(8,128)}, bf16[32,32,576]{2,1,0:T(8,128)(2,1)}) custom-call(s32[1]{0:T(128)} %bitcast.refs_0_, bf16[32,32,576]{2,1,0:T(8,128)(2,1)S(1)} %all-to-all-done.refs_1_, bf16[2048,576]{1,0:T(8,128)(2,1)} %bitcast.21, bf16[2048,512]{1,0:T(8,128)(2,1)} %bitcast.24, f32[4,2,512]{2,1,0:T(2,128)S(1)} %copy-done, ...), custom_call_target="tpu_custom_call" | custom-call | flops 1048576 | bytes 1179648 | tf_op jit(solution)/shard_map/grads/pallas_call | solution.py:150
  74.2 3.7 %all-to-all-start.1 = ((bf16[16,64,576]{2,1,0:T(8,128)(2,1)}), bf16[16,64,576]{2,1,0:T(8,128)(2,1)S(1)}, u32[]{:S(2)}, u32[]{:S(2)}) async-start(bf16[16,64,576]{2,1,0:T(8,128)(2,1)} %bitcast.27), calls=%async_computation.1 | async-start | bytes 2621440 | tf_op jit(solution)/shard_map/all_to_all | solution.py:246
  77.9 0.0 collective-permute-done.4.refs_1_
  77.9 15.8 %collective-permute-done.5.refs_2_ = bf16[64,16,576]{2,1,0:T(8,128)(2,1)S(1)} collective-permute-done((bf16[64,16,576]{2,1,0:T(8,128)(2,1)}, bf16[64,16,576]{2,1,0:T(8,128)(2,1)S(1)}, u32[]{:S(2)}, u32[]{:S(2)}) %collective-permute-start.5) | collective-permute-done | bytes 1179680 | tf_op jit(solution)/shard_map/ppermute | solution.py:39
  93.7 0.0 copy-start.1
  93.7 1.1 %copy-done.1 = bf16[64,16,576]{2,1,0:T(8,128)(2,1)} copy-done((bf16[64,16,576]{2,1,0:T(8,128)(2,1)}, bf16[64,16,576]{2,1,0:T(8,128)(2,1)S(1)}, u32[]{:S(2)}) %copy-start.1) | copy-done | bytes 1179672
  94.8 4.8 %add.7.after_ref = f32[64,16,576]{2,1,0:T(8,128)} custom-call(f32[64,16,576]{2,1,0:T(8,128)} %bitcast.26, f32[64,16,576]{2,1,0:T(8,128)} %collective-permute-done.4.refs_1_, bf16[64,16,576]{2,1,0:T(8,128)(2,1)} %copy-done.1), custom_call_target="tpu_custom_call" | custom-call | flops 1179648 | bytes 2359296 | tf_op jit(solution)/shard_map/add/pallas_call | solution.py:178
  99.5 0.2 all-to-all-done.1.parts_ref
  99.8 0.2 sum_parts.1
  99.9 0.1 collective-permute-start.6
  100.1 4.4 %collective-permute-done.6 = f32[32,576]{1,0:T(8,128)S(1)} collective-permute-done((f32[32,576]{1,0:T(8,128)S(1)}, f32[32,576]{1,0:T(8,128)S(1)}, u32[]{:S(2)}, u32[]{:S(2)}) %collective-permute-start.6) | collective-permute-done | bytes 73760 | tf_op jit(solution)/shard_map/ppermute | solution.py:39
  104.5 0.6 add.5
Async XLA Ops:
  0.6 11.9 %copy-start.2 = (f32[128,16]{0,1:T(8,128)S(1)}, f32[128,16]{0,1:T(8,128)}, u32[]{:S(2)}) copy-start(f32[128,16]{0,1:T(8,128)} %param.8) | copy-start | bytes 24580
  0.6 11.9 %copy-start.3 = (f32[128,16]{0,1:T(8,128)S(1)}, f32[128,16]{0,1:T(8,128)}, u32[]{:S(2)}) copy-start(f32[128,16]{0,1:T(8,128)} %param.9) | copy-start | bytes 24580
  0.7 21.2 %collective-permute-start = (bf16[128,16,576]{0,2,1:T(8,128)(2,1)}, bf16[128,16,576]{0,2,1:T(8,128)(2,1)}, u32[]{:S(2)}, u32[]{:S(2)}) collective-permute-start(bf16[128,16,576]{0,2,1:T(8,128)(2,1)} %param.5), channel_id=1, source_target_pairs={{0,16},{16,0},{1,17},{17,1},{2,18},{18,2},{3,19},{19,3},{4,20},{20... | collective-permute-start | bytes 7077896 | tf_op jit(solution)/shard_map/ppermute | solution.py:39
  0.7 32.7 %collective-permute-start.1 = (bf16[128,16,512]{2,1,0:T(8,128)(2,1)}, bf16[128,16,512]{2,1,0:T(8,128)(2,1)S(1)}, u32[]{:S(2)}, u32[]{:S(2)}) collective-permute-start(bf16[128,16,512]{2,1,0:T(8,128)(2,1)} %param.7), channel_id=1, source_target_pairs={{0,16},{16,0},{1,17},{17,1},{2,18},{18,2},{3,19},{19,3},{4,20},{20... | collective-permute-start | bytes 6291464 | tf_op jit(solution)/shard_map/ppermute | solution.py:39
  3.2 30.2 %all-to-all-start = ((bf16[32,32,576]{2,1,0:T(8,128)(2,1)}), bf16[32,32,576]{2,1,0:T(8,128)(2,1)S(1)}, u32[]{:S(2)}, u32[]{:S(2)}) async-start(bf16[32,32,576]{2,1,0:T(8,128)(2,1)} %broadcast_in_dim.13), calls=%async_computation | async-start | bytes 2621440 | tf_op jit(solution)/shard_map/all_to_all | solution.py:221
  13.1 6.4 %collective-permute-start.2 = (f32[2,128,16]{1,2,0:T(8,128)}, f32[2,128,16]{1,2,0:T(8,128)}, u32[]{:S(2)}, u32[]{:S(2)}) collective-permute-start(f32[2,128,16]{1,2,0:T(8,128)} %pad_maximum_fusion), channel_id=1, source_target_pairs={{0,16},{16,0},{1,17},{17,1},{2,18},{18,2},{3,19},{19,3},{4,20},{20... | collective-permute-start | bytes 49160 | tf_op jit(solution)/shard_map/ppermute | solution.py:39
  33.5 16.8 %copy-start = (f32[4,2,512]{2,1,0:T(2,128)S(1)}, f32[4,2,512]{2,1,0:T(2,128)}, u32[]{:S(2)}) copy-start(f32[4,2,512]{2,1,0:T(2,128)} %get-tuple-element.24.refs_7_.refs_4_) | copy-start | bytes 49156
  49.7 9.6 %collective-permute-start.3 = (f32[64,16,576]{2,1,0:T(8,128)}, f32[64,16,576]{2,1,0:T(8,128)S(1)}, u32[]{:S(2)}, u32[]{:S(2)}) collective-permute-start(f32[64,16,576]{2,1,0:T(8,128)} %bitcast.31), channel_id=1, source_target_pairs={{0,16},{16,0},{1,17},{17,1},{2,18},{18,2},{3,19},{19,3},{4,20},{20... | collective-permute-start | bytes 7077896 | tf_op jit(solution)/shard_map/ppermute | solution.py:39
  49.8 28.1 %collective-permute-start.4 = (f32[64,16,576]{2,1,0:T(8,128)}, f32[64,16,576]{2,1,0:T(8,128)}, u32[]{:S(2)}, u32[]{:S(2)}) collective-permute-start(f32[64,16,576]{2,1,0:T(8,128)} %bitcast.30), channel_id=1, source_target_pairs={{0,16},{16,0},{1,17},{17,1},{2,18},{18,2},{3,19},{19,3},{4,20},{20... | collective-permute-start | bytes 7077896 | tf_op jit(solution)/shard_map/ppermute | solution.py:39
  61.0 32.7 %collective-permute-start.5 = (bf16[64,16,576]{2,1,0:T(8,128)(2,1)}, bf16[64,16,576]{2,1,0:T(8,128)(2,1)S(1)}, u32[]{:S(2)}, u32[]{:S(2)}) collective-permute-start(bf16[64,16,576]{2,1,0:T(8,128)(2,1)} %add.6.refs_7_), channel_id=1, source_target_pairs={{0,1},{1,0},{2,3},{3,2},{4,5},{5,4},{6,7},{7,6},{8,9},{9,8},{10,11... | collective-permute-start | bytes 3538952 | tf_op jit(solution)/shard_map/ppermute | solution.py:39
  74.2 25.6 %all-to-all-start.1 = ((bf16[16,64,576]{2,1,0:T(8,128)(2,1)}), bf16[16,64,576]{2,1,0:T(8,128)(2,1)S(1)}, u32[]{:S(2)}, u32[]{:S(2)}) async-start(bf16[16,64,576]{2,1,0:T(8,128)(2,1)} %bitcast.27), calls=%async_computation.1 | async-start | bytes 2621440 | tf_op jit(solution)/shard_map/all_to_all | solution.py:246
  93.7 1.1 %copy-start.1 = (bf16[64,16,576]{2,1,0:T(8,128)(2,1)}, bf16[64,16,576]{2,1,0:T(8,128)(2,1)S(1)}, u32[]{:S(2)}) copy-start(bf16[64,16,576]{2,1,0:T(8,128)(2,1)S(1)} %collective-permute-done.5.refs_2_) | copy-start | bytes 3538948
  99.9 4.5 %collective-permute-start.6 = (f32[32,576]{1,0:T(8,128)S(1)}, f32[32,576]{1,0:T(8,128)S(1)}, u32[]{:S(2)}, u32[]{:S(2)}) collective-permute-start(f32[32,576]{1,0:T(8,128)S(1)} %get-tuple-element.23), channel_id=1, source_target_pairs={{0,2},{2,0},{1,3},{3,1},{4,6},{6,4},{5,7},{7,5},{8,10},{10,8},{9,1... | collective-permute-start | bytes 221192 | tf_op jit(solution)/shard_map/ppermute | solution.py:39

commit v4 on v3

--- a/solution.py
+++ b/solution.py
@@ -18,7 +18,6 @@
 
 NT = (((1,), (1,)), ((), ()))
 NN = (((1,), (0,)), ((), ()))
-TN = (((0,), (0,)), ((), ()))
 VMEM = pl.BlockSpec(memory_space=pltpu.VMEM)
 HBM = pl.BlockSpec(memory_space=pl.ANY)
 
@@ -70,6 +69,7 @@
         copies.append(pair)
 
     keys = key_ref[...].reshape(rows, key_width)
+    keys_t = keys.T
     for tile, pair in enumerate(copies):
         for copy in pair:
             copy.wait()
@@ -83,13 +83,13 @@
         dscores = (probs * (dprobs - stats[1:2, :])).astype(jnp.bfloat16)
         dq_at = dq_refs[tile // per_half].at[pl.ds(tile % per_half * TILE, TILE), :]
         if stays:
-            dq_at[...] = f32_dot(dscores, keys, TN)
+            dq_at[...] = f32_dot(keys_t, dscores, NN).T
         else:
-            dq_tiles[0][tile] = f32_dot(dscores, keys, TN)
+            dq_tiles[0][tile] = f32_dot(keys_t, dscores, NN).T
             result = pltpu.make_async_copy(dq_tiles[0].at[tile], dq_at, sems.at[2, tile])
             result.start()
             results.append(result)
-        key_part = f32_dot(dscores, queries, NN)
+        key_part = f32_dot(queries.T, dscores, NT)
         value_part = f32_dot(probs.astype(jnp.bfloat16), douts, NN)
         if tile > 0:
             key_acc[...] += key_part
@@ -103,9 +103,10 @@
 
     if last:
         shape = dkv_ref.shape[:2]
-        summed = key_acc[:, :width] * softmax_scale + value_acc[...]
+        key_sum = key_acc[...].T * softmax_scale
+        summed = key_sum[:, :width] + value_acc[...]
         dkv_ref[:, :, :width] = summed.astype(dkv_ref.dtype).reshape(shape + (width,))
-        rest = key_acc[:, width:] * softmax_scale
+        rest = key_sum[:, width:]
         dkv_ref[:, :, width:] = rest.astype(dkv_ref.dtype).reshape(shape + (key_width - width,))
     for result in results:
         result.wait()
@@ -121,7 +122,7 @@
     first = sums is None
     operands = [half, in_vmem(keys), in_hbm(queries), (in_vmem if do_stays else in_hbm)(douts), in_vmem(stats)]
     in_specs = [VMEM, HBM, VMEM if do_stays else HBM, VMEM]
-    sum_shapes = [(rows, key_width), (rows, width)]
+    sum_shapes = [(key_width, rows), (rows, width)]
     out_shape = [(pltpu.VMEM if stays else pltpu.HBM)((count, key_width), jnp.float32)] * halves
     out_specs = [VMEM if stays else HBM] * halves
     scratch = [
@@ -171,14 +172,15 @@
     out_ref[...] = (total * out_scale if out_scale else total).astype(out_ref.dtype)
 
 
-def add(addends, dtype, out_scale=None, resident=True):
+def add(addends, dtype, out_scale=None, resident=None):
     rows, heads, key_width = addends[0].shape
     steps = 4
+    resident = resident or [True] * len(addends)
     block = pl.BlockSpec((rows // steps, heads, key_width), lambda i: (i, 0, 0))
     return pl.pallas_call(
         functools.partial(add_kernel, out_scale),
         grid=(steps,),
-        in_specs=[VMEM if resident else block] * len(addends),
+        in_specs=[VMEM if stays else block for stays in resident],
         out_specs=block,
         out_shape=pltpu.HBM((rows, heads, key_width), dtype),
         compiler_params=pltpu.CompilerParams(vmem_limit_bytes=12 << 20),
@@ -186,10 +188,10 @@
             flops=rows * heads * key_width * 2, bytes_accessed=rows * heads * key_width * 4, transcendentals=0
         ),
         name="add",
-    )(*[(in_vmem if resident else in_hbm)(addend) for addend in addends])
-
-
-def sum_kernel(place, parts_ref, after_ref, mine_ref, other_ref):
+    )(*[(in_vmem if stays else in_hbm)(addend) for addend, stays in zip(addends, resident)])
+
+
+def sum_kernel(place, parts_ref, mine_ref, other_ref):
     shard = mine_ref.shape[0]
     for out_ref, at in ((mine_ref, place[0]), (other_ref, 1 - place[0])):
         rows = pl.ds(pl.multiple_of(at * shard, shard), shard)
@@ -199,17 +201,30 @@
         out_ref[...] = total
 
 
-def sum_parts(parts, place, after):
+def sum_parts(parts, place):
     _, rows, key_width = parts.shape
     return pl.pallas_call(
         sum_kernel,
-        grid_spec=pltpu.PrefetchScalarGridSpec(
-            num_scalar_prefetch=1, grid=(1,), in_specs=[VMEM, HBM], out_specs=[VMEM, VMEM]
-        ),
-        out_shape=[jax.ShapeDtypeStruct((rows // 2, key_width), jnp.float32)] * 2,
+        grid_spec=pltpu.PrefetchScalarGridSpec(num_scalar_prefetch=1, grid=(1,), in_specs=[VMEM], out_specs=[VMEM, VMEM]),
+        out_shape=[pltpu.VMEM((rows // 2, key_width), jnp.float32)] * 2,
         compiler_params=pltpu.CompilerParams(vmem_limit_bytes=4 << 20),
         name="sum_parts",
-    )(place, in_vmem(parts), in_hbm(after))
+    )(place, in_vmem(parts))
+
+
+def join_kernel(own_ref, other_ref, after_ref, out_ref):
+    out_ref[...] = own_ref[...] + other_ref[...]
+
+
+def join(own, other, after):
+    return pl.pallas_call(
+        join_kernel,
+        in_specs=[VMEM, VMEM, HBM],
+        out_specs=VMEM,
+        out_shape=jax.ShapeDtypeStruct(own.shape, own.dtype),
+        compiler_params=pltpu.CompilerParams(vmem_limit_bytes=4 << 20),
+        name="join",
+    )(in_vmem(own), in_vmem(other), in_hbm(after))
 
 
 def on_device(queries, latent, out_grad, log_norms, row_dots):
@@ -242,10 +257,10 @@
     received = swap(over_cores, "y_hi")
     dq_mine, dkv = grads(keys, kept, mine, sums=sums, last=True, before=[over_cores])
     returned = swap(dq_theirs.reshape(whole), "core")
-    query_grad = add([dq_mine.reshape(whole), returned, received], jnp.float32, softmax_scale, resident=False)
+    query_grad = add([dq_mine.reshape(whole), returned, received], jnp.float32, softmax_scale, resident=[False, False, True])
     parts = lax.all_to_all(dkv.reshape(-1, 2 * shard, key_width), PLANE, 0, 0, tiled=True)
-    own, other = sum_parts(parts, lax.axis_index("y_lo").astype(jnp.int32)[None], query_grad)
-    return (query_grad, own + swap(other, "y_lo"))
+    own, other = sum_parts(parts, lax.axis_index("y_lo").astype(jnp.int32)[None])
+    return (query_grad, join(own, swap(other, "y_lo"), query_grad))
 
 
 def solution(mesh):

time: 106 us -> 104 us (0.981)
  Pallas kernels: 42.1 us -> 40.5 us
  waiting for transfers between devices: 27.1 us -> 28.5 us
    all_to_all x1, waiting for transfers between devices: 0.23 us -> 21.8 us  [on_device(): lax.all_to_all(dkv.reshape(-1, 2 * shard, key_width), PLANE, 0, 0, tiled=...]
    ppermute x7, waiting for transfers between devices: 20.2 us -> 0.02 us  [swap(): return lax.ppermute(array, axis, [(0, 1), (1, 0)])]
    pallas_call x3, Pallas kernels: 35.5 us -> 33.3 us  [grads(): pl.pallas_call(functools.partial(grads_kernel, first, last, stays, do_sta...]
    unnamed x11 -> x9, local copies, waits for them, and re-layouts: 6.13 us -> 5.06 us
  transfers between devices with their start and end apart: 9 -> 9, of which waited for: 4 -> 2; matrix products, arithmetic and copies ran while one was open for 15% -> 16% of each run, Pallas kernels for 24% -> 24%
where the time goes in v4:
time: 104 us; the launch traced here: 103 us
  Pallas kernels  40.5 us (39%)
  waiting for transfers between devices  28.5 us (27%)
  starting transfers between devices  17.1 us (16%)
  local copies, waits for them, and re-layouts  14.3 us (14%)
  other arithmetic  1.95 us (2%)
    pallas_call x3, Pallas kernels, grads(): pl.pallas_call(functools.partial(grads_kernel, first, last, stays, do_sta...  33.3 us
    all_to_all x1, waiting for transfers between devices, on_device(): lax.all_to_all(dkv.reshape(-1, 2 * shard, key_width), PLANE, 0, 0, tiled=...  21.8 us
    all_to_all x1, starting transfers between devices, on_device(): keys = lax.all_to_all(spread, CHIPS, 0, 0, tiled=True)  9.26 us
    all_to_all x1, waiting for transfers between devices, on_device(): keys = lax.all_to_all(spread, CHIPS, 0, 0, tiled=True)  6.69 us
    pallas_call x2, Pallas kernels, add(): pl.pallas_call(functools.partial(add_kernel, out_scale), grid=(steps,), i...  6.38 us
    ppermute x2, local copies, waits for them, and re-layouts, swap(): return lax.ppermute(array, axis, [(0, 1), (1, 0)])  5.73 us
    unnamed x9, local copies, waits for them, and re-layouts  5.06 us
    ppermute x7, starting transfers between devices, swap(): return lax.ppermute(array, axis, [(0, 1), (1, 0)])  4.14 us
  transfers between devices with their start and end apart: 9, of which 2 were waited for; matrix products, arithmetic and copies ran while one was open for 16% of the time, Pallas kernels for 24%

profile of v4, /device:TPU:0, one launch (start us, length us, event | category | flops | bytes accessed | tf_op | source)
XLA Modules:
  0.0 103.1 jit_solution(17008948829975206250)
XLA Ops:
  0.6 0.0 copy-start.1
  0.6 0.0 copy-start.2
  0.7 0.1 collective-permute-start
  0.7 0.5 collective-permute-start.1
  1.2 2.0 %broadcast_in_dim.13 = bf16[32,32,576]{2,1,0:T(8,128)(2,1)} broadcast(bf16[32,576]{1,0:T(8,128)(2,1)} %param.6), dimensions={1,2} | broadcast | bytes 1216512 | tf_op jit(solution)/shard_map/broadcast_in_dim | solution.py:235
  3.2 9.3 %all-to-all-start = ((bf16[32,32,576]{2,1,0:T(8,128)(2,1)}), bf16[32,32,576]{2,1,0:T(8,128)(2,1)S(1)}, u32[]{:S(2)}, u32[]{:S(2)}) async-start(bf16[32,32,576]{2,1,0:T(8,128)(2,1)} %broadcast_in_dim.13), calls=%async_computation | async-start | bytes 2621440 | tf_op jit(solution)/shard_map/all_to_all | solution.py:236
  12.5 0.0 copy-done.1
  12.5 0.0 copy-done.2
  12.5 0.6 pad_maximum_fusion
  13.1 0.0 collective-permute-start.2
  13.1 0.1 copy.14
  13.2 0.1 copy.15
  13.3 4.8 %copy.13 = bf16[128,16,576]{2,1,0:T(8,128)(2,1)} copy(bf16[128,16,576]{0,2,1:T(8,128)(2,1)} %param.5) | data formatting | bytes 4718592 | tf_op args[0]
  18.2 0.7 stack.21
  18.9 0.7 stack.22
  19.5 0.0 collective-permute-done.2
  19.5 0.8 copy.19
  20.4 0.1 reshape.44
  20.5 1.3 %maximum_bitcast_fusion = (f32[4,2,512]{2,1,0:T(2,128)}, f32[4,2,512]{2,1,0:T(2,128)S(1)}) fusion(f32[1,4,512]{2,0,1:T(1,128)} %stack.22, f32[1,4,512]{2,0,1:T(1,128)} %stack.21, f32[2,4,512]{2,1,0:T(4,128)S(1)} %reshape.44), kind=kLoop, calls=%fused_computation | loop fusion | flops 4096 | bytes 65536 | tf_op jit(solution)/shard_map/transpose | solution.py:243
  21.8 0.0 collective-permute-done
  21.8 4.9 %copy.18 = bf16[128,16,576]{2,1,0:T(8,128)(2,1)} copy(bf16[128,16,576]{0,2,1:T(8,128)(2,1)} %collective-permute-done) | data formatting | bytes 4718592 | tf_op jit(solution)/shard_map/ppermute | solution.py:38
  26.8 6.7 %all-to-all-done.refs_1_ = bf16[32,32,576]{2,1,0:T(8,128)(2,1)S(1)} async-done(((bf16[32,32,576]{2,1,0:T(8,128)(2,1)}), bf16[32,32,576]{2,1,0:T(8,128)(2,1)S(1)}, u32[]{:S(2)}, u32[]{:S(2)}) %all-to-all-start) | async-done | bytes 1179680 | tf_op jit(solution)/shard_map/all_to_all | solution.py:236
  33.4 0.0 collective-permute-done.1
  33.4 0.0 copy-start
  33.4 15.6 %grads.3 = (f32[1024,576]{1,0:T(8,128)}, f32[1024,576]{1,0:T(8,128)}, f32[576,1024]{1,0:T(8,128)S(1)}, f32[1024,512]{1,0:T(8,128)S(1)}) custom-call(s32[1]{0:T(128)S(6)} %sub.3.refs_0_, bf16[32,32,576]{2,1,0:T(8,128)(2,1)S(1)} %all-to-all-done.refs_1_, bf16[2048,576]{1,0:T(8,128)(2,1)} %bitcast.25, bf16[2048,512]{1,0:T(8,128)(2,1)S(1)} %bitcast.18, ...), custom_call_target="tpu_custom_call" | custom-call | flops 1048576 | bytes 1179648 | tf_op jit(solution)/shard_map/grads/pallas_call | solution.py:151
  49.0 0.1 collective-permute-start.3
  49.1 0.5 collective-permute-start.4
  49.6 0.0 copy-done
  49.6 8.1 %grads.4 = (f32[1024,576]{1,0:T(8,128)S(1)}, f32[576,1024]{1,0:T(8,128)S(1)}, f32[1024,512]{1,0:T(8,128)S(1)}) custom-call(s32[1]{0:T(128)S(6)} %sub.3.refs_0_, bf16[32,32,576]{2,1,0:T(8,128)(2,1)S(1)} %all-to-all-done.refs_1_, bf16[2048,576]{1,0:T(8,128)(2,1)} %bitcast.20, ...), custom_call_target="tpu_custom_call", output_to_operand_aliasing={{1}: (5, {}), {2}: (6, {})} | custom-call | flops 1048576 | bytes 1179648 | tf_op jit(solution)/shard_map/grads/pallas_call | solution.py:151
  57.8 0.0 collective-permute-done.3.refs_1_
  57.8 1.8 %add.2.refs_7_ = bf16[64,16,576]{2,1,0:T(8,128)(2,1)} custom-call(f32[64,16,576]{2,1,0:T(8,128)S(1)} %bitcast.17, f32[64,16,576]{2,1,0:T(8,128)S(1)} %collective-permute-done.3.refs_1_), custom_call_target="tpu_custom_call" | custom-call | flops 1179648 | bytes 2359296 | tf_op jit(solution)/shard_map/add/pallas_call | solution.py:180
  59.6 2.9 %collective-permute-start.5 = (bf16[64,16,576]{2,1,0:T(8,128)(2,1)}, bf16[64,16,576]{2,1,0:T(8,128)(2,1)S(1)}, u32[]{:S(2)}, u32[]{:S(2)}) collective-permute-start(bf16[64,16,576]{2,1,0:T(8,128)(2,1)} %add.2.refs_7_), channel_id=1, source_target_pairs={{0,1},{1,0},{2,3},{3,2},{4,5},{5,4},{6,7},{7,6},{8,9},{9,8},{10,11... | collective-permute-start | bytes 3538952 | tf_op jit(solution)/shard_map/ppermute | solution.py:38
  62.5 9.6 %grads.5 = (f32[1024,576]{1,0:T(8,128)}, bf16[32,32,576]{2,1,0:T(8,128)(2,1)}) custom-call(s32[1]{0:T(128)} %bitcast.refs_0_, bf16[32,32,576]{2,1,0:T(8,128)(2,1)S(1)} %all-to-all-done.refs_1_, bf16[2048,576]{1,0:T(8,128)(2,1)} %bitcast.21, bf16[2048,512]{1,0:T(8,128)(2,1)} %bitcast.24, f32[4,2,512]{2,1,0:T(2,128)S(1)} %copy-done, ...), custom_call_target="tpu_custom_call" | custom-call | flops 1048576 | bytes 1179648 | tf_op jit(solution)/shard_map/grads/pallas_call | solution.py:151
  72.1 3.7 %all-to-all-start.1 = ((bf16[16,64,576]{2,1,0:T(8,128)(2,1)}), bf16[16,64,576]{2,1,0:T(8,128)(2,1)S(1)}, u32[]{:S(2)}, u32[]{:S(2)}) async-start(bf16[16,64,576]{2,1,0:T(8,128)(2,1)} %bitcast.27), calls=%async_computation.1 | async-start | bytes 2621440 | tf_op jit(solution)/shard_map/all_to_all | solution.py:261
  75.8 21.8 %all-to-all-done.1.parts_ref = bf16[16,64,576]{2,1,0:T(8,128)(2,1)S(1)} async-done(((bf16[16,64,576]{2,1,0:T(8,128)(2,1)}), bf16[16,64,576]{2,1,0:T(8,128)(2,1)S(1)}, u32[]{:S(2)}, u32[]{:S(2)}) %all-to-all-start.1) | async-done | bytes 1179680 | tf_op jit(solution)/shard_map/all_to_all | solution.py:261
  97.6 0.2 sum_parts.1
  97.8 0.1 collective-permute-start.6
  97.9 0.0 collective-permute-done.4.refs_1_
  97.9 0.0 collective-permute-done.5.refs_2_
  97.9 4.5 %add.3.after_ref = f32[64,16,576]{2,1,0:T(8,128)} custom-call(f32[64,16,576]{2,1,0:T(8,128)} %bitcast.26, f32[64,16,576]{2,1,0:T(8,128)} %collective-permute-done.4.refs_1_, bf16[64,16,576]{2,1,0:T(8,128)(2,1)S(1)} %collective-permute-done.5.refs_2_), custom_call_target="tpu_custom_call" | custom-call | flops 1179648 | bytes 2359296 | tf_op jit(solution)/shard_map/add/pallas_call | solution.py:180
  102.5 0.0 collective-permute-done.6.other_ref
  102.5 0.6 join.1
Async XLA Ops:
  0.6 11.9 %copy-start.1 = (f32[128,16]{0,1:T(8,128)S(1)}, f32[128,16]{0,1:T(8,128)}, u32[]{:S(2)}) copy-start(f32[128,16]{0,1:T(8,128)} %param.8) | copy-start | bytes 24580
  0.6 11.9 %copy-start.2 = (f32[128,16]{0,1:T(8,128)S(1)}, f32[128,16]{0,1:T(8,128)}, u32[]{:S(2)}) copy-start(f32[128,16]{0,1:T(8,128)} %param.9) | copy-start | bytes 24580
  0.7 21.2 %collective-permute-start = (bf16[128,16,576]{0,2,1:T(8,128)(2,1)}, bf16[128,16,576]{0,2,1:T(8,128)(2,1)}, u32[]{:S(2)}, u32[]{:S(2)}) collective-permute-start(bf16[128,16,576]{0,2,1:T(8,128)(2,1)} %param.5), channel_id=1, source_target_pairs={{0,16},{16,0},{1,17},{17,1},{2,18},{18,2},{3,19},{19,3},{4,20},{20... | collective-permute-start | bytes 7077896 | tf_op jit(solution)/shard_map/ppermute | solution.py:38
  0.7 32.7 %collective-permute-start.1 = (bf16[128,16,512]{2,1,0:T(8,128)(2,1)}, bf16[128,16,512]{2,1,0:T(8,128)(2,1)S(1)}, u32[]{:S(2)}, u32[]{:S(2)}) collective-permute-start(bf16[128,16,512]{2,1,0:T(8,128)(2,1)} %param.7), channel_id=1, source_target_pairs={{0,16},{16,0},{1,17},{17,1},{2,18},{18,2},{3,19},{19,3},{4,20},{20... | collective-permute-start | bytes 6291464 | tf_op jit(solution)/shard_map/ppermute | solution.py:38
  3.2 30.2 %all-to-all-start = ((bf16[32,32,576]{2,1,0:T(8,128)(2,1)}), bf16[32,32,576]{2,1,0:T(8,128)(2,1)S(1)}, u32[]{:S(2)}, u32[]{:S(2)}) async-start(bf16[32,32,576]{2,1,0:T(8,128)(2,1)} %broadcast_in_dim.13), calls=%async_computation | async-start | bytes 2621440 | tf_op jit(solution)/shard_map/all_to_all | solution.py:236
  13.1 6.4 %collective-permute-start.2 = (f32[2,128,16]{1,2,0:T(8,128)}, f32[2,128,16]{1,2,0:T(8,128)}, u32[]{:S(2)}, u32[]{:S(2)}) collective-permute-start(f32[2,128,16]{1,2,0:T(8,128)} %pad_maximum_fusion), channel_id=1, source_target_pairs={{0,16},{16,0},{1,17},{17,1},{2,18},{18,2},{3,19},{19,3},{4,20},{20... | collective-permute-start | bytes 49160 | tf_op jit(solution)/shard_map/ppermute | solution.py:38
  33.4 16.2 %copy-start = (f32[4,2,512]{2,1,0:T(2,128)S(1)}, f32[4,2,512]{2,1,0:T(2,128)}, u32[]{:S(2)}) copy-start(f32[4,2,512]{2,1,0:T(2,128)} %get-tuple-element.24.refs_7_.refs_4_) | copy-start | bytes 49156
  49.0 8.7 %collective-permute-start.3 = (f32[64,16,576]{2,1,0:T(8,128)}, f32[64,16,576]{2,1,0:T(8,128)S(1)}, u32[]{:S(2)}, u32[]{:S(2)}) collective-permute-start(f32[64,16,576]{2,1,0:T(8,128)} %bitcast.31), channel_id=1, source_target_pairs={{0,16},{16,0},{1,17},{17,1},{2,18},{18,2},{3,19},{19,3},{4,20},{20... | collective-permute-start | bytes 7077896 | tf_op jit(solution)/shard_map/ppermute | solution.py:38
  49.1 48.8 %collective-permute-start.4 = (f32[64,16,576]{2,1,0:T(8,128)}, f32[64,16,576]{2,1,0:T(8,128)}, u32[]{:S(2)}, u32[]{:S(2)}) collective-permute-start(f32[64,16,576]{2,1,0:T(8,128)} %bitcast.30), channel_id=1, source_target_pairs={{0,16},{16,0},{1,17},{17,1},{2,18},{18,2},{3,19},{19,3},{4,20},{20... | collective-permute-start | bytes 7077896 | tf_op jit(solution)/shard_map/ppermute | solution.py:38
  59.6 38.3 %collective-permute-start.5 = (bf16[64,16,576]{2,1,0:T(8,128)(2,1)}, bf16[64,16,576]{2,1,0:T(8,128)(2,1)S(1)}, u32[]{:S(2)}, u32[]{:S(2)}) collective-permute-start(bf16[64,16,576]{2,1,0:T(8,128)(2,1)} %add.2.refs_7_), channel_id=1, source_target_pairs={{0,1},{1,0},{2,3},{3,2},{4,5},{5,4},{6,7},{7,6},{8,9},{9,8},{10,11... | collective-permute-start | bytes 3538952 | tf_op jit(solution)/shard_map/ppermute | solution.py:38
  72.1 25.5 %all-to-all-start.1 = ((bf16[16,64,576]{2,1,0:T(8,128)(2,1)}), bf16[16,64,576]{2,1,0:T(8,128)(2,1)S(1)}, u32[]{:S(2)}, u32[]{:S(2)}) async-start(bf16[16,64,576]{2,1,0:T(8,128)(2,1)} %bitcast.27), calls=%async_computation.1 | async-start | bytes 2621440 | tf_op jit(solution)/shard_map/all_to_all | solution.py:261
  97.8 4.7 %collective-permute-start.6 = (f32[32,576]{1,0:T(8,128)S(1)}, f32[32,576]{1,0:T(8,128)S(1)}, u32[]{:S(2)}, u32[]{:S(2)}) collective-permute-start(f32[32,576]{1,0:T(8,128)S(1)} %get-tuple-element.23), channel_id=1, source_target_pairs={{0,2},{2,0},{1,3},{3,1},{4,6},{6,4},{5,7},{7,5},{8,10},{10,8},{9,1... | collective-permute-start | bytes 221192 | tf_op jit(solution)/shard_map/ppermute | solution.py:38

commit v5 on v4

--- a/solution.py
+++ b/solution.py
@@ -15,6 +15,7 @@
 CHIPS = ("z", "x", "y_lo")
 PLANE = ("z", "x")
 TILE = 512
+PIECES = 4
 
 NT = (((1,), (1,)), ((), ()))
 NN = (((1,), (0,)), ((), ()))
@@ -32,6 +33,22 @@
 
 def in_hbm(array):
     return pltpu.with_memory_space_constraint(array, pltpu.HBM)
+
+
+def core_sum_kernel(mine_ref, theirs_ref, out_ref):
+    out_ref[...] = (mine_ref[...] + theirs_ref[...]).astype(out_ref.dtype)
+
+
+def core_sum(mine, theirs):
+    return pl.pallas_call(
+        core_sum_kernel,
+        in_specs=[VMEM, VMEM],
+        out_specs=VMEM,
+        out_shape=pltpu.VMEM(mine.shape, jnp.bfloat16),
+        compiler_params=pltpu.CompilerParams(vmem_limit_bytes=4 << 20),
+        cost_estimate=pl.CostEstimate(flops=mine.size, bytes_accessed=mine.size, transcendentals=0),
+        name="core_sum",
+    )(in_vmem(mine), in_vmem(theirs))
 
 
 def swap(array, axis):
@@ -47,6 +64,7 @@
     dq_refs = take(n_halves)
     dkv_ref = refs.pop(0) if last else None
     key_acc, value_acc, q_tiles, sems, *refs = refs
+    dkv_tiles = refs.pop() if last else None
     dq_tiles = [] if stays else [refs.pop(0)]
     do_tiles = refs
     rows, width = value_acc.shape
@@ -82,10 +100,11 @@
         probs = jnp.exp2(scores * (softmax_scale * log2_e) - stats[0:1, :] * log2_e)
         dscores = (probs * (dprobs - stats[1:2, :])).astype(jnp.bfloat16)
         dq_at = dq_refs[tile // per_half].at[pl.ds(tile % per_half * TILE, TILE), :]
+        query_part = f32_dot(keys_t, dscores, NN).T
         if stays:
-            dq_at[...] = f32_dot(keys_t, dscores, NN).T
+            dq_at[...] = query_part
         else:
-            dq_tiles[0][tile] = f32_dot(keys_t, dscores, NN).T
+            dq_tiles[0][tile] = query_part
             result = pltpu.make_async_copy(dq_tiles[0].at[tile], dq_at, sems.at[2, tile])
             result.start()
             results.append(result)
@@ -100,14 +119,20 @@
         else:
             key_acc[...] = sum_in[0][...] + key_part
             value_acc[...] = sum_in[1][...] + value_part
-
-    if last:
-        shape = dkv_ref.shape[:2]
-        key_sum = key_acc[...].T * softmax_scale
-        summed = key_sum[:, :width] + value_acc[...]
-        dkv_ref[:, :, :width] = summed.astype(dkv_ref.dtype).reshape(shape + (width,))
-        rest = key_sum[:, width:]
-        dkv_ref[:, :, width:] = rest.astype(dkv_ref.dtype).reshape(shape + (key_width - width,))
+        if last and tile == len(copies) - 1:
+            some = dkv_tiles.shape[0] // PIECES
+            for piece in range(PIECES):
+                shards = pl.ds(piece * some, some)
+                at = slice(piece * rows // PIECES, (piece + 1) * rows // PIECES)
+                shape = (some, dkv_tiles.shape[1])
+                key_sum = key_acc[:, at].T * softmax_scale
+                summed = key_sum[:, :width] + value_acc[at, :]
+                dkv_tiles[shards, :, :width] = summed.astype(dkv_tiles.dtype).reshape(shape + (width,))
+                rest = key_sum[:, width:].astype(dkv_tiles.dtype)
+                dkv_tiles[shards, :, width:] = rest.reshape(shape + (key_width - width,))
+                result = pltpu.make_async_copy(dkv_tiles.at[shards], dkv_ref.at[shards], sems.at[3, piece])
+                result.start()
+                results.append(result)
     for result in results:
         result.wait()
 
@@ -127,7 +152,7 @@
     out_specs = [VMEM if stays else HBM] * halves
     scratch = [
         pltpu.VMEM((tiles, TILE, key_width), queries.dtype),
-        pltpu.SemaphoreType.DMA((3, tiles)),
+        pltpu.SemaphoreType.DMA((4, max(tiles, PIECES))),
     ]
     if not stays:
         scratch.append(pltpu.VMEM((tiles, TILE, key_width), jnp.float32))
@@ -141,13 +166,15 @@
         in_specs += [VMEM, VMEM]
     if last:
         out_shape.append(pltpu.HBM(keys.shape, keys.dtype))
-        out_specs.append(pl.BlockSpec(keys.shape, lambda i, at: (0, 0, 0)))
+        out_specs.append(HBM)
         scratch = [pltpu.VMEM(shape, jnp.float32) for shape in sum_shapes] + scratch
+        scratch.append(pltpu.VMEM(keys.shape, keys.dtype))
     else:
         out_shape += [pltpu.VMEM(shape, jnp.float32) for shape in sum_shapes]
         out_specs += [VMEM, VMEM]
-    operands += [in_hbm(array) for array in before]
-    in_specs += [HBM] * len(before)
+    place, spec = (in_hbm, HBM) if first else (in_vmem, VMEM)
+    operands += [place(array) for array in before]
+    in_specs += [spec] * len(before)
     return pl.pallas_call(
         functools.partial(grads_kernel, first, last, stays, do_stays, halves, len(before)),
         grid_spec=pltpu.PrefetchScalarGridSpec(
@@ -253,7 +280,7 @@
     dq_sent_theirs, dq_theirs, *sums = grads(keys, sent, theirs, halves=2, do_stays=True, before=mine)
     returned = swap(dq_sent_theirs.reshape(whole), "core")
     dq_sent_mine, *sums = grads(keys, sent, mine, sums=sums, stays=True)
-    over_cores = add([dq_sent_mine.reshape(whole), returned], jnp.bfloat16)
+    over_cores = core_sum(dq_sent_mine.reshape(whole), returned)
     received = swap(over_cores, "y_hi")
     dq_mine, dkv = grads(keys, kept, mine, sums=sums, last=True, before=[over_cores])
     returned = swap(dq_theirs.reshape(whole), "core")

time: 104 us -> 103 us (level)
  Pallas kernels: 40.5 us -> 39.1 us
    pallas_call x2 -> x1, Pallas kernels: 6.38 us -> 4.99 us  [add(): pl.pallas_call(functools.partial(add_kernel, out_scale), grid=(steps,), i...]
  transfers between devices with their start and end apart: 9 -> 9, of which waited for: 2 -> 2; matrix products, arithmetic and copies ran while one was open for 16% -> 16% of each run, Pallas kernels for 24% -> 22%
where the time goes in v5:
time: 103 us; the launch traced here: 102 us
  Pallas kernels  39.1 us (38%)
  waiting for transfers between devices  28.5 us (28%)
  starting transfers between devices  17.4 us (17%)
  local copies, waits for them, and re-layouts  14.3 us (14%)
  other arithmetic  1.95 us (2%)
    pallas_call x3, Pallas kernels, grads(): pl.pallas_call(functools.partial(grads_kernel, first, last, stays, do_sta...  33.1 us
    all_to_all x1, waiting for transfers between devices, on_device(): lax.all_to_all(dkv.reshape(-1, 2 * shard, key_width), PLANE, 0, 0, tiled=...  21.8 us
    all_to_all x1, starting transfers between devices, on_device(): keys = lax.all_to_all(spread, CHIPS, 0, 0, tiled=True)  9.26 us
    all_to_all x1, waiting for transfers between devices, on_device(): keys = lax.all_to_all(spread, CHIPS, 0, 0, tiled=True)  6.69 us
    ppermute x2, local copies, waits for them, and re-layouts, swap(): return lax.ppermute(array, axis, [(0, 1), (1, 0)])  5.73 us
    unnamed x9, local copies, waits for them, and re-layouts  5.06 us
    pallas_call x1, Pallas kernels, add(): pl.pallas_call(functools.partial(add_kernel, out_scale), grid=(steps,), i...  4.99 us
    ppermute x7, starting transfers between devices, swap(): return lax.ppermute(array, axis, [(0, 1), (1, 0)])  4.44 us
  transfers between devices with their start and end apart: 9, of which 2 were waited for; matrix products, arithmetic and copies ran while one was open for 16% of the time, Pallas kernels for 22%

profile of v5, /device:TPU:0, one launch (start us, length us, event | category | flops | bytes accessed | tf_op | source)
XLA Modules:
  0.0 102.1 jit_solution(1642985967152979852)
XLA Ops:
  0.6 0.0 copy-start.1
  0.6 0.0 copy-start.2
  0.7 0.1 collective-permute-start
  0.7 0.5 collective-permute-start.1
  1.2 2.0 %broadcast_in_dim.13 = bf16[32,32,576]{2,1,0:T(8,128)(2,1)} broadcast(bf16[32,576]{1,0:T(8,128)(2,1)} %param.6), dimensions={1,2} | broadcast | bytes 1216512 | tf_op jit(solution)/shard_map/broadcast_in_dim | solution.py:262
  3.2 9.3 %all-to-all-start = ((bf16[32,32,576]{2,1,0:T(8,128)(2,1)}), bf16[32,32,576]{2,1,0:T(8,128)(2,1)S(1)}, u32[]{:S(2)}, u32[]{:S(2)}) async-start(bf16[32,32,576]{2,1,0:T(8,128)(2,1)} %broadcast_in_dim.13), calls=%async_computation | async-start | bytes 2621440 | tf_op jit(solution)/shard_map/all_to_all | solution.py:263
  12.5 0.0 copy-done.1
  12.5 0.0 copy-done.2
  12.5 0.6 pad_maximum_fusion
  13.1 0.0 collective-permute-start.2
  13.1 0.1 copy.14
  13.2 0.1 copy.15
  13.3 4.8 %copy.13 = bf16[128,16,576]{2,1,0:T(8,128)(2,1)} copy(bf16[128,16,576]{0,2,1:T(8,128)(2,1)} %param.5) | data formatting | bytes 4718592 | tf_op args[0]
  18.2 0.7 stack.21
  18.9 0.7 stack.22
  19.5 0.0 collective-permute-done.2
  19.5 0.8 copy.19
  20.4 0.1 reshape.44
  20.5 1.3 %maximum_bitcast_fusion = (f32[4,2,512]{2,1,0:T(2,128)}, f32[4,2,512]{2,1,0:T(2,128)S(1)}) fusion(f32[1,4,512]{2,0,1:T(1,128)} %stack.22, f32[1,4,512]{2,0,1:T(1,128)} %stack.21, f32[2,4,512]{2,1,0:T(4,128)S(1)} %reshape.44), kind=kLoop, calls=%fused_computation | loop fusion | flops 4096 | bytes 65536 | tf_op jit(solution)/shard_map/transpose | solution.py:270
  21.8 0.0 collective-permute-done
  21.8 4.9 %copy.18 = bf16[128,16,576]{2,1,0:T(8,128)(2,1)} copy(bf16[128,16,576]{0,2,1:T(8,128)(2,1)} %collective-permute-done) | data formatting | bytes 4718592 | tf_op jit(solution)/shard_map/ppermute | solution.py:55
  26.8 6.7 %all-to-all-done.refs_1_ = bf16[32,32,576]{2,1,0:T(8,128)(2,1)S(1)} async-done(((bf16[32,32,576]{2,1,0:T(8,128)(2,1)}), bf16[32,32,576]{2,1,0:T(8,128)(2,1)S(1)}, u32[]{:S(2)}, u32[]{:S(2)}) %all-to-all-start) | async-done | bytes 1179680 | tf_op jit(solution)/shard_map/all_to_all | solution.py:263
  33.4 0.0 collective-permute-done.1
  33.4 0.0 copy-start
  33.4 15.6 %grads.3 = (f32[1024,576]{1,0:T(8,128)}, f32[1024,576]{1,0:T(8,128)}, f32[576,1024]{1,0:T(8,128)S(1)}, f32[1024,512]{1,0:T(8,128)S(1)}) custom-call(s32[1]{0:T(128)S(6)} %sub.3.refs_0_, bf16[32,32,576]{2,1,0:T(8,128)(2,1)S(1)} %all-to-all-done.refs_1_, bf16[2048,576]{1,0:T(8,128)(2,1)} %bitcast.25, bf16[2048,512]{1,0:T(8,128)(2,1)S(1)} %bitcast.18, ...), custom_call_target="tpu_custom_call" | custom-call | flops 1048576 | bytes 1179648 | tf_op jit(solution)/shard_map/grads/pallas_call | solution.py:178
  49.1 0.1 collective-permute-start.3
  49.2 0.5 collective-permute-start.4
  49.7 0.0 copy-done
  49.7 8.2 %grads.4 = (f32[1024,576]{1,0:T(8,128)S(1)}, f32[576,1024]{1,0:T(8,128)S(1)}, f32[1024,512]{1,0:T(8,128)S(1)}) custom-call(s32[1]{0:T(128)S(6)} %sub.3.refs_0_, bf16[32,32,576]{2,1,0:T(8,128)(2,1)S(1)} %all-to-all-done.refs_1_, bf16[2048,576]{1,0:T(8,128)(2,1)} %bitcast.20, ...), custom_call_target="tpu_custom_call", output_to_operand_aliasing={{1}: (5, {}), {2}: (6, {})} | custom-call | flops 1048576 | bytes 1179648 | tf_op jit(solution)/shard_map/grads/pallas_call | solution.py:178
  57.9 0.0 collective-permute-done.3.theirs_ref
  57.9 0.2 core_sum.1.refs_7_
  58.1 3.2 %collective-permute-start.5 = (bf16[64,16,576]{2,1,0:T(8,128)(2,1)S(1)}, bf16[64,16,576]{2,1,0:T(8,128)(2,1)}, u32[]{:S(2)}, u32[]{:S(2)}) collective-permute-start(bf16[64,16,576]{2,1,0:T(8,128)(2,1)S(1)} %core_sum.1.refs_7_), channel_id=1, source_target_pairs={{0,1},{1,0},{2,3},{3,2},{4,5},{5,4},{6,7},{7,6},{8,9},{9,8},{10,11... | collective-permute-start | bytes 3538952 | tf_op jit(solution)/shard_map/ppermute | solution.py:55
  61.3 9.3 %grads.5 = (f32[1024,576]{1,0:T(8,128)}, bf16[32,32,576]{2,1,0:T(8,128)(2,1)}) custom-call(s32[1]{0:T(128)} %bitcast.refs_0_, bf16[32,32,576]{2,1,0:T(8,128)(2,1)S(1)} %all-to-all-done.refs_1_, bf16[2048,576]{1,0:T(8,128)(2,1)} %bitcast.21, bf16[2048,512]{1,0:T(8,128)(2,1)} %bitcast.24, f32[4,2,512]{2,1,0:T(2,128)S(1)} %copy-done, ...), custom_call_target="tpu_custom_call" | custom-call | flops 1048576 | bytes 1179648 | tf_op jit(solution)/shard_map/grads/pallas_call | solution.py:178
  70.6 3.7 %all-to-all-start.1 = ((bf16[16,64,576]{2,1,0:T(8,128)(2,1)}), bf16[16,64,576]{2,1,0:T(8,128)(2,1)S(1)}, u32[]{:S(2)}, u32[]{:S(2)}) async-start(bf16[16,64,576]{2,1,0:T(8,128)(2,1)} %bitcast.27), calls=%async_computation.1 | async-start | bytes 2621440 | tf_op jit(solution)/shard_map/all_to_all | solution.py:288
  74.3 21.8 %all-to-all-done.1.parts_ref = bf16[16,64,576]{2,1,0:T(8,128)(2,1)S(1)} async-done(((bf16[16,64,576]{2,1,0:T(8,128)(2,1)}), bf16[16,64,576]{2,1,0:T(8,128)(2,1)S(1)}, u32[]{:S(2)}, u32[]{:S(2)}) %all-to-all-start.1) | async-done | bytes 1179680 | tf_op jit(solution)/shard_map/all_to_all | solution.py:288
  96.1 0.2 sum_parts.1
  96.3 0.1 collective-permute-start.6
  96.4 0.0 collective-permute-done.4.refs_1_
  96.4 0.0 collective-permute-done.5.refs_2_
  96.4 5.0 %add.1.after_ref = f32[64,16,576]{2,1,0:T(8,128)} custom-call(f32[64,16,576]{2,1,0:T(8,128)} %bitcast.26, f32[64,16,576]{2,1,0:T(8,128)} %collective-permute-done.4.refs_1_, bf16[64,16,576]{2,1,0:T(8,128)(2,1)} %collective-permute-done.5.refs_2_), custom_call_target="tpu_custom_call" | custom-call | flops 1179648 | bytes 2359296 | tf_op jit(solution)/shard_map/add/pallas_call | solution.py:207
  101.4 0.0 collective-permute-done.6.other_ref
  101.4 0.6 join.1
Async XLA Ops:
  0.6 11.9 %copy-start.1 = (f32[128,16]{0,1:T(8,128)S(1)}, f32[128,16]{0,1:T(8,128)}, u32[]{:S(2)}) copy-start(f32[128,16]{0,1:T(8,128)} %param.8) | copy-start | bytes 24580
  0.6 11.9 %copy-start.2 = (f32[128,16]{0,1:T(8,128)S(1)}, f32[128,16]{0,1:T(8,128)}, u32[]{:S(2)}) copy-start(f32[128,16]{0,1:T(8,128)} %param.9) | copy-start | bytes 24580
  0.7 21.2 %collective-permute-start = (bf16[128,16,576]{0,2,1:T(8,128)(2,1)}, bf16[128,16,576]{0,2,1:T(8,128)(2,1)}, u32[]{:S(2)}, u32[]{:S(2)}) collective-permute-start(bf16[128,16,576]{0,2,1:T(8,128)(2,1)} %param.5), channel_id=1, source_target_pairs={{0,16},{16,0},{1,17},{17,1},{2,18},{18,2},{3,19},{19,3},{4,20},{20... | collective-permute-start | bytes 7077896 | tf_op jit(solution)/shard_map/ppermute | solution.py:55
  0.7 32.7 %collective-permute-start.1 = (bf16[128,16,512]{2,1,0:T(8,128)(2,1)}, bf16[128,16,512]{2,1,0:T(8,128)(2,1)S(1)}, u32[]{:S(2)}, u32[]{:S(2)}) collective-permute-start(bf16[128,16,512]{2,1,0:T(8,128)(2,1)} %param.7), channel_id=1, source_target_pairs={{0,16},{16,0},{1,17},{17,1},{2,18},{18,2},{3,19},{19,3},{4,20},{20... | collective-permute-start | bytes 6291464 | tf_op jit(solution)/shard_map/ppermute | solution.py:55
  3.2 30.2 %all-to-all-start = ((bf16[32,32,576]{2,1,0:T(8,128)(2,1)}), bf16[32,32,576]{2,1,0:T(8,128)(2,1)S(1)}, u32[]{:S(2)}, u32[]{:S(2)}) async-start(bf16[32,32,576]{2,1,0:T(8,128)(2,1)} %broadcast_in_dim.13), calls=%async_computation | async-start | bytes 2621440 | tf_op jit(solution)/shard_map/all_to_all | solution.py:263
  13.1 6.4 %collective-permute-start.2 = (f32[2,128,16]{1,2,0:T(8,128)}, f32[2,128,16]{1,2,0:T(8,128)}, u32[]{:S(2)}, u32[]{:S(2)}) collective-permute-start(f32[2,128,16]{1,2,0:T(8,128)} %pad_maximum_fusion), channel_id=1, source_target_pairs={{0,16},{16,0},{1,17},{17,1},{2,18},{18,2},{3,19},{19,3},{4,20},{20... | collective-permute-start | bytes 49160 | tf_op jit(solution)/shard_map/ppermute | solution.py:55
  33.4 16.2 %copy-start = (f32[4,2,512]{2,1,0:T(2,128)S(1)}, f32[4,2,512]{2,1,0:T(2,128)}, u32[]{:S(2)}) copy-start(f32[4,2,512]{2,1,0:T(2,128)} %get-tuple-element.24.refs_7_.refs_4_) | copy-start | bytes 49156
  49.1 8.8 %collective-permute-start.3 = (f32[64,16,576]{2,1,0:T(8,128)}, f32[64,16,576]{2,1,0:T(8,128)S(1)}, u32[]{:S(2)}, u32[]{:S(2)}) collective-permute-start(f32[64,16,576]{2,1,0:T(8,128)} %bitcast.31), channel_id=1, source_target_pairs={{0,16},{16,0},{1,17},{17,1},{2,18},{18,2},{3,19},{19,3},{4,20},{20... | collective-permute-start | bytes 7077896 | tf_op jit(solution)/shard_map/ppermute | solution.py:55
  49.2 47.2 %collective-permute-start.4 = (f32[64,16,576]{2,1,0:T(8,128)}, f32[64,16,576]{2,1,0:T(8,128)}, u32[]{:S(2)}, u32[]{:S(2)}) collective-permute-start(f32[64,16,576]{2,1,0:T(8,128)} %bitcast.30), channel_id=1, source_target_pairs={{0,16},{16,0},{1,17},{17,1},{2,18},{18,2},{3,19},{19,3},{4,20},{20... | collective-permute-start | bytes 7077896 | tf_op jit(solution)/shard_map/ppermute | solution.py:55
  58.1 38.3 %collective-permute-start.5 = (bf16[64,16,576]{2,1,0:T(8,128)(2,1)S(1)}, bf16[64,16,576]{2,1,0:T(8,128)(2,1)}, u32[]{:S(2)}, u32[]{:S(2)}) collective-permute-start(bf16[64,16,576]{2,1,0:T(8,128)(2,1)S(1)} %core_sum.1.refs_7_), channel_id=1, source_target_pairs={{0,1},{1,0},{2,3},{3,2},{4,5},{5,4},{6,7},{7,6},{8,9},{9,8},{10,11... | collective-permute-start | bytes 3538952 | tf_op jit(solution)/shard_map/ppermute | solution.py:55
  70.6 25.5 %all-to-all-start.1 = ((bf16[16,64,576]{2,1,0:T(8,128)(2,1)}), bf16[16,64,576]{2,1,0:T(8,128)(2,1)S(1)}, u32[]{:S(2)}, u32[]{:S(2)}) async-start(bf16[16,64,576]{2,1,0:T(8,128)(2,1)} %bitcast.27), calls=%async_computation.1 | async-start | bytes 2621440 | tf_op jit(solution)/shard_map/all_to_all | solution.py:288
  96.3 5.1 %collective-permute-start.6 = (f32[32,576]{1,0:T(8,128)S(1)}, f32[32,576]{1,0:T(8,128)S(1)}, u32[]{:S(2)}, u32[]{:S(2)}) collective-permute-start(f32[32,576]{1,0:T(8,128)S(1)} %get-tuple-element.23), channel_id=1, source_target_pairs={{0,2},{2,0},{1,3},{3,1},{4,6},{6,4},{5,7},{7,5},{8,10},{10,8},{9,1... | collective-permute-start | bytes 221192 | tf_op jit(solution)/shard_map/ppermute | solution.py:55

commit v6 on v5

--- a/solution.py
+++ b/solution.py
@@ -15,6 +15,7 @@
 CHIPS = ("z", "x", "y_lo")
 PLANE = ("z", "x")
 TILE = 512
+LANES = 128
 PIECES = 4
 
 NT = (((1,), (1,)), ((), ()))
@@ -124,12 +125,15 @@
             for piece in range(PIECES):
                 shards = pl.ds(piece * some, some)
                 at = slice(piece * rows // PIECES, (piece + 1) * rows // PIECES)
-                shape = (some, dkv_tiles.shape[1])
+                shard = rows // dkv_tiles.shape[0]
                 key_sum = key_acc[:, at].T * softmax_scale
-                summed = key_sum[:, :width] + value_acc[at, :]
-                dkv_tiles[shards, :, :width] = summed.astype(dkv_tiles.dtype).reshape(shape + (width,))
-                rest = key_sum[:, width:].astype(dkv_tiles.dtype)
-                dkv_tiles[shards, :, width:] = rest.reshape(shape + (key_width - width,))
+                summed = (key_sum[:, :width] + value_acc[at, :]).astype(dkv_tiles.dtype)
+                for block in range(width // LANES):
+                    columns = summed[:, block * LANES : (block + 1) * LANES].reshape(some, shard, LANES)
+                    dkv_tiles[shards, block * shard : (block + 1) * shard, :] = columns
+                rest = key_sum[:, width:].astype(dkv_tiles.dtype).reshape(some, 2, shard // 2, LANES // 2)
+                rest = jnp.concatenate([rest[:, 0], rest[:, 1]], axis=-1)
+                dkv_tiles[shards, width // LANES * shard :, :] = rest
                 result = pltpu.make_async_copy(dkv_tiles.at[shards], dkv_ref.at[shards], sems.at[3, piece])
                 result.start()
                 results.append(result)
@@ -165,10 +169,11 @@
         operands += [in_vmem(array) for array in sums]
         in_specs += [VMEM, VMEM]
     if last:
-        out_shape.append(pltpu.HBM(keys.shape, keys.dtype))
+        packed = (shards, shard * key_width // LANES, LANES)
+        out_shape.append(pltpu.HBM(packed, keys.dtype))
         out_specs.append(HBM)
         scratch = [pltpu.VMEM(shape, jnp.float32) for shape in sum_shapes] + scratch
-        scratch.append(pltpu.VMEM(keys.shape, keys.dtype))
+        scratch.append(pltpu.VMEM(packed, keys.dtype))
     else:
         out_shape += [pltpu.VMEM(shape, jnp.float32) for shape in sum_shapes]
         out_specs += [VMEM, VMEM]
@@ -219,21 +224,26 @@
 
 
 def sum_kernel(place, parts_ref, mine_ref, other_ref):
-    shard = mine_ref.shape[0]
+    shard, key_width = mine_ref.shape
+    packed = parts_ref.shape[1] // 2
+    blocks = key_width // LANES
     for out_ref, at in ((mine_ref, place[0]), (other_ref, 1 - place[0])):
-        rows = pl.ds(pl.multiple_of(at * shard, shard), shard)
+        rows = pl.ds(pl.multiple_of(at * packed, shard // 2), packed)
         total = parts_ref[0, rows, :].astype(jnp.float32)
         for part in range(1, parts_ref.shape[0]):
             total += parts_ref[part, rows, :].astype(jnp.float32)
-        out_ref[...] = total
-
-
-def sum_parts(parts, place):
-    _, rows, key_width = parts.shape
+        for block in range(blocks):
+            out_ref[:, block * LANES : (block + 1) * LANES] = total[block * shard : (block + 1) * shard, :]
+        rest = total[blocks * shard :, :]
+        out_ref[: shard // 2, blocks * LANES :] = rest[:, : LANES // 2]
+        out_ref[shard // 2 :, blocks * LANES :] = rest[:, LANES // 2 :]
+
+
+def sum_parts(parts, place, shape):
     return pl.pallas_call(
         sum_kernel,
         grid_spec=pltpu.PrefetchScalarGridSpec(num_scalar_prefetch=1, grid=(1,), in_specs=[VMEM], out_specs=[VMEM, VMEM]),
-        out_shape=[pltpu.VMEM((rows // 2, key_width), jnp.float32)] * 2,
+        out_shape=[pltpu.VMEM(shape, jnp.float32)] * 2,
         compiler_params=pltpu.CompilerParams(vmem_limit_bytes=4 << 20),
         name="sum_parts",
     )(place, in_vmem(parts))
@@ -285,8 +295,8 @@
     dq_mine, dkv = grads(keys, kept, mine, sums=sums, last=True, before=[over_cores])
     returned = swap(dq_theirs.reshape(whole), "core")
     query_grad = add([dq_mine.reshape(whole), returned, received], jnp.float32, softmax_scale, resident=[False, False, True])
-    parts = lax.all_to_all(dkv.reshape(-1, 2 * shard, key_width), PLANE, 0, 0, tiled=True)
-    own, other = sum_parts(parts, lax.axis_index("y_lo").astype(jnp.int32)[None])
+    parts = lax.all_to_all(dkv.reshape(-1, 2 * dkv.shape[1], LANES), PLANE, 0, 0, tiled=True)
+    own, other = sum_parts(parts, lax.axis_index("y_lo").astype(jnp.int32)[None], latent.shape)
     return (query_grad, join(own, swap(other, "y_lo"), query_grad))
 
 

time: 103 us -> 101 us (0.981)
  waiting for transfers between devices: 28.5 us -> 26.6 us
    all_to_all x1, waiting for transfers between devices: 21.8 us -> 19.9 us  [on_device(): lax.all_to_all(dkv.reshape(-1, 2 * dkv.shape[1], LANES), PLANE, 0, 0, til...]
  transfers between devices with their start and end apart: 9 -> 9, of which waited for: 2 -> 2; matrix products, arithmetic and copies ran while one was open for 16% -> 16% of each run, Pallas kernels for 22% -> 23%
where the time goes in v6:
time: 101 us; the launch traced here: 100 us
  Pallas kernels  39.1 us (39%)
  waiting for transfers between devices  26.6 us (26%)
  starting transfers between devices  17.4 us (17%)
  local copies, waits for them, and re-layouts  14.3 us (14%)
  other arithmetic  1.95 us (2%)
    pallas_call x3, Pallas kernels, grads(): pl.pallas_call(functools.partial(grads_kernel, first, last, stays, do_sta...  33.1 us
    all_to_all x1, waiting for transfers between devices, on_device(): lax.all_to_all(dkv.reshape(-1, 2 * dkv.shape[1], LANES), PLANE, 0, 0, til...  19.9 us
    all_to_all x1, starting transfers between devices, on_device(): keys = lax.all_to_all(spread, CHIPS, 0, 0, tiled=True)  9.26 us
    all_to_all x1, waiting for transfers between devices, on_device(): keys = lax.all_to_all(spread, CHIPS, 0, 0, tiled=True)  6.69 us
    ppermute x2, local copies, waits for them, and re-layouts, swap(): return lax.ppermute(array, axis, [(0, 1), (1, 0)])  5.73 us
    unnamed x9, local copies, waits for them, and re-layouts  5.06 us
    pallas_call x1, Pallas kernels, add(): pl.pallas_call(functools.partial(add_kernel, out_scale), grid=(steps,), i...  4.99 us
    ppermute x7, starting transfers between devices, swap(): return lax.ppermute(array, axis, [(0, 1), (1, 0)])  4.44 us
  transfers between devices with their start and end apart: 9, of which 2 were waited for; matrix products, arithmetic and copies ran while one was open for 16% of the time, Pallas kernels for 23%

profile of v6, /device:TPU:0, one launch (start us, length us, event | category | flops | bytes accessed | tf_op | source)
XLA Modules:
  0.0 100.1 jit_solution(13955320321974063142)
XLA Ops:
  0.6 0.0 copy-start.1
  0.6 0.0 copy-start.2
  0.7 0.1 collective-permute-start
  0.7 0.5 collective-permute-start.1
  1.2 2.0 %broadcast_in_dim.13 = bf16[32,32,576]{2,1,0:T(8,128)(2,1)} broadcast(bf16[32,576]{1,0:T(8,128)(2,1)} %param.6), dimensions={1,2} | broadcast | bytes 1216512 | tf_op jit(solution)/shard_map/broadcast_in_dim | solution.py:272
  3.2 9.3 %all-to-all-start = ((bf16[32,32,576]{2,1,0:T(8,128)(2,1)}), bf16[32,32,576]{2,1,0:T(8,128)(2,1)S(1)}, u32[]{:S(2)}, u32[]{:S(2)}) async-start(bf16[32,32,576]{2,1,0:T(8,128)(2,1)} %broadcast_in_dim.13), calls=%async_computation | async-start | bytes 2621440 | tf_op jit(solution)/shard_map/all_to_all | solution.py:273
  12.5 0.0 copy-done.1
  12.5 0.0 copy-done.2
  12.5 0.6 pad_maximum_fusion
  13.1 0.0 collective-permute-start.2
  13.1 0.1 copy.14
  13.2 0.1 copy.15
  13.3 4.8 %copy.13 = bf16[128,16,576]{2,1,0:T(8,128)(2,1)} copy(bf16[128,16,576]{0,2,1:T(8,128)(2,1)} %param.5) | data formatting | bytes 4718592 | tf_op args[0]
  18.2 0.7 stack.21
  18.9 0.7 stack.22
  19.5 0.0 collective-permute-done.2
  19.5 0.8 copy.19
  20.4 0.1 reshape.44
  20.5 1.3 %maximum_bitcast_fusion = (f32[4,2,512]{2,1,0:T(2,128)}, f32[4,2,512]{2,1,0:T(2,128)S(1)}) fusion(f32[1,4,512]{2,0,1:T(1,128)} %stack.22, f32[1,4,512]{2,0,1:T(1,128)} %stack.21, f32[2,4,512]{2,1,0:T(4,128)S(1)} %reshape.44), kind=kLoop, calls=%fused_computation | loop fusion | flops 4096 | bytes 65536 | tf_op jit(solution)/shard_map/transpose | solution.py:280
  21.8 0.0 collective-permute-done
  21.8 4.9 %copy.18 = bf16[128,16,576]{2,1,0:T(8,128)(2,1)} copy(bf16[128,16,576]{0,2,1:T(8,128)(2,1)} %collective-permute-done) | data formatting | bytes 4718592 | tf_op jit(solution)/shard_map/ppermute | solution.py:56
  26.8 6.7 %all-to-all-done.refs_1_ = bf16[32,32,576]{2,1,0:T(8,128)(2,1)S(1)} async-done(((bf16[32,32,576]{2,1,0:T(8,128)(2,1)}), bf16[32,32,576]{2,1,0:T(8,128)(2,1)S(1)}, u32[]{:S(2)}, u32[]{:S(2)}) %all-to-all-start) | async-done | bytes 1179680 | tf_op jit(solution)/shard_map/all_to_all | solution.py:273
  33.4 0.0 collective-permute-done.1
  33.4 0.0 copy-start
  33.4 15.6 %grads.3 = (f32[1024,576]{1,0:T(8,128)}, f32[1024,576]{1,0:T(8,128)}, f32[576,1024]{1,0:T(8,128)S(1)}, f32[1024,512]{1,0:T(8,128)S(1)}) custom-call(s32[1]{0:T(128)S(6)} %sub.3.refs_0_, bf16[32,32,576]{2,1,0:T(8,128)(2,1)S(1)} %all-to-all-done.refs_1_, bf16[2048,576]{1,0:T(8,128)(2,1)} %bitcast.25, bf16[2048,512]{1,0:T(8,128)(2,1)S(1)} %bitcast.18, ...), custom_call_target="tpu_custom_call" | custom-call | flops 1048576 | bytes 1179648 | tf_op jit(solution)/shard_map/grads/pallas_call | solution.py:183
  49.1 0.1 collective-permute-start.3
  49.2 0.5 collective-permute-start.4
  49.7 0.0 copy-done
  49.7 8.2 %grads.4 = (f32[1024,576]{1,0:T(8,128)S(1)}, f32[576,1024]{1,0:T(8,128)S(1)}, f32[1024,512]{1,0:T(8,128)S(1)}) custom-call(s32[1]{0:T(128)S(6)} %sub.3.refs_0_, bf16[32,32,576]{2,1,0:T(8,128)(2,1)S(1)} %all-to-all-done.refs_1_, bf16[2048,576]{1,0:T(8,128)(2,1)} %bitcast.20, ...), custom_call_target="tpu_custom_call", output_to_operand_aliasing={{1}: (5, {}), {2}: (6, {})} | custom-call | flops 1048576 | bytes 1179648 | tf_op jit(solution)/shard_map/grads/pallas_call | solution.py:183
  57.9 0.0 collective-permute-done.3.theirs_ref
  57.9 0.2 core_sum.1.refs_7_
  58.1 3.2 %collective-permute-start.5 = (bf16[64,16,576]{2,1,0:T(8,128)(2,1)S(1)}, bf16[64,16,576]{2,1,0:T(8,128)(2,1)}, u32[]{:S(2)}, u32[]{:S(2)}) collective-permute-start(bf16[64,16,576]{2,1,0:T(8,128)(2,1)S(1)} %core_sum.1.refs_7_), channel_id=1, source_target_pairs={{0,1},{1,0},{2,3},{3,2},{4,5},{5,4},{6,7},{7,6},{8,9},{9,8},{10,11... | collective-permute-start | bytes 3538952 | tf_op jit(solution)/shard_map/ppermute | solution.py:56
  61.3 9.2 %grads.5 = (f32[1024,576]{1,0:T(8,128)}, bf16[32,144,128]{2,1,0:T(8,128)(2,1)}) custom-call(s32[1]{0:T(128)} %bitcast.refs_0_, bf16[32,32,576]{2,1,0:T(8,128)(2,1)S(1)} %all-to-all-done.refs_1_, bf16[2048,576]{1,0:T(8,128)(2,1)} %bitcast.21, bf16[2048,512]{1,0:T(8,128)(2,1)} %bitcast.24, f32[4,2,512]{2,1,0:T(2,128)S(1)} %copy-done, ...), custom_call_target="tpu_custom_call" | custom-call | flops 1048576 | bytes 1179648 | tf_op jit(solution)/shard_map/grads/pallas_call | solution.py:183
  70.6 3.7 %all-to-all-start.1 = ((bf16[16,288,128]{2,1,0:T(8,128)(2,1)}), bf16[16,288,128]{2,1,0:T(8,128)(2,1)S(1)}, u32[]{:S(2)}, u32[]{:S(2)}) async-start(bf16[16,288,128]{2,1,0:T(8,128)(2,1)} %bitcast.27), calls=%async_computation.1 | async-start | bytes 2359296 | tf_op jit(solution)/shard_map/all_to_all | solution.py:298
  74.3 19.9 %all-to-all-done.1.parts_ref = bf16[16,288,128]{2,1,0:T(8,128)(2,1)S(1)} async-done(((bf16[16,288,128]{2,1,0:T(8,128)(2,1)}), bf16[16,288,128]{2,1,0:T(8,128)(2,1)S(1)}, u32[]{:S(2)}, u32[]{:S(2)}) %all-to-all-start.1) | async-done | bytes 1179680 | tf_op jit(solution)/shard_map/all_to_all | solution.py:298
  94.2 0.2 sum_parts.1
  94.4 0.1 collective-permute-start.6
  94.5 0.0 collective-permute-done.4.refs_1_
  94.5 0.0 collective-permute-done.5.refs_2_
  94.5 5.0 %add.1.after_ref = f32[64,16,576]{2,1,0:T(8,128)} custom-call(f32[64,16,576]{2,1,0:T(8,128)} %bitcast.26, f32[64,16,576]{2,1,0:T(8,128)} %collective-permute-done.4.refs_1_, bf16[64,16,576]{2,1,0:T(8,128)(2,1)} %collective-permute-done.5.refs_2_), custom_call_target="tpu_custom_call" | custom-call | flops 1179648 | bytes 2359296 | tf_op jit(solution)/shard_map/add/pallas_call | solution.py:212
  99.5 0.0 collective-permute-done.6.other_ref
  99.5 0.6 join.1
Async XLA Ops:
  0.6 11.9 %copy-start.1 = (f32[128,16]{0,1:T(8,128)S(1)}, f32[128,16]{0,1:T(8,128)}, u32[]{:S(2)}) copy-start(f32[128,16]{0,1:T(8,128)} %param.8) | copy-start | bytes 24580
  0.6 11.9 %copy-start.2 = (f32[128,16]{0,1:T(8,128)S(1)}, f32[128,16]{0,1:T(8,128)}, u32[]{:S(2)}) copy-start(f32[128,16]{0,1:T(8,128)} %param.9) | copy-start | bytes 24580
  0.7 21.2 %collective-permute-start = (bf16[128,16,576]{0,2,1:T(8,128)(2,1)}, bf16[128,16,576]{0,2,1:T(8,128)(2,1)}, u32[]{:S(2)}, u32[]{:S(2)}) collective-permute-start(bf16[128,16,576]{0,2,1:T(8,128)(2,1)} %param.5), channel_id=1, source_target_pairs={{0,16},{16,0},{1,17},{17,1},{2,18},{18,2},{3,19},{19,3},{4,20},{20... | collective-permute-start | bytes 7077896 | tf_op jit(solution)/shard_map/ppermute | solution.py:56
  0.7 32.7 %collective-permute-start.1 = (bf16[128,16,512]{2,1,0:T(8,128)(2,1)}, bf16[128,16,512]{2,1,0:T(8,128)(2,1)S(1)}, u32[]{:S(2)}, u32[]{:S(2)}) collective-permute-start(bf16[128,16,512]{2,1,0:T(8,128)(2,1)} %param.7), channel_id=1, source_target_pairs={{0,16},{16,0},{1,17},{17,1},{2,18},{18,2},{3,19},{19,3},{4,20},{20... | collective-permute-start | bytes 6291464 | tf_op jit(solution)/shard_map/ppermute | solution.py:56
  3.2 30.2 %all-to-all-start = ((bf16[32,32,576]{2,1,0:T(8,128)(2,1)}), bf16[32,32,576]{2,1,0:T(8,128)(2,1)S(1)}, u32[]{:S(2)}, u32[]{:S(2)}) async-start(bf16[32,32,576]{2,1,0:T(8,128)(2,1)} %broadcast_in_dim.13), calls=%async_computation | async-start | bytes 2621440 | tf_op jit(solution)/shard_map/all_to_all | solution.py:273
  13.1 6.4 %collective-permute-start.2 = (f32[2,128,16]{1,2,0:T(8,128)}, f32[2,128,16]{1,2,0:T(8,128)}, u32[]{:S(2)}, u32[]{:S(2)}) collective-permute-start(f32[2,128,16]{1,2,0:T(8,128)} %pad_maximum_fusion), channel_id=1, source_target_pairs={{0,16},{16,0},{1,17},{17,1},{2,18},{18,2},{3,19},{19,3},{4,20},{20... | collective-permute-start | bytes 49160 | tf_op jit(solution)/shard_map/ppermute | solution.py:56
  33.4 16.2 %copy-start = (f32[4,2,512]{2,1,0:T(2,128)S(1)}, f32[4,2,512]{2,1,0:T(2,128)}, u32[]{:S(2)}) copy-start(f32[4,2,512]{2,1,0:T(2,128)} %get-tuple-element.24.refs_7_.refs_4_) | copy-start | bytes 49156
  49.1 8.8 %collective-permute-start.3 = (f32[64,16,576]{2,1,0:T(8,128)}, f32[64,16,576]{2,1,0:T(8,128)S(1)}, u32[]{:S(2)}, u32[]{:S(2)}) collective-permute-start(f32[64,16,576]{2,1,0:T(8,128)} %bitcast.31), channel_id=1, source_target_pairs={{0,16},{16,0},{1,17},{17,1},{2,18},{18,2},{3,19},{19,3},{4,20},{20... | collective-permute-start | bytes 7077896 | tf_op jit(solution)/shard_map/ppermute | solution.py:56
  49.2 45.3 %collective-permute-start.4 = (f32[64,16,576]{2,1,0:T(8,128)}, f32[64,16,576]{2,1,0:T(8,128)}, u32[]{:S(2)}, u32[]{:S(2)}) collective-permute-start(f32[64,16,576]{2,1,0:T(8,128)} %bitcast.30), channel_id=1, source_target_pairs={{0,16},{16,0},{1,17},{17,1},{2,18},{18,2},{3,19},{19,3},{4,20},{20... | collective-permute-start | bytes 7077896 | tf_op jit(solution)/shard_map/ppermute | solution.py:56
  58.1 36.3 %collective-permute-start.5 = (bf16[64,16,576]{2,1,0:T(8,128)(2,1)S(1)}, bf16[64,16,576]{2,1,0:T(8,128)(2,1)}, u32[]{:S(2)}, u32[]{:S(2)}) collective-permute-start(bf16[64,16,576]{2,1,0:T(8,128)(2,1)S(1)} %core_sum.1.refs_7_), channel_id=1, source_target_pairs={{0,1},{1,0},{2,3},{3,2},{4,5},{5,4},{6,7},{7,6},{8,9},{9,8},{10,11... | collective-permute-start | bytes 3538952 | tf_op jit(solution)/shard_map/ppermute | solution.py:56
  70.6 23.6 %all-to-all-start.1 = ((bf16[16,288,128]{2,1,0:T(8,128)(2,1)}), bf16[16,288,128]{2,1,0:T(8,128)(2,1)S(1)}, u32[]{:S(2)}, u32[]{:S(2)}) async-start(bf16[16,288,128]{2,1,0:T(8,128)(2,1)} %bitcast.27), calls=%async_computation.1 | async-start | bytes 2359296 | tf_op jit(solution)/shard_map/all_to_all | solution.py:298
  94.4 5.1 %collective-permute-start.6 = (f32[32,576]{1,0:T(8,128)S(1)}, f32[32,576]{1,0:T(8,128)S(1)}, u32[]{:S(2)}, u32[]{:S(2)}) collective-permute-start(f32[32,576]{1,0:T(8,128)S(1)} %get-tuple-element.23), channel_id=1, source_target_pairs={{0,2},{2,0},{1,3},{3,1},{4,6},{6,4},{5,7},{7,5},{8,10},{10,8},{9,1... | collective-permute-start | bytes 221192 | tf_op jit(solution)/shard_map/ppermute | solution.py:56

commit v7 on v6

--- a/solution.py
+++ b/solution.py
@@ -56,6 +56,26 @@
     return lax.ppermute(array, axis, [(0, 1), (1, 0)])
 
 
+def pack_kernel(latent_ref, packed_ref):
+    shard, key_width = latent_ref.shape
+    blocks = key_width // LANES
+    for block in range(blocks):
+        packed_ref[block * shard : (block + 1) * shard, :] = latent_ref[:, block * LANES : (block + 1) * LANES]
+    rest = latent_ref[:, blocks * LANES :]
+    packed_ref[blocks * shard :, :] = jnp.concatenate([rest[: shard // 2], rest[shard // 2 :]], axis=-1)
+
+
+def pack(latent):
+    return pl.pallas_call(
+        pack_kernel,
+        in_specs=[VMEM],
+        out_specs=VMEM,
+        out_shape=jax.ShapeDtypeStruct((latent.size // LANES, LANES), latent.dtype),
+        compiler_params=pltpu.CompilerParams(vmem_limit_bytes=4 << 20),
+        name="pack",
+    )(latent)
+
+
 def grads_kernel(first, last, stays, do_stays, n_halves, n_before, *refs):
     refs = list(refs)
     take = lambda number: [refs.pop(0) for _ in range(number)]
@@ -64,12 +84,13 @@
     take(n_before)
     dq_refs = take(n_halves)
     dkv_ref = refs.pop(0) if last else None
+    keys_ref = refs.pop(0) if first else key_ref
     key_acc, value_acc, q_tiles, sems, *refs = refs
     dkv_tiles = refs.pop() if last else None
     dq_tiles = [] if stays else [refs.pop(0)]
     do_tiles = refs
     rows, width = value_acc.shape
-    key_width = key_ref.shape[-1]
+    key_width = keys_ref.shape[-1]
     count = dq_refs[0].shape[0]
     per_half = count // TILE
 
@@ -87,7 +108,17 @@
             copy.start()
         copies.append(pair)
 
-    keys = key_ref[...].reshape(rows, key_width)
+    if first:
+        blocks = width // LANES
+        shards = key_ref.shape[0]
+        shard = rows // shards
+        for block in range(blocks):
+            columns = key_ref[:, block * shard : (block + 1) * shard, :].reshape(rows, LANES)
+            keys_ref[:, block * LANES : (block + 1) * LANES] = columns
+        rest = key_ref[:, blocks * shard :, :]
+        rest = jnp.stack([rest[:, :, : LANES // 2], rest[:, :, LANES // 2 :]], axis=1)
+        keys_ref[:, width:] = rest.reshape(rows, key_width - width)
+    keys = keys_ref[...]
     keys_t = keys.T
     for tile, pair in enumerate(copies):
         for copy in pair:
@@ -141,14 +172,14 @@
         result.wait()
 
 
-def grads(keys, half, side, halves=1, sums=None, last=False, stays=False, do_stays=False, before=()):
-    shards, shard, key_width = keys.shape
-    rows = shards * shard
+def grads(keys, half, side, halves=1, sums=None, shards=0, stays=False, do_stays=False, before=()):
     queries, douts, stats = side
+    key_width = queries.shape[1]
+    rows = keys.size // key_width
     total, width = douts.shape
     count = total // 2
     tiles = halves * count // TILE
-    first = sums is None
+    first, last = sums is None, shards > 0
     operands = [half, in_vmem(keys), in_hbm(queries), (in_vmem if do_stays else in_hbm)(douts), in_vmem(stats)]
     in_specs = [VMEM, HBM, VMEM if do_stays else HBM, VMEM]
     sum_shapes = [(key_width, rows), (rows, width)]
@@ -169,12 +200,15 @@
         operands += [in_vmem(array) for array in sums]
         in_specs += [VMEM, VMEM]
     if last:
-        packed = (shards, shard * key_width // LANES, LANES)
+        packed = (shards, rows // shards * key_width // LANES, LANES)
         out_shape.append(pltpu.HBM(packed, keys.dtype))
         out_specs.append(HBM)
         scratch = [pltpu.VMEM(shape, jnp.float32) for shape in sum_shapes] + scratch
         scratch.append(pltpu.VMEM(packed, keys.dtype))
     else:
+        if first:
+            out_shape.append(pltpu.VMEM((rows, key_width), keys.dtype))
+            out_specs.append(VMEM)
         out_shape += [pltpu.VMEM(shape, jnp.float32) for shape in sum_shapes]
         out_specs += [VMEM, VMEM]
     place, spec = (in_hbm, HBM) if first else (in_vmem, VMEM)
@@ -266,11 +300,11 @@
 
 def on_device(queries, latent, out_grad, log_norms, row_dots):
     number, heads, key_width = queries.shape
-    shard = latent.shape[0]
     half = number // 2
 
-    spread = jnp.broadcast_to(latent[None], (lax.axis_size(CHIPS), shard, key_width))
-    keys = lax.all_to_all(spread, CHIPS, 0, 0, tiled=True)
+    chips = lax.axis_size(CHIPS)
+    packed = pack(latent)
+    keys = lax.all_to_all(jnp.broadcast_to(packed[None], (chips, *packed.shape)), CHIPS, 0, 0, tiled=True)
 
     def flat(queries, out_grad, stats):
         rows = number * heads
@@ -287,12 +321,12 @@
     kept = lax.axis_index("y_hi").astype(jnp.int32)[None]
     sent = 1 - kept
     whole = (half, heads, key_width)
-    dq_sent_theirs, dq_theirs, *sums = grads(keys, sent, theirs, halves=2, do_stays=True, before=mine)
+    dq_sent_theirs, dq_theirs, keys, *sums = grads(keys, sent, theirs, halves=2, do_stays=True, before=mine)
     returned = swap(dq_sent_theirs.reshape(whole), "core")
     dq_sent_mine, *sums = grads(keys, sent, mine, sums=sums, stays=True)
     over_cores = core_sum(dq_sent_mine.reshape(whole), returned)
     received = swap(over_cores, "y_hi")
-    dq_mine, dkv = grads(keys, kept, mine, sums=sums, last=True, before=[over_cores])
+    dq_mine, dkv = grads(keys, kept, mine, sums=sums, shards=chips, before=[over_cores])
     returned = swap(dq_theirs.reshape(whole), "core")
     query_grad = add([dq_mine.reshape(whole), returned, received], jnp.float32, softmax_scale, resident=[False, False, True])
     parts = lax.all_to_all(dkv.reshape(-1, 2 * dkv.shape[1], LANES), PLANE, 0, 0, tiled=True)

time: 101 us -> 99.8 us (0.988)
  local copies, waits for them, and re-layouts: 14.3 us -> 12.3 us
  waiting for transfers between devices: 26.6 us -> 28.3 us
  other arithmetic: 1.95 us -> 0.64 us
    all_to_all x1, waiting for transfers between devices: 6.69 us -> 8.4 us  [on_device(): lax.all_to_all(jnp.broadcast_to(packed[None], (chips, *packed.shape)), CH...]
    another operation x2, local copies, waits for them, and re-layouts: 1.37 us -> 0.18 us  [on_device(): mine = (queries, out_grad, jnp.stack([log_norms, row_dots]))]
    unnamed x9 -> x11, local copies, waits for them, and re-layouts: 5.06 us -> 5.9 us
  transfers between devices with their start and end apart: 9 -> 9, of which waited for: 2 -> 2; matrix products, arithmetic and copies ran while one was open for 16% -> 12% of each run, Pallas kernels for 23% -> 23%
where the time goes in v7:
time: 99.8 us; the launch traced here: 98.8 us
  Pallas kernels  39.2 us (39%)
  waiting for transfers between devices  28.3 us (28%)
  starting transfers between devices  17.5 us (18%)
  local copies, waits for them, and re-layouts  12.3 us (12%)
    pallas_call x3, Pallas kernels, grads(): pl.pallas_call(functools.partial(grads_kernel, first, last, stays, do_sta...  33.1 us
    all_to_all x1, waiting for transfers between devices, on_device(): lax.all_to_all(dkv.reshape(-1, 2 * dkv.shape[1], LANES), PLANE, 0, 0, til...  19.9 us
    all_to_all x1, starting transfers between devices, on_device(): lax.all_to_all(jnp.broadcast_to(packed[None], (chips, *packed.shape)), CH...  9.26 us
    all_to_all x1, waiting for transfers between devices, on_device(): lax.all_to_all(jnp.broadcast_to(packed[None], (chips, *packed.shape)), CH...  8.4 us
    unnamed x11, local copies, waits for them, and re-layouts  5.9 us
    pallas_call x1, Pallas kernels, add(): pl.pallas_call(functools.partial(add_kernel, out_scale), grid=(steps,), i...  4.99 us
    ppermute x2, local copies, waits for them, and re-layouts, swap(): return lax.ppermute(array, axis, [(0, 1), (1, 0)])  4.94 us
    ppermute x7, starting transfers between devices, swap(): return lax.ppermute(array, axis, [(0, 1), (1, 0)])  4.54 us
  transfers between devices with their start and end apart: 9, of which 2 were waited for; matrix products, arithmetic and copies ran while one was open for 12% of the time, Pallas kernels for 23%

profile of v7, /device:TPU:0, one launch (start us, length us, event | category | flops | bytes accessed | tf_op | source)
XLA Modules:
  0.0 98.8 jit_solution(1149443472757085247)
XLA Ops:
  0.6 0.1 collective-permute-start
  0.7 0.5 collective-permute-start.1
  1.2 0.0 copy-start.1
  1.2 0.8 copy-done.1
  2.0 0.0 copy-start.2
  2.0 0.0 copy-start.3
  2.0 0.1 pack.1
  2.1 1.2 %broadcast_in_dim.13 = bf16[32,144,128]{2,1,0:T(8,128)(2,1)} broadcast(bf16[144,128]{1,0:T(8,128)(2,1)S(1)} %pack.1), dimensions={1,2} | broadcast | bytes 1216512 | tf_op jit(solution)/shard_map/broadcast_in_dim | solution.py:307
  3.3 9.3 %all-to-all-start = ((bf16[32,144,128]{2,1,0:T(8,128)(2,1)}), bf16[32,144,128]{2,1,0:T(8,128)(2,1)S(1)}, u32[]{:S(2)}, u32[]{:S(2)}) async-start(bf16[32,144,128]{2,1,0:T(8,128)(2,1)} %broadcast_in_dim.13), calls=%async_computation | async-start | bytes 2359296 | tf_op jit(solution)/shard_map/all_to_all | solution.py:307
  12.5 0.0 copy-done.2
  12.5 0.0 copy-done.3
  12.6 0.1 collective-permute-start.2
  12.7 0.1 copy.17
  12.8 0.1 copy.18
  12.9 4.9 %copy.16 = bf16[128,16,576]{2,1,0:T(8,128)(2,1)} copy(bf16[128,16,576]{0,2,1:T(8,128)(2,1)} %param.5) | data formatting | bytes 4718592 | tf_op args[0]
  17.8 0.1 stack.21
  17.9 0.1 stack.22
  18.0 0.0 collective-permute-done.2
  18.0 0.1 copy.14
  18.1 0.1 reshape.42
  18.2 0.6 maximum_bitcast_fusion
  18.8 0.0 collective-permute-done
  18.8 4.8 %copy.13 = bf16[128,16,576]{2,1,0:T(8,128)(2,1)} copy(bf16[128,16,576]{0,2,1:T(8,128)(2,1)} %collective-permute-done) | data formatting | bytes 4718592 | tf_op jit(solution)/shard_map/ppermute | solution.py:56
  23.7 8.4 %all-to-all-done.refs_1_ = bf16[32,144,128]{2,1,0:T(8,128)(2,1)S(1)} async-done(((bf16[32,144,128]{2,1,0:T(8,128)(2,1)}), bf16[32,144,128]{2,1,0:T(8,128)(2,1)S(1)}, u32[]{:S(2)}, u32[]{:S(2)}) %all-to-all-start) | async-done | bytes 1179680 | tf_op jit(solution)/shard_map/all_to_all | solution.py:307
  32.1 0.0 collective-permute-done.1
  32.1 0.0 copy-start
  32.1 15.6 %grads.3 = (f32[1024,576]{1,0:T(8,128)}, f32[1024,576]{1,0:T(8,128)}, bf16[1024,576]{1,0:T(8,128)(2,1)S(1)}, f32[576,1024]{1,0:T(8,128)S(1)}, f32[1024,512]{1,0:T(8,128)S(1)}) custom-call(s32[1]{0:T(128)S(6)} %sub.3.refs_0_, bf16[32,144,128]{2,1,0:T(8,128)(2,1)S(1)} %all-to-all-done.refs_1_, bf16[2048,576]{1,0:T(8,128)(2,1)} %bitcast.25, ...), custom_call_target="tpu_custom_call" | custom-call | flops 1048576 | bytes 1179648 | tf_op jit(solution)/shard_map/grads/pallas_call | solution.py:217
  47.7 0.1 collective-permute-start.3
  47.8 0.5 collective-permute-start.4
  48.3 0.0 copy-done
  48.3 8.2 %grads.4 = (f32[1024,576]{1,0:T(8,128)S(1)}, f32[576,1024]{1,0:T(8,128)S(1)}, f32[1024,512]{1,0:T(8,128)S(1)}) custom-call(s32[1]{0:T(128)S(6)} %sub.3.refs_0_, bf16[1024,576]{1,0:T(8,128)(2,1)S(1)} %get-tuple-element.14.refs_1_, bf16[2048,576]{1,0:T(8,128)(2,1)} %bitcast.20, ...), custom_call_target="tpu_custom_call", output_to_operand_aliasing={{1}: (5, {}), {2}: (6, {})} | custom-call | flops 1048576 | bytes 1179648 | tf_op jit(solution)/shard_map/grads/pallas_call | solution.py:217
  56.5 0.0 collective-permute-done.3.theirs_ref
  56.6 0.2 core_sum.1.refs_7_
  56.8 3.2 %collective-permute-start.5 = (bf16[64,16,576]{2,1,0:T(8,128)(2,1)S(1)}, bf16[64,16,576]{2,1,0:T(8,128)(2,1)}, u32[]{:S(2)}, u32[]{:S(2)}) collective-permute-start(bf16[64,16,576]{2,1,0:T(8,128)(2,1)S(1)} %core_sum.1.refs_7_), channel_id=1, source_target_pairs={{0,1},{1,0},{2,3},{3,2},{4,5},{5,4},{6,7},{7,6},{8,9},{9,8},{10,11... | collective-permute-start | bytes 3538952 | tf_op jit(solution)/shard_map/ppermute | solution.py:56
  60.0 9.2 %grads.5 = (f32[1024,576]{1,0:T(8,128)}, bf16[32,144,128]{2,1,0:T(8,128)(2,1)}) custom-call(s32[1]{0:T(128)} %bitcast.refs_0_, bf16[1024,576]{1,0:T(8,128)(2,1)S(1)} %get-tuple-element.14.refs_1_, bf16[2048,576]{1,0:T(8,128)(2,1)} %bitcast.21, bf16[2048,512]{1,0:T(8,128)(2,1)} %bitcast.24, f32[4,2,512]{2,1,0:T(2,128)S(1)} %copy-done, ...), custom_call_target="tpu_custom_call" | custom-call | flops 1048576 | bytes 1179648 | tf_op jit(solution)/shard_map/grads/pallas_call | solution.py:217
  69.2 3.7 %all-to-all-start.1 = ((bf16[16,288,128]{2,1,0:T(8,128)(2,1)}), bf16[16,288,128]{2,1,0:T(8,128)(2,1)S(1)}, u32[]{:S(2)}, u32[]{:S(2)}) async-start(bf16[16,288,128]{2,1,0:T(8,128)(2,1)} %bitcast.27), calls=%async_computation.1 | async-start | bytes 2359296 | tf_op jit(solution)/shard_map/all_to_all | solution.py:332
  73.0 19.9 %all-to-all-done.1.parts_ref = bf16[16,288,128]{2,1,0:T(8,128)(2,1)S(1)} async-done(((bf16[16,288,128]{2,1,0:T(8,128)(2,1)}), bf16[16,288,128]{2,1,0:T(8,128)(2,1)S(1)}, u32[]{:S(2)}, u32[]{:S(2)}) %all-to-all-start.1) | async-done | bytes 1179680 | tf_op jit(solution)/shard_map/all_to_all | solution.py:332
  92.9 0.2 sum_parts.1
  93.0 0.1 collective-permute-start.6
  93.1 0.0 collective-permute-done.4.refs_1_
  93.2 0.0 collective-permute-done.5.refs_2_
  93.2 5.0 %add.1.after_ref = f32[64,16,576]{2,1,0:T(8,128)} custom-call(f32[64,16,576]{2,1,0:T(8,128)} %bitcast.26, f32[64,16,576]{2,1,0:T(8,128)} %collective-permute-done.4.refs_1_, bf16[64,16,576]{2,1,0:T(8,128)(2,1)} %collective-permute-done.5.refs_2_), custom_call_target="tpu_custom_call" | custom-call | flops 1179648 | bytes 2359296 | tf_op jit(solution)/shard_map/add/pallas_call | solution.py:246
  98.2 0.0 collective-permute-done.6.other_ref
  98.2 0.6 join.1
  (1 shorter events, 0.0 us)
Async XLA Ops:
  0.6 18.2 %collective-permute-start = (bf16[128,16,576]{0,2,1:T(8,128)(2,1)}, bf16[128,16,576]{0,2,1:T(8,128)(2,1)}, u32[]{:S(2)}, u32[]{:S(2)}) collective-permute-start(bf16[128,16,576]{0,2,1:T(8,128)(2,1)} %param.5), channel_id=1, source_target_pairs={{0,16},{16,0},{1,17},{17,1},{2,18},{18,2},{3,19},{19,3},{4,20},{20... | collective-permute-start | bytes 7077896 | tf_op jit(solution)/shard_map/ppermute | solution.py:56
  0.7 31.3 %collective-permute-start.1 = (bf16[128,16,512]{2,1,0:T(8,128)(2,1)}, bf16[128,16,512]{2,1,0:T(8,128)(2,1)S(1)}, u32[]{:S(2)}, u32[]{:S(2)}) collective-permute-start(bf16[128,16,512]{2,1,0:T(8,128)(2,1)} %param.7), channel_id=1, source_target_pairs={{0,16},{16,0},{1,17},{17,1},{2,18},{18,2},{3,19},{19,3},{4,20},{20... | collective-permute-start | bytes 6291464 | tf_op jit(solution)/shard_map/ppermute | solution.py:56
  1.2 0.8 copy-start.1
  2.0 10.5 %copy-start.2 = (f32[128,16]{0,1:T(8,128)S(1)}, f32[128,16]{0,1:T(8,128)}, u32[]{:S(2)}) copy-start(f32[128,16]{0,1:T(8,128)} %param.8) | copy-start | bytes 24580
  2.0 10.5 %copy-start.3 = (f32[128,16]{0,1:T(8,128)S(1)}, f32[128,16]{0,1:T(8,128)}, u32[]{:S(2)}) copy-start(f32[128,16]{0,1:T(8,128)} %param.9) | copy-start | bytes 24580
  3.3 28.8 %all-to-all-start = ((bf16[32,144,128]{2,1,0:T(8,128)(2,1)}), bf16[32,144,128]{2,1,0:T(8,128)(2,1)S(1)}, u32[]{:S(2)}, u32[]{:S(2)}) async-start(bf16[32,144,128]{2,1,0:T(8,128)(2,1)} %broadcast_in_dim.13), calls=%async_computation | async-start | bytes 2359296 | tf_op jit(solution)/shard_map/all_to_all | solution.py:307
  12.6 5.4 %collective-permute-start.2 = (f32[2,128,16]{1,2,0:T(8,128)S(1)}, f32[2,128,16]{1,2,0:T(8,128)S(1)}, u32[]{:S(2)}, u32[]{:S(2)}) collective-permute-start(f32[2,128,16]{1,2,0:T(8,128)S(1)} %pad_maximum_fusion), channel_id=1, source_target_pairs={{0,16},{16,0},{1,17},{17,1},{2,18},{18,2},{3,19},{19,3},{4,20},{20... | collective-permute-start | bytes 49160 | tf_op jit(solution)/shard_map/ppermute | solution.py:56
  32.1 16.2 %copy-start = (f32[4,2,512]{2,1,0:T(2,128)S(1)}, f32[4,2,512]{2,1,0:T(2,128)}, u32[]{:S(2)}) copy-start(f32[4,2,512]{2,1,0:T(2,128)} %get-tuple-element.26.refs_7_.refs_4_) | copy-start | bytes 49156
  47.7 8.8 %collective-permute-start.3 = (f32[64,16,576]{2,1,0:T(8,128)}, f32[64,16,576]{2,1,0:T(8,128)S(1)}, u32[]{:S(2)}, u32[]{:S(2)}) collective-permute-start(f32[64,16,576]{2,1,0:T(8,128)} %bitcast.31), channel_id=1, source_target_pairs={{0,16},{16,0},{1,17},{17,1},{2,18},{18,2},{3,19},{19,3},{4,20},{20... | collective-permute-start | bytes 7077896 | tf_op jit(solution)/shard_map/ppermute | solution.py:56
  47.8 45.3 %collective-permute-start.4 = (f32[64,16,576]{2,1,0:T(8,128)}, f32[64,16,576]{2,1,0:T(8,128)}, u32[]{:S(2)}, u32[]{:S(2)}) collective-permute-start(f32[64,16,576]{2,1,0:T(8,128)} %bitcast.30), channel_id=1, source_target_pairs={{0,16},{16,0},{1,17},{17,1},{2,18},{18,2},{3,19},{19,3},{4,20},{20... | collective-permute-start | bytes 7077896 | tf_op jit(solution)/shard_map/ppermute | solution.py:56
  56.8 36.4 %collective-permute-start.5 = (bf16[64,16,576]{2,1,0:T(8,128)(2,1)S(1)}, bf16[64,16,576]{2,1,0:T(8,128)(2,1)}, u32[]{:S(2)}, u32[]{:S(2)}) collective-permute-start(bf16[64,16,576]{2,1,0:T(8,128)(2,1)S(1)} %core_sum.1.refs_7_), channel_id=1, source_target_pairs={{0,1},{1,0},{2,3},{3,2},{4,5},{5,4},{6,7},{7,6},{8,9},{9,8},{10,11... | collective-permute-start | bytes 3538952 | tf_op jit(solution)/shard_map/ppermute | solution.py:56
  69.2 23.7 %all-to-all-start.1 = ((bf16[16,288,128]{2,1,0:T(8,128)(2,1)}), bf16[16,288,128]{2,1,0:T(8,128)(2,1)S(1)}, u32[]{:S(2)}, u32[]{:S(2)}) async-start(bf16[16,288,128]{2,1,0:T(8,128)(2,1)} %bitcast.27), calls=%async_computation.1 | async-start | bytes 2359296 | tf_op jit(solution)/shard_map/all_to_all | solution.py:332
  93.0 5.1 %collective-permute-start.6 = (f32[32,576]{1,0:T(8,128)S(1)}, f32[32,576]{1,0:T(8,128)S(1)}, u32[]{:S(2)}, u32[]{:S(2)}) collective-permute-start(f32[32,576]{1,0:T(8,128)S(1)} %get-tuple-element.25), channel_id=1, source_target_pairs={{0,2},{2,0},{1,3},{3,1},{4,6},{6,4},{5,7},{7,5},{8,10},{10,8},{9,1... | collective-permute-start | bytes 221192 | tf_op jit(solution)/shard_map/ppermute | solution.py:56

commit v8 on v7

--- a/solution.py
+++ b/solution.py
@@ -240,7 +240,7 @@
 
 def add(addends, dtype, out_scale=None, resident=None):
     rows, heads, key_width = addends[0].shape
-    steps = 4
+    steps = 2
     resident = resident or [True] * len(addends)
     block = pl.BlockSpec((rows // steps, heads, key_width), lambda i: (i, 0, 0))
     return pl.pallas_call(

time: 99.8 us -> 98.8 us (0.990)
  transfers between devices with their start and end apart: 9 -> 9, of which waited for: 2 -> 3; matrix products, arithmetic and copies ran while one was open for 12% -> 12% of each run, Pallas kernels for 23% -> 22%
where the time goes in v8:
time: 98.8 us; the launch traced here: 98.2 us
  Pallas kernels  38.3 us (39%)
  waiting for transfers between devices  28.6 us (29%)
  starting transfers between devices  17.5 us (18%)
  local copies, waits for them, and re-layouts  12.3 us (12%)
    pallas_call x3, Pallas kernels, grads(): pl.pallas_call(functools.partial(grads_kernel, first, last, stays, do_sta...  33.1 us
    all_to_all x1, waiting for transfers between devices, on_device(): lax.all_to_all(dkv.reshape(-1, 2 * dkv.shape[1], LANES), PLANE, 0, 0, til...  19.9 us
    all_to_all x1, starting transfers between devices, on_device(): lax.all_to_all(jnp.broadcast_to(packed[None], (chips, *packed.shape)), CH...  9.26 us
    all_to_all x1, waiting for transfers between devices, on_device(): lax.all_to_all(jnp.broadcast_to(packed[None], (chips, *packed.shape)), CH...  8.4 us
    unnamed x11, local copies, waits for them, and re-layouts  5.9 us
    ppermute x2, local copies, waits for them, and re-layouts, swap(): return lax.ppermute(array, axis, [(0, 1), (1, 0)])  4.94 us
    ppermute x7, starting transfers between devices, swap(): return lax.ppermute(array, axis, [(0, 1), (1, 0)])  4.54 us
    pallas_call x1, Pallas kernels, add(): pl.pallas_call(functools.partial(add_kernel, out_scale), grid=(steps,), i...  4.14 us
  transfers between devices with their start and end apart: 9, of which 3 were waited for; matrix products, arithmetic and copies ran while one was open for 12% of the time, Pallas kernels for 22%

profile of v8, /device:TPU:0, one launch (start us, length us, event | category | flops | bytes accessed | tf_op | source)
XLA Modules:
  0.0 98.2 jit_solution(18086786119701558397)
XLA Ops:
  0.6 0.1 collective-permute-start
  0.7 0.5 collective-permute-start.1
  1.2 0.0 copy-start.1
  1.2 0.8 copy-done.1
  2.0 0.0 copy-start.2
  2.0 0.0 copy-start.3
  2.0 0.1 pack.1
  2.1 1.2 %broadcast_in_dim.13 = bf16[32,144,128]{2,1,0:T(8,128)(2,1)} broadcast(bf16[144,128]{1,0:T(8,128)(2,1)S(1)} %pack.1), dimensions={1,2} | broadcast | bytes 1216512 | tf_op jit(solution)/shard_map/broadcast_in_dim | solution.py:307
  3.3 9.3 %all-to-all-start = ((bf16[32,144,128]{2,1,0:T(8,128)(2,1)}), bf16[32,144,128]{2,1,0:T(8,128)(2,1)S(1)}, u32[]{:S(2)}, u32[]{:S(2)}) async-start(bf16[32,144,128]{2,1,0:T(8,128)(2,1)} %broadcast_in_dim.13), calls=%async_computation | async-start | bytes 2359296 | tf_op jit(solution)/shard_map/all_to_all | solution.py:307
  12.5 0.0 copy-done.2
  12.5 0.0 copy-done.3
  12.6 0.1 collective-permute-start.2
  12.7 0.1 copy.17
  12.8 0.1 copy.18
  12.9 4.9 %copy.16 = bf16[128,16,576]{2,1,0:T(8,128)(2,1)} copy(bf16[128,16,576]{0,2,1:T(8,128)(2,1)} %param.5) | data formatting | bytes 4718592 | tf_op args[0]
  17.8 0.1 stack.21
  17.9 0.1 stack.22
  18.0 0.0 collective-permute-done.2
  18.0 0.1 copy.14
  18.1 0.1 reshape.42
  18.2 0.6 maximum_bitcast_fusion
  18.8 0.0 collective-permute-done
  18.8 4.8 %copy.13 = bf16[128,16,576]{2,1,0:T(8,128)(2,1)} copy(bf16[128,16,576]{0,2,1:T(8,128)(2,1)} %collective-permute-done) | data formatting | bytes 4718592 | tf_op jit(solution)/shard_map/ppermute | solution.py:56
  23.7 8.4 %all-to-all-done.refs_1_ = bf16[32,144,128]{2,1,0:T(8,128)(2,1)S(1)} async-done(((bf16[32,144,128]{2,1,0:T(8,128)(2,1)}), bf16[32,144,128]{2,1,0:T(8,128)(2,1)S(1)}, u32[]{:S(2)}, u32[]{:S(2)}) %all-to-all-start) | async-done | bytes 1179680 | tf_op jit(solution)/shard_map/all_to_all | solution.py:307
  32.1 0.0 collective-permute-done.1
  32.1 0.0 copy-start
  32.1 15.6 %grads.3 = (f32[1024,576]{1,0:T(8,128)}, f32[1024,576]{1,0:T(8,128)}, bf16[1024,576]{1,0:T(8,128)(2,1)S(1)}, f32[576,1024]{1,0:T(8,128)S(1)}, f32[1024,512]{1,0:T(8,128)S(1)}) custom-call(s32[1]{0:T(128)S(6)} %sub.3.refs_0_, bf16[32,144,128]{2,1,0:T(8,128)(2,1)S(1)} %all-to-all-done.refs_1_, bf16[2048,576]{1,0:T(8,128)(2,1)} %bitcast.25, ...), custom_call_target="tpu_custom_call" | custom-call | flops 1048576 | bytes 1179648 | tf_op jit(solution)/shard_map/grads/pallas_call | solution.py:217
  47.7 0.1 collective-permute-start.3
  47.8 0.5 collective-permute-start.4
  48.3 0.0 copy-done
  48.3 8.2 %grads.4 = (f32[1024,576]{1,0:T(8,128)S(1)}, f32[576,1024]{1,0:T(8,128)S(1)}, f32[1024,512]{1,0:T(8,128)S(1)}) custom-call(s32[1]{0:T(128)S(6)} %sub.3.refs_0_, bf16[1024,576]{1,0:T(8,128)(2,1)S(1)} %get-tuple-element.14.refs_1_, bf16[2048,576]{1,0:T(8,128)(2,1)} %bitcast.20, ...), custom_call_target="tpu_custom_call", output_to_operand_aliasing={{1}: (5, {}), {2}: (6, {})} | custom-call | flops 1048576 | bytes 1179648 | tf_op jit(solution)/shard_map/grads/pallas_call | solution.py:217
  56.5 0.0 collective-permute-done.3.theirs_ref
  56.6 0.2 core_sum.1.refs_7_
  56.8 3.2 %collective-permute-start.5 = (bf16[64,16,576]{2,1,0:T(8,128)(2,1)S(1)}, bf16[64,16,576]{2,1,0:T(8,128)(2,1)}, u32[]{:S(2)}, u32[]{:S(2)}) collective-permute-start(bf16[64,16,576]{2,1,0:T(8,128)(2,1)S(1)} %core_sum.1.refs_7_), channel_id=1, source_target_pairs={{0,1},{1,0},{2,3},{3,2},{4,5},{5,4},{6,7},{7,6},{8,9},{9,8},{10,11... | collective-permute-start | bytes 3538952 | tf_op jit(solution)/shard_map/ppermute | solution.py:56
  60.0 9.2 %grads.5 = (f32[1024,576]{1,0:T(8,128)}, bf16[32,144,128]{2,1,0:T(8,128)(2,1)}) custom-call(s32[1]{0:T(128)} %bitcast.refs_0_, bf16[1024,576]{1,0:T(8,128)(2,1)S(1)} %get-tuple-element.14.refs_1_, bf16[2048,576]{1,0:T(8,128)(2,1)} %bitcast.21, bf16[2048,512]{1,0:T(8,128)(2,1)} %bitcast.24, f32[4,2,512]{2,1,0:T(2,128)S(1)} %copy-done, ...), custom_call_target="tpu_custom_call" | custom-call | flops 1048576 | bytes 1179648 | tf_op jit(solution)/shard_map/grads/pallas_call | solution.py:217
  69.2 3.7 %all-to-all-start.1 = ((bf16[16,288,128]{2,1,0:T(8,128)(2,1)}), bf16[16,288,128]{2,1,0:T(8,128)(2,1)S(1)}, u32[]{:S(2)}, u32[]{:S(2)}) async-start(bf16[16,288,128]{2,1,0:T(8,128)(2,1)} %bitcast.27), calls=%async_computation.1 | async-start | bytes 2359296 | tf_op jit(solution)/shard_map/all_to_all | solution.py:332
  73.0 19.9 %all-to-all-done.1.parts_ref = bf16[16,288,128]{2,1,0:T(8,128)(2,1)S(1)} async-done(((bf16[16,288,128]{2,1,0:T(8,128)(2,1)}), bf16[16,288,128]{2,1,0:T(8,128)(2,1)S(1)}, u32[]{:S(2)}, u32[]{:S(2)}) %all-to-all-start.1) | async-done | bytes 1179680 | tf_op jit(solution)/shard_map/all_to_all | solution.py:332
  92.9 0.2 sum_parts.1
  93.0 0.1 collective-permute-start.6
  93.1 0.0 collective-permute-done.4.refs_1_
  93.2 0.0 collective-permute-done.5.refs_2_
  93.2 4.1 %add.1.after_ref = f32[64,16,576]{2,1,0:T(8,128)} custom-call(f32[64,16,576]{2,1,0:T(8,128)} %bitcast.26, f32[64,16,576]{2,1,0:T(8,128)} %collective-permute-done.4.refs_1_, bf16[64,16,576]{2,1,0:T(8,128)(2,1)} %collective-permute-done.5.refs_2_), custom_call_target="tpu_custom_call" | custom-call | flops 1179648 | bytes 2359296 | tf_op jit(solution)/shard_map/add/pallas_call | solution.py:246
  97.3 0.3 collective-permute-done.6.other_ref
  97.6 0.6 join.1
  (1 shorter events, 0.0 us)
Async XLA Ops:
  0.6 18.2 %collective-permute-start = (bf16[128,16,576]{0,2,1:T(8,128)(2,1)}, bf16[128,16,576]{0,2,1:T(8,128)(2,1)}, u32[]{:S(2)}, u32[]{:S(2)}) collective-permute-start(bf16[128,16,576]{0,2,1:T(8,128)(2,1)} %param.5), channel_id=1, source_target_pairs={{0,16},{16,0},{1,17},{17,1},{2,18},{18,2},{3,19},{19,3},{4,20},{20... | collective-permute-start | bytes 7077896 | tf_op jit(solution)/shard_map/ppermute | solution.py:56
  0.7 31.3 %collective-permute-start.1 = (bf16[128,16,512]{2,1,0:T(8,128)(2,1)}, bf16[128,16,512]{2,1,0:T(8,128)(2,1)S(1)}, u32[]{:S(2)}, u32[]{:S(2)}) collective-permute-start(bf16[128,16,512]{2,1,0:T(8,128)(2,1)} %param.7), channel_id=1, source_target_pairs={{0,16},{16,0},{1,17},{17,1},{2,18},{18,2},{3,19},{19,3},{4,20},{20... | collective-permute-start | bytes 6291464 | tf_op jit(solution)/shard_map/ppermute | solution.py:56
  1.2 0.8 copy-start.1
  2.0 10.5 %copy-start.2 = (f32[128,16]{0,1:T(8,128)S(1)}, f32[128,16]{0,1:T(8,128)}, u32[]{:S(2)}) copy-start(f32[128,16]{0,1:T(8,128)} %param.8) | copy-start | bytes 24580
  2.0 10.5 %copy-start.3 = (f32[128,16]{0,1:T(8,128)S(1)}, f32[128,16]{0,1:T(8,128)}, u32[]{:S(2)}) copy-start(f32[128,16]{0,1:T(8,128)} %param.9) | copy-start | bytes 24580
  3.3 28.8 %all-to-all-start = ((bf16[32,144,128]{2,1,0:T(8,128)(2,1)}), bf16[32,144,128]{2,1,0:T(8,128)(2,1)S(1)}, u32[]{:S(2)}, u32[]{:S(2)}) async-start(bf16[32,144,128]{2,1,0:T(8,128)(2,1)} %broadcast_in_dim.13), calls=%async_computation | async-start | bytes 2359296 | tf_op jit(solution)/shard_map/all_to_all | solution.py:307
  12.6 5.4 %collective-permute-start.2 = (f32[2,128,16]{1,2,0:T(8,128)S(1)}, f32[2,128,16]{1,2,0:T(8,128)S(1)}, u32[]{:S(2)}, u32[]{:S(2)}) collective-permute-start(f32[2,128,16]{1,2,0:T(8,128)S(1)} %pad_maximum_fusion), channel_id=1, source_target_pairs={{0,16},{16,0},{1,17},{17,1},{2,18},{18,2},{3,19},{19,3},{4,20},{20... | collective-permute-start | bytes 49160 | tf_op jit(solution)/shard_map/ppermute | solution.py:56
  32.1 16.2 %copy-start = (f32[4,2,512]{2,1,0:T(2,128)S(1)}, f32[4,2,512]{2,1,0:T(2,128)}, u32[]{:S(2)}) copy-start(f32[4,2,512]{2,1,0:T(2,128)} %get-tuple-element.26.refs_7_.refs_4_) | copy-start | bytes 49156
  47.7 8.8 %collective-permute-start.3 = (f32[64,16,576]{2,1,0:T(8,128)}, f32[64,16,576]{2,1,0:T(8,128)S(1)}, u32[]{:S(2)}, u32[]{:S(2)}) collective-permute-start(f32[64,16,576]{2,1,0:T(8,128)} %bitcast.31), channel_id=1, source_target_pairs={{0,16},{16,0},{1,17},{17,1},{2,18},{18,2},{3,19},{19,3},{4,20},{20... | collective-permute-start | bytes 7077896 | tf_op jit(solution)/shard_map/ppermute | solution.py:56
  47.8 45.3 %collective-permute-start.4 = (f32[64,16,576]{2,1,0:T(8,128)}, f32[64,16,576]{2,1,0:T(8,128)}, u32[]{:S(2)}, u32[]{:S(2)}) collective-permute-start(f32[64,16,576]{2,1,0:T(8,128)} %bitcast.30), channel_id=1, source_target_pairs={{0,16},{16,0},{1,17},{17,1},{2,18},{18,2},{3,19},{19,3},{4,20},{20... | collective-permute-start | bytes 7077896 | tf_op jit(solution)/shard_map/ppermute | solution.py:56
  56.8 36.4 %collective-permute-start.5 = (bf16[64,16,576]{2,1,0:T(8,128)(2,1)S(1)}, bf16[64,16,576]{2,1,0:T(8,128)(2,1)}, u32[]{:S(2)}, u32[]{:S(2)}) collective-permute-start(bf16[64,16,576]{2,1,0:T(8,128)(2,1)S(1)} %core_sum.1.refs_7_), channel_id=1, source_target_pairs={{0,1},{1,0},{2,3},{3,2},{4,5},{5,4},{6,7},{7,6},{8,9},{9,8},{10,11... | collective-permute-start | bytes 3538952 | tf_op jit(solution)/shard_map/ppermute | solution.py:56
  69.2 23.7 %all-to-all-start.1 = ((bf16[16,288,128]{2,1,0:T(8,128)(2,1)}), bf16[16,288,128]{2,1,0:T(8,128)(2,1)S(1)}, u32[]{:S(2)}, u32[]{:S(2)}) async-start(bf16[16,288,128]{2,1,0:T(8,128)(2,1)} %bitcast.27), calls=%async_computation.1 | async-start | bytes 2359296 | tf_op jit(solution)/shard_map/all_to_all | solution.py:332
  93.0 4.5 %collective-permute-start.6 = (f32[32,576]{1,0:T(8,128)S(1)}, f32[32,576]{1,0:T(8,128)S(1)}, u32[]{:S(2)}, u32[]{:S(2)}) collective-permute-start(f32[32,576]{1,0:T(8,128)S(1)} %get-tuple-element.25), channel_id=1, source_target_pairs={{0,2},{2,0},{1,3},{3,1},{4,6},{6,4},{5,7},{7,5},{8,10},{10,8},{9,1... | collective-permute-start | bytes 221192 | tf_op jit(solution)/shard_map/ppermute | solution.py:56

commit v9 on v8

--- a/solution.py
+++ b/solution.py
@@ -68,12 +68,13 @@
 def pack(latent):
     return pl.pallas_call(
         pack_kernel,
-        in_specs=[VMEM],
+        grid=(1,),
+        in_specs=[pl.BlockSpec(latent.shape, lambda i: (0, 0))],
         out_specs=VMEM,
         out_shape=jax.ShapeDtypeStruct((latent.size // LANES, LANES), latent.dtype),
         compiler_params=pltpu.CompilerParams(vmem_limit_bytes=4 << 20),
         name="pack",
-    )(latent)
+    )(in_hbm(latent))
 
 
 def grads_kernel(first, last, stays, do_stays, n_halves, n_before, *refs):

time: 98.8 us -> 98.9 us (level)
    unnamed x11 -> x9, local copies, waits for them, and re-layouts: 5.9 us -> 5.1 us
  transfers between devices with their start and end apart: 9 -> 9, of which waited for: 3 -> 3; matrix products, arithmetic and copies ran while one was open for 12% -> 12% of each run, Pallas kernels for 22% -> 23%
where the time goes in v9:
time: 98.9 us; the launch traced here: 98.3 us
  Pallas kernels  39.1 us (40%)
  waiting for transfers between devices  28.6 us (29%)
  starting transfers between devices  17.5 us (18%)
  local copies, waits for them, and re-layouts  11.5 us (12%)
    pallas_call x3, Pallas kernels, grads(): pl.pallas_call(functools.partial(grads_kernel, first, last, stays, do_sta...  33.1 us
    all_to_all x1, waiting for transfers between devices, on_device(): lax.all_to_all(dkv.reshape(-1, 2 * dkv.shape[1], LANES), PLANE, 0, 0, til...  19.9 us
    all_to_all x1, starting transfers between devices, on_device(): lax.all_to_all(jnp.broadcast_to(packed[None], (chips, *packed.shape)), CH...  9.26 us
    all_to_all x1, waiting for transfers between devices, on_device(): lax.all_to_all(jnp.broadcast_to(packed[None], (chips, *packed.shape)), CH...  8.42 us
    unnamed x9, local copies, waits for them, and re-layouts  5.1 us
    ppermute x2, local copies, waits for them, and re-layouts, swap(): return lax.ppermute(array, axis, [(0, 1), (1, 0)])  4.94 us
    ppermute x7, starting transfers between devices, swap(): return lax.ppermute(array, axis, [(0, 1), (1, 0)])  4.53 us
    pallas_call x1, Pallas kernels, add(): pl.pallas_call(functools.partial(add_kernel, out_scale), grid=(steps,), i...  4.14 us
  transfers between devices with their start and end apart: 9, of which 3 were waited for; matrix products, arithmetic and copies ran while one was open for 12% of the time, Pallas kernels for 23%

profile of v9, /device:TPU:0, one launch (start us, length us, event | category | flops | bytes accessed | tf_op | source)
XLA Modules:
  0.0 98.3 jit_solution(8485181204041167806)
XLA Ops:
  0.6 0.0 copy-start.1
  0.6 0.0 copy-start.2
  0.7 0.1 collective-permute-start
  0.7 0.5 collective-permute-start.1
  1.2 0.9 pack.1
  2.1 1.2 %broadcast_in_dim.13 = bf16[32,144,128]{2,1,0:T(8,128)(2,1)} broadcast(bf16[144,128]{1,0:T(8,128)(2,1)S(1)} %pack.1), dimensions={1,2} | broadcast | bytes 1216512 | tf_op jit(solution)/shard_map/broadcast_in_dim | solution.py:308
  3.3 9.3 %all-to-all-start = ((bf16[32,144,128]{2,1,0:T(8,128)(2,1)}), bf16[32,144,128]{2,1,0:T(8,128)(2,1)S(1)}, u32[]{:S(2)}, u32[]{:S(2)}) async-start(bf16[32,144,128]{2,1,0:T(8,128)(2,1)} %broadcast_in_dim.13), calls=%async_computation | async-start | bytes 2359296 | tf_op jit(solution)/shard_map/all_to_all | solution.py:308
  12.6 0.0 copy-done.1
  12.6 0.0 copy-done.2
  12.6 0.1 collective-permute-start.2
  12.7 0.1 copy.17
  12.8 0.1 copy.18
  12.9 4.9 %copy.16 = bf16[128,16,576]{2,1,0:T(8,128)(2,1)} copy(bf16[128,16,576]{0,2,1:T(8,128)(2,1)} %param.5) | data formatting | bytes 4718592 | tf_op args[0]
  17.8 0.1 stack.21
  17.9 0.1 stack.22
  18.0 0.0 collective-permute-done.2
  18.0 0.1 copy.14
  18.1 0.1 reshape.42
  18.2 0.6 maximum_bitcast_fusion
  18.8 0.0 collective-permute-done
  18.8 4.8 %copy.13 = bf16[128,16,576]{2,1,0:T(8,128)(2,1)} copy(bf16[128,16,576]{0,2,1:T(8,128)(2,1)} %collective-permute-done) | data formatting | bytes 4718592 | tf_op jit(solution)/shard_map/ppermute | solution.py:56
  23.7 8.4 %all-to-all-done.refs_1_ = bf16[32,144,128]{2,1,0:T(8,128)(2,1)S(1)} async-done(((bf16[32,144,128]{2,1,0:T(8,128)(2,1)}), bf16[32,144,128]{2,1,0:T(8,128)(2,1)S(1)}, u32[]{:S(2)}, u32[]{:S(2)}) %all-to-all-start) | async-done | bytes 1179680 | tf_op jit(solution)/shard_map/all_to_all | solution.py:308
  32.1 0.0 collective-permute-done.1
  32.1 0.0 copy-start
  32.1 15.6 %grads.3 = (f32[1024,576]{1,0:T(8,128)}, f32[1024,576]{1,0:T(8,128)}, bf16[1024,576]{1,0:T(8,128)(2,1)S(1)}, f32[576,1024]{1,0:T(8,128)S(1)}, f32[1024,512]{1,0:T(8,128)S(1)}) custom-call(s32[1]{0:T(128)S(6)} %sub.3.refs_0_, bf16[32,144,128]{2,1,0:T(8,128)(2,1)S(1)} %all-to-all-done.refs_1_, bf16[2048,576]{1,0:T(8,128)(2,1)} %bitcast.25, ...), custom_call_target="tpu_custom_call" | custom-call | flops 1048576 | bytes 1179648 | tf_op jit(solution)/shard_map/grads/pallas_call | solution.py:218
  47.8 0.1 collective-permute-start.3
  47.8 0.5 collective-permute-start.4
  48.3 0.0 copy-done
  48.3 8.2 %grads.4 = (f32[1024,576]{1,0:T(8,128)S(1)}, f32[576,1024]{1,0:T(8,128)S(1)}, f32[1024,512]{1,0:T(8,128)S(1)}) custom-call(s32[1]{0:T(128)S(6)} %sub.3.refs_0_, bf16[1024,576]{1,0:T(8,128)(2,1)S(1)} %get-tuple-element.14.refs_1_, bf16[2048,576]{1,0:T(8,128)(2,1)} %bitcast.20, ...), custom_call_target="tpu_custom_call", output_to_operand_aliasing={{1}: (5, {}), {2}: (6, {})} | custom-call | flops 1048576 | bytes 1179648 | tf_op jit(solution)/shard_map/grads/pallas_call | solution.py:218
  56.6 0.0 collective-permute-done.3.theirs_ref
  56.6 0.2 core_sum.1.refs_7_
  56.8 3.2 %collective-permute-start.5 = (bf16[64,16,576]{2,1,0:T(8,128)(2,1)S(1)}, bf16[64,16,576]{2,1,0:T(8,128)(2,1)}, u32[]{:S(2)}, u32[]{:S(2)}) collective-permute-start(bf16[64,16,576]{2,1,0:T(8,128)(2,1)S(1)} %core_sum.1.refs_7_), channel_id=1, source_target_pairs={{0,1},{1,0},{2,3},{3,2},{4,5},{5,4},{6,7},{7,6},{8,9},{9,8},{10,11... | collective-permute-start | bytes 3538952 | tf_op jit(solution)/shard_map/ppermute | solution.py:56
  60.0 9.2 %grads.5 = (f32[1024,576]{1,0:T(8,128)}, bf16[32,144,128]{2,1,0:T(8,128)(2,1)}) custom-call(s32[1]{0:T(128)} %bitcast.refs_0_, bf16[1024,576]{1,0:T(8,128)(2,1)S(1)} %get-tuple-element.14.refs_1_, bf16[2048,576]{1,0:T(8,128)(2,1)} %bitcast.21, bf16[2048,512]{1,0:T(8,128)(2,1)} %bitcast.24, f32[4,2,512]{2,1,0:T(2,128)S(1)} %copy-done, ...), custom_call_target="tpu_custom_call" | custom-call | flops 1048576 | bytes 1179648 | tf_op jit(solution)/shard_map/grads/pallas_call | solution.py:218
  69.3 3.7 %all-to-all-start.1 = ((bf16[16,288,128]{2,1,0:T(8,128)(2,1)}), bf16[16,288,128]{2,1,0:T(8,128)(2,1)S(1)}, u32[]{:S(2)}, u32[]{:S(2)}) async-start(bf16[16,288,128]{2,1,0:T(8,128)(2,1)} %bitcast.27), calls=%async_computation.1 | async-start | bytes 2359296 | tf_op jit(solution)/shard_map/all_to_all | solution.py:333
  73.0 19.9 %all-to-all-done.1.parts_ref = bf16[16,288,128]{2,1,0:T(8,128)(2,1)S(1)} async-done(((bf16[16,288,128]{2,1,0:T(8,128)(2,1)}), bf16[16,288,128]{2,1,0:T(8,128)(2,1)S(1)}, u32[]{:S(2)}, u32[]{:S(2)}) %all-to-all-start.1) | async-done | bytes 1179680 | tf_op jit(solution)/shard_map/all_to_all | solution.py:333
  92.9 0.2 sum_parts.1
  93.1 0.1 collective-permute-start.6
  93.2 0.0 collective-permute-done.4.refs_1_
  93.2 0.0 collective-permute-done.5.refs_2_
  93.2 4.1 %add.1.after_ref = f32[64,16,576]{2,1,0:T(8,128)} custom-call(f32[64,16,576]{2,1,0:T(8,128)} %bitcast.26, f32[64,16,576]{2,1,0:T(8,128)} %collective-permute-done.4.refs_1_, bf16[64,16,576]{2,1,0:T(8,128)(2,1)} %collective-permute-done.5.refs_2_), custom_call_target="tpu_custom_call" | custom-call | flops 1179648 | bytes 2359296 | tf_op jit(solution)/shard_map/add/pallas_call | solution.py:247
  97.4 0.3 collective-permute-done.6.other_ref
  97.6 0.6 join.1
  (1 shorter events, 0.0 us)
Async XLA Ops:
  0.6 11.9 %copy-start.1 = (f32[128,16]{0,1:T(8,128)S(1)}, f32[128,16]{0,1:T(8,128)}, u32[]{:S(2)}) copy-start(f32[128,16]{0,1:T(8,128)} %param.8) | copy-start | bytes 24580
  0.6 11.9 %copy-start.2 = (f32[128,16]{0,1:T(8,128)S(1)}, f32[128,16]{0,1:T(8,128)}, u32[]{:S(2)}) copy-start(f32[128,16]{0,1:T(8,128)} %param.9) | copy-start | bytes 24580
  0.7 18.2 %collective-permute-start = (bf16[128,16,576]{0,2,1:T(8,128)(2,1)}, bf16[128,16,576]{0,2,1:T(8,128)(2,1)}, u32[]{:S(2)}, u32[]{:S(2)}) collective-permute-start(bf16[128,16,576]{0,2,1:T(8,128)(2,1)} %param.5), channel_id=1, source_target_pairs={{0,16},{16,0},{1,17},{17,1},{2,18},{18,2},{3,19},{19,3},{4,20},{20... | collective-permute-start | bytes 7077896 | tf_op jit(solution)/shard_map/ppermute | solution.py:56
  0.7 31.4 %collective-permute-start.1 = (bf16[128,16,512]{2,1,0:T(8,128)(2,1)}, bf16[128,16,512]{2,1,0:T(8,128)(2,1)S(1)}, u32[]{:S(2)}, u32[]{:S(2)}) collective-permute-start(bf16[128,16,512]{2,1,0:T(8,128)(2,1)} %param.7), channel_id=1, source_target_pairs={{0,16},{16,0},{1,17},{17,1},{2,18},{18,2},{3,19},{19,3},{4,20},{20... | collective-permute-start | bytes 6291464 | tf_op jit(solution)/shard_map/ppermute | solution.py:56
  3.3 28.8 %all-to-all-start = ((bf16[32,144,128]{2,1,0:T(8,128)(2,1)}), bf16[32,144,128]{2,1,0:T(8,128)(2,1)S(1)}, u32[]{:S(2)}, u32[]{:S(2)}) async-start(bf16[32,144,128]{2,1,0:T(8,128)(2,1)} %broadcast_in_dim.13), calls=%async_computation | async-start | bytes 2359296 | tf_op jit(solution)/shard_map/all_to_all | solution.py:308
  12.6 5.4 %collective-permute-start.2 = (f32[2,128,16]{1,2,0:T(8,128)S(1)}, f32[2,128,16]{1,2,0:T(8,128)S(1)}, u32[]{:S(2)}, u32[]{:S(2)}) collective-permute-start(f32[2,128,16]{1,2,0:T(8,128)S(1)} %pad_maximum_fusion), channel_id=1, source_target_pairs={{0,16},{16,0},{1,17},{17,1},{2,18},{18,2},{3,19},{19,3},{4,20},{20... | collective-permute-start | bytes 49160 | tf_op jit(solution)/shard_map/ppermute | solution.py:56
  32.1 16.2 %copy-start = (f32[4,2,512]{2,1,0:T(2,128)S(1)}, f32[4,2,512]{2,1,0:T(2,128)}, u32[]{:S(2)}) copy-start(f32[4,2,512]{2,1,0:T(2,128)} %get-tuple-element.26.refs_7_.refs_4_) | copy-start | bytes 49156
  47.8 8.8 %collective-permute-start.3 = (f32[64,16,576]{2,1,0:T(8,128)}, f32[64,16,576]{2,1,0:T(8,128)S(1)}, u32[]{:S(2)}, u32[]{:S(2)}) collective-permute-start(f32[64,16,576]{2,1,0:T(8,128)} %bitcast.31), channel_id=1, source_target_pairs={{0,16},{16,0},{1,17},{17,1},{2,18},{18,2},{3,19},{19,3},{4,20},{20... | collective-permute-start | bytes 7077896 | tf_op jit(solution)/shard_map/ppermute | solution.py:56
  47.8 45.3 %collective-permute-start.4 = (f32[64,16,576]{2,1,0:T(8,128)}, f32[64,16,576]{2,1,0:T(8,128)}, u32[]{:S(2)}, u32[]{:S(2)}) collective-permute-start(f32[64,16,576]{2,1,0:T(8,128)} %bitcast.30), channel_id=1, source_target_pairs={{0,16},{16,0},{1,17},{17,1},{2,18},{18,2},{3,19},{19,3},{4,20},{20... | collective-permute-start | bytes 7077896 | tf_op jit(solution)/shard_map/ppermute | solution.py:56
  56.8 36.4 %collective-permute-start.5 = (bf16[64,16,576]{2,1,0:T(8,128)(2,1)S(1)}, bf16[64,16,576]{2,1,0:T(8,128)(2,1)}, u32[]{:S(2)}, u32[]{:S(2)}) collective-permute-start(bf16[64,16,576]{2,1,0:T(8,128)(2,1)S(1)} %core_sum.1.refs_7_), channel_id=1, source_target_pairs={{0,1},{1,0},{2,3},{3,2},{4,5},{5,4},{6,7},{7,6},{8,9},{9,8},{10,11... | collective-permute-start | bytes 3538952 | tf_op jit(solution)/shard_map/ppermute | solution.py:56
  69.3 23.7 %all-to-all-start.1 = ((bf16[16,288,128]{2,1,0:T(8,128)(2,1)}), bf16[16,288,128]{2,1,0:T(8,128)(2,1)S(1)}, u32[]{:S(2)}, u32[]{:S(2)}) async-start(bf16[16,288,128]{2,1,0:T(8,128)(2,1)} %bitcast.27), calls=%async_computation.1 | async-start | bytes 2359296 | tf_op jit(solution)/shard_map/all_to_all | solution.py:333
  93.1 4.5 %collective-permute-start.6 = (f32[32,576]{1,0:T(8,128)S(1)}, f32[32,576]{1,0:T(8,128)S(1)}, u32[]{:S(2)}, u32[]{:S(2)}) collective-permute-start(f32[32,576]{1,0:T(8,128)S(1)} %get-tuple-element.25), channel_id=1, source_target_pairs={{0,2},{2,0},{1,3},{3,1},{4,6},{6,4},{5,7},{7,5},{8,10},{10,8},{9,1... | collective-permute-start | bytes 221192 | tf_op jit(solution)/shard_map/ppermute | solution.py:56
